TPU v7x, 128 devices: a whole 4x4x4 slice. The times are simulated.
128 devices in a mesh: child: 2 (over z_lo), row: 16 (over x, y), col: 4 (over z_hi, core).
Axes of the slice: x: 4, y: 4, z: 4 (z_hi: 2, z_lo: 2; z = z_hi * 2 + z_lo), core: 2. Of those that a mesh axis runs over, the one named last changes fastest.
Arguments:
- child_fronts: float32 [2, 4096, 4096], P('child', 'row', 'col'), as said below
- root_front: float32 [8192, 8192], P('col', ('child', 'row')), as said below
- block_maps: int32 [2, 24], replicated, may hold values from 0 to 63, as said below
Outputs:
- child_factor: float32 [2, 4096, 1024], P('child', 'row')
- root_factor: float32 [8192, 512], P('col')
- root_trailing: float32 [8192, 8192], P('col', ('child', 'row'))
Inputs may be any that keep to these rules, and one draw needn't show every extreme that they name: `block_maps`: row c lists 24 different root blocks in increasing order; block 0 appears in the first row and the last root block in the last row. `child_fronts`: each front is symmetric and positive definite. `root_front`: symmetric and positive definite.
All inputs are finite; a program needn't handle non-finite values.
Results may differ from a plain program's by a relative error of at most 0.0003.
Values may be sent and summed in bfloat16 or wider, within the bound.
No kernel may reach another device: no remote copies, remote signals or barrier semaphores. Data moves between devices by JAX's collectives and lax.ppermute only.
A program may use at most 128 MiB of HBM per device.

v0:
```python
import functools

import jax
import jax.numpy as jnp
from jax import lax
from jax.experimental import pallas as pl
from jax.experimental.pallas import tpu as pltpu
from jax.sharding import PartitionSpec as P

F32 = jnp.float32
BF16 = jnp.bfloat16
HI = lax.Precision.HIGHEST
ROWS, COLS = 16, 4
NCB = 24
VM = pltpu.CompilerParams(vmem_limit_bytes=56 << 20)


def lane_copy(v, k):
    return jnp.broadcast_to(v[:, k:k + 1], (8, 128))


def sub_copy(v, k):
    return jnp.broadcast_to(v[k:k + 1, :], (8, 128))


def dot(a, b, ca, cb):
    return lax.dot_general(a, b, (((ca,), (cb,)), ((), ())), precision=HI, preferred_element_type=F32)


def dot16(a, b, ca, cb):
    return lax.dot_general(a, b, (((ca,), (cb,)), ((), ())), preferred_element_type=F32)


def inverse_factor128(block):
    lane = lax.broadcasted_iota(jnp.int32, (8, 128), 1)
    sub = lax.broadcasted_iota(jnp.int32, (8, 128), 0)
    w = [block[8 * t:8 * t + 8, :] for t in range(16)]
    for s in range(16):
        c = {t: [lane_copy(w[t], 8 * s + j) for j in range(8)] for t in range(s, 16)}
        inside = (lane >= 8 * s) & (lane < 8 * s + 8)
        w[s] = jnp.where(inside, (lane - 8 * s == sub).astype(F32), w[s])
        for t in range(s + 1, 16):
            w[t] = jnp.where(inside, 0.0, w[t])
        for j in range(8):
            scale = lax.rsqrt(sub_copy(c[s][j], j))
            pivot_row = sub_copy(w[s], j) * scale
            ahead = {k: sub_copy(c[s][j], k) * scale for k in range(j + 1, 8)}
            for t in range(s, 16):
                l = c[t][j] * scale
                if t == s:
                    l = jnp.where(sub > j, l, 0.0)
                for k in range(j + 1, 8):
                    c[t][k] = c[t][k] - l * ahead[k]
                w[t] = w[t] - l * pivot_row
            w[s] = jnp.where(sub == j, pivot_row, w[s])
    return jnp.concatenate([jnp.where(lane <= sub + 8 * t, w[t], 0.0) for t in range(16)], axis=0)


def inverse_factor512(a, b, g):
    n = 512
    b[...] = jnp.zeros((n, n), F32)

    def block(k, carry):
        o = pl.multiple_of(128 * k, 128)
        g[...] = inverse_factor128(a[pl.ds(o, 128), pl.ds(o, 128)])
        for step in range(n // 128):
            pl.when(k == step)(functools.partial(outer, 128 * step))
        return carry

    def outer(o):
        inv = g[...]
        if o > 0:
            b[o:o + 128, 0:o] = dot(inv, b[o:o + 128, 0:o], 1, 0)
        b[o:o + 128, o:o + 128] = inv
        r = o + 128
        if r < n:
            l = dot(a[r:n, o:o + 128], inv, 1, 1)
            a[r:n, r:n] = a[r:n, r:n] - dot(l, l, 1, 1)
            b[r:n, 0:r] = b[r:n, 0:r] - dot(l, b[o:o + 128, 0:r], 1, 0)

    lax.fori_loop(0, n // 128, block, 0)


def head_rows():
    for s in range(16):
        for q in range(4):
            for h in range(2):
                yield 256 * h + 128 * (s // 8) + 32 * q + 4 * (s % 8), (s, 2 * q + h)


def head_kernel(d_ref, c_ref, inv_ref, p_ref, u_ref, a, g):
    for o, piece in head_rows():
        a[o:o + 4, :] = d_ref[piece]
    inverse_factor512(a, inv_ref, g)
    p = dot(c_ref[...], inv_ref[...], 1, 1)
    p_ref[...] = p
    u_ref[...] = p.astype(BF16)


def second_kernel(mask_ref, d_ref, inv0_ref, c_ref, u0_ref, p_ref, u_ref, d10, inv1, a, g):
    for o, (s, i) in head_rows():
        d10[o:o + 4, :] = d_ref[s, i, :, 0:512]
        a[o:o + 4, :] = d_ref[s, i, :, 512:1024]
    u10 = dot(d10[...], inv0_ref[...], 1, 1).astype(BF16)
    a[...] = a[...] - dot16(u10, u10, 1, 1)
    c1 = c_ref[...] - dot16(u0_ref[...], u10, 1, 1)
    inverse_factor512(a, inv1, g)
    p1 = dot(c1, inv1[...], 1, 1)
    p_ref[...] = jnp.where(mask_ref[0] > 0, p1, 0.0)
    u_ref[...] = p1.astype(BF16)


def place(b, y_ref):
    col = pl.multiple_of(jnp.maximum(b, 0) * 128, 128)
    return jnp.where(b >= 0, y_ref[:, pl.ds(col, 128)], 0.0)


def place_panel_kernel(panel_ref, y_ref, p_ref):
    for m in range(4):
        p_ref[:, 128 * m:128 * m + 128] = place(panel_ref[m], y_ref)


def place_kernel(bulk_ref, y_ref, o_ref):
    def one(slot, carry):
        out = pl.multiple_of((slot % 4) * 128, 128)
        o_ref[slot // 4, :, pl.ds(out, 128)] = place(bulk_ref[slot], y_ref)
        return carry

    lax.fori_loop(0, 64, one, 0)


def picked(b, ref):
    v = ref[jnp.maximum(b, 0) + 8]
    return jnp.where(b >= 0, v, jnp.zeros_like(v))


def sender(refs, q_ref, p):
    j = p ^ q_ref[0]

    def read(i):
        x, near, far, corner = [ref[i] for ref in refs]
        return jnp.where(j >= 2, jnp.where(j == 3, corner, far), jnp.where(j == 1, near, x))

    return read


def columns_of(refs, q_ref):
    return jnp.concatenate([sender(refs, q_ref, q)(m) for m in range(4) for q in range(4)], axis=0)


def select_kernel(panel_ref, bulk_ref, u0_ref, u1_ref, p_ref, o_ref):
    for ref, out in ((panel_ref, p_ref), (bulk_ref, o_ref)):
        for i in range(4):
            out[i, :, 0:512] = picked(ref[i], u0_ref)
            out[i, :, 512:1024] = picked(ref[i], u1_ref)


def panel_kernel(q_ref, rows_ref, panel_ref, u0_ref, u1_ref, fp_ref, c0, c1, c2, c3, z_ref, t_ref):
    upan = columns_of((c0, c1, c2, c3), q_ref)
    for ref, out in ((panel_ref, t_ref), (rows_ref, z_ref)):
        f, u0, u1 = [jnp.concatenate([picked(ref[i], x) for i in range(4)], axis=0) for x in (fp_ref, u0_ref, u1_ref)]
        out[...] = f - dot16(jnp.concatenate([u0, u1], axis=1), upan, 1, 1)


def bulk_kernel(q_ref, panel_ref, u0_ref, u1_ref, f_ref, c0, c1, c2, c3, own_ref, other_ref, first_ref, send_ref):
    ubulk = columns_of((c0, c1, c2, c3), q_ref)
    rows = jnp.concatenate([u0_ref[8:32].reshape(768, 512), u1_ref[8:32].reshape(768, 512)], axis=1)
    s = f_ref[8:32].reshape(768, 512) - dot16(rows, ubulk, 1, 1)
    own_ref[...] = s[:, 0:256]
    other_ref[...] = s[:, 256:512]
    for m in range(4):
        b = panel_ref[m]
        rows = pl.ds(pl.multiple_of(32 * jnp.maximum(b, 0), 32), 32)
        first_ref[m] = jnp.where(b >= 0, own_ref[rows, :], 0.0)
        send_ref[m] = jnp.where(b >= 0, other_ref[rows, :], 0.0)


def root_kernel(q_ref, t0, t1, t2, t3, inv_ref, a, g):
    for q in range(4):
        read = sender((t0, t1, t2, t3), q_ref, q)
        for m in range(4):
            a[128 * m + 32 * q:128 * m + 32 * q + 32, :] = read(m)
    inverse_factor512(a, inv_ref, g)


def spread_kernel(mine_ref, theirs_ref, own_ref, got_ref, o_ref):
    def one(m, carry):
        i = mine_ref[m]
        j = theirs_ref[m]
        v = own_ref[jnp.maximum(i, 0)]
        w = got_ref[jnp.maximum(j, 0)]
        o_ref[m] = jnp.where(i >= 0, v, 0.0) + jnp.where(j >= 0, w, 0.0)
        return carry

    lax.fori_loop(0, 64, one, 0)


def factor_kernel(flag_ref, panel_ref, inv_ref, cp_ref, p_ref, u_ref, ug_ref, cps):
    step = pl.program_id(0)

    @pl.when(step == 0)
    def _():
        for q in range(4):
            for m in range(4):
                cps[128 * m + 32 * q:128 * m + 32 * q + 32, :] = cp_ref[q, m]
        v = dot(inv_ref[...], cps[...], 1, 0).astype(BF16)
        ug_ref[...] = jnp.where(flag_ref[0] > 0, v, jnp.zeros_like(v))

    p = dot(panel_ref[...], inv_ref[...], 1, 1)
    p_ref[...] = p
    u = p.astype(BF16)
    u_ref[...] = jnp.where((flag_ref[1] > 0) | (step >= 1), u, jnp.zeros_like(u))


def last_kernel(q_ref, u_ref, ug_ref, root_ref, g0, g1, g2, g3, o_ref):
    upd = dot16(u_ref[...], ug_ref[...], 1, 0)
    for q in range(4):
        read = sender((g0, g1, g2, g3), q_ref, q)
        for m in range(4):
            o = 128 * m + 32 * q
            o_ref[o:o + 32, :] = root_ref[o:o + 32, :] + read(m) - upd[o:o + 32, :]


def vmem():
    return pl.BlockSpec(memory_space=pltpu.VMEM)


def smem():
    return pl.BlockSpec(memory_space=pltpu.SMEM)


def call(kernel, outs, n_scalar, n_vector, scratch=(), flops=0, name=None):
    return pl.pallas_call(
        kernel,
        out_shape=outs,
        in_specs=[smem()] * n_scalar + [vmem()] * n_vector,
        out_specs=jax.tree.map(lambda _: vmem(), outs),
        scratch_shapes=list(scratch),
        compiler_params=VM,
        cost_estimate=pl.CostEstimate(flops=flops, transcendentals=0, bytes_accessed=1 << 20),
        name=name,
    )


def sds(shape, dtype=F32):
    return jax.ShapeDtypeStruct(shape, dtype)


CHOL = [pltpu.VMEM((512, 512), F32), pltpu.VMEM((128, 128), F32)]


def exchange(x, axis):
    return lax.all_to_all(x, axis, split_axis=0, concat_axis=0, tiled=True)


def gather(x, axis, n):
    return exchange(jnp.broadcast_to(x[None], (n,) + x.shape), axis)


def in_order(own, near, far, corner, q):
    even = q % 2 == 0
    low = q < 2
    a0, a1 = jnp.where(even, own, near), jnp.where(even, near, own)
    b0, b1 = jnp.where(even, far, corner), jnp.where(even, corner, far)
    return jnp.stack([jnp.where(low, a0, b0), jnp.where(low, a1, b1), jnp.where(low, b0, a0), jnp.where(low, b1, a1)])


def across(x, k):
    return lax.ppermute(x, "col", [(i, i ^ k) for i in range(4)])


def around(x):
    far = across(x, 2)
    return [x, across(x, 1), far, across(far, 1)]


def gather_col(x, q):
    return in_order(*around(x), q)


def from_first_col(x, q):
    sent = [lax.ppermute(x[k], "col", [(0, k)]) for k in (1, 2, 3)]
    return jnp.where(q == 0, x[0], sent[0] + sent[1] + sent[2])


def exchange_col(x, q):
    return in_order(*sent_col(x, q), q)


def sent_col(x, q):
    parts = [lax.dynamic_index_in_dim(x, q ^ k, 0, keepdims=False) for k in range(4)]
    return [parts[0]] + [across(parts[k], k) for k in (1, 2, 3)]


def after(x, *earlier):
    return lax.optimization_barrier((x,) + earlier)[0]


def swap_child(x):
    return lax.ppermute(x, "child", [(0, 1), (1, 0)])


def local(child_fronts, root_front, block_maps):
    front = child_fronts[0]
    child = lax.axis_index("child")
    r = lax.axis_index("row")
    q = lax.axis_index("col")
    blocks = jnp.arange(64, dtype=jnp.int32)
    order = jnp.arange(1, NCB + 1, dtype=jnp.int32)
    inverse = jnp.sum(jnp.where(block_maps[:, :, None] == blocks, order[None, :, None], 0), axis=1) - 1
    mine = jnp.where(child == 0, inverse[0], inverse[1])
    theirs = jnp.where(child == 0, inverse[1], inverse[0])

    def pick(idx):
        return jnp.sum(jnp.where(idx[:, None] == blocks[None, :], mine[None, :], 0), axis=1)

    slot = jnp.arange(64, dtype=jnp.int32)
    half = jnp.where(slot % 4 >= 2, 1 - child, child)
    bulk_idx = pick(32 * half + 2 * (slot // 4) + slot % 2)
    panel_idx = mine[0:4]
    at = q[None]
    four = jnp.arange(4, dtype=jnp.int32)
    col_idx = pick(32 * jnp.where(four >= 2, 1 - child, child) + 2 * r + four % 2)
    row_idx = pick(16 * four + r)

    quarters = front.reshape(2, 4, 32, 1024).transpose(1, 0, 2, 3).reshape(4, 64, 1024)
    raw_top = root_front[0:512].reshape(4, 4, 32, 256).transpose(1, 0, 2, 3).reshape(4, 2, 64, 256)
    pack = from_first_col(jnp.concatenate([quarters, raw_top[:, 0], raw_top[:, 1]], axis=2), q)
    left = pack[:, 0:512]
    top = jnp.concatenate([pack[:, 1024:1280], pack[:, 1280:1536]], axis=0)

    heads = exchange(pack.reshape(16, 4, 1536), "row")
    first, second, corner0, corner1 = lax.optimization_barrier(
        (heads[0:2, :, 0:512], heads[2:4, :, 0:1024], heads[0:1, :, 1024:1536], heads[1:2, :, 1024:1536]))
    d00 = gather(gather_col(first, q).reshape(8, 4, 512), "row", ROWS)
    corner = jnp.concatenate([corner0, corner1], axis=2)
    second = jnp.concatenate([gather_col(second, q).reshape(8, 4, 1024), corner], axis=0)
    second = jnp.broadcast_to(second[None], (ROWS,) + second.shape)
    d00, second = lax.optimization_barrier((d00, second))
    d1 = exchange(second, "row")
    raw_diag = jnp.concatenate([
        jnp.concatenate([d1[:, 8, :, c:c + 256] for c in (o, o + 512)], axis=2).reshape(64, 512) for o in (0, 256)
    ], axis=0)
    raw_diag = jnp.where(child == 0, raw_diag, 0.0)

    y = exchange_col(after(quarters, pack), q)
    panel_y = y[1][:, 0:512]
    placed_panel = call(place_panel_kernel, sds((64, 512)), 1, 1, name="place_panel")(panel_idx, panel_y)

    raw_rows = 0.0
    tile_top = after(root_front[0:512], pack)
    for j in range(2):
        pairs = []
        for g in range(32):
            m = 2 * g + j
            pairs.append((4 * g, (m // 32 * 16 + m % 16) * 4 + m // 16))
        raw_rows += lax.ppermute(tile_top[:, 128 * j:128 * j + 128], ("child", "row", "col"), pairs)
    d00, placed_panel, raw_rows = lax.optimization_barrier((d00, placed_panel, raw_rows))
    raw_rows = raw_rows.T
    inv0, p0, u0 = call(
        head_kernel, (sds((512, 512)), sds((64, 512)), sds((64, 512), BF16)), 0, 2, CHOL, 2 * 10**10, "head")(d00, left)
    f_panel = lax.all_gather(placed_panel, "row").reshape(32, 32, 512)
    u0_all = jnp.broadcast_to(u0.reshape(1, 2, 32, 512), (ROWS, 2, 32, 512))
    d1, u0_all = lax.optimization_barrier((d1, u0_all))
    u0_all = exchange(u0_all, "row").reshape(32, 32, 512)

    below = (r >= 2).astype(jnp.int32)[None]
    p1, u1 = call(
        second_kernel, (sds((64, 512)), sds((64, 512), BF16)), 1, 4,
        [pltpu.VMEM((512, 512), F32)] * 2 + CHOL, 3 * 10**10, "second")(below, d1, inv0, pack[:, 512:1024], u0)
    factor0 = p0.reshape(2, 32, 512)
    u1, u0_all, far0 = lax.optimization_barrier((u1, u0_all, across(factor0, 2)))
    u1_all = gather(u1.reshape(2, 32, 512), "row", ROWS).reshape(32, 32, 512)
    wide = after(jnp.concatenate([y[1], y[2], y[3]], axis=1), u1)
    placed = call(place_kernel, sds((16, 64, 512)), 1, 1, name="place")(bulk_idx, wide)
    factor0 = after(factor0, u1)
    factor0 = in_order(factor0, across(factor0, 1), far0, across(far0, 1), q)
    u1_all, placed, factor0 = lax.optimization_barrier((u1_all, placed, factor0))
    f_bulk = exchange(placed, "row").reshape(32, 32, 512)

    some = sds((4, 32, 1024), BF16)
    u_panel, u_bulk = call(select_kernel, (some, some), 2, 2, name="select")(panel_idx, col_idx, u0_all, u1_all)
    u_panel = around(u_panel)
    u_bulk = after(u_bulk, u_panel[2])
    bulk_far = across(u_bulk, 2)
    z, t = call(panel_kernel, (sds((128, 512)), sds((128, 512))), 3, 7, flops=10**9, name="panel")(
        at, row_idx, panel_idx, u0_all, u1_all, f_panel, *u_panel)
    z, t, bulk_far = lax.optimization_barrier((z, t, bulk_far))
    t = t + raw_diag
    t = t + swap_child(t)
    u_bulk = [u_bulk, across(u_bulk, 1), bulk_far, across(bulk_far, 1)]
    z = exchange_col(z.reshape(4, 32, 512), q).reshape(128, 512) + raw_rows
    z, t, u_bulk, f_bulk = lax.optimization_barrier((z, t, u_bulk, f_bulk))
    z_swapped = swap_child(z)
    z = z + z_swapped
    panel = lax.all_gather(z, "row", tiled=True)
    t_all = around(t.reshape(4, 32, 512))

    half, block = sds((768, 256)), sds((4, 32, 256))
    own, other, first, sent = call(bulk_kernel, (half, half, block, block), 2, 7, flops=2 * 10**9, name="bulk")(
        at, panel_idx, u0_all, u1_all, f_bulk, *u_bulk)
    head_cols = top.reshape(4, 32, 256) + first + swap_child(sent)
    t_all, z, other, head_cols = lax.optimization_barrier((t_all, z, other, head_cols))
    factor1 = p1.reshape(2, 32, 512)
    far1 = across(after(factor1, other), 2)
    head_far = across(head_cols, 2)
    inv_root = call(root_kernel, sds((512, 512)), 1, 4, CHOL, 2 * 10**10, "root")(at, *t_all)
    got, inv_root, far1, head_far = lax.optimization_barrier((swap_child(other), inv_root, far1, head_far))
    spread = call(spread_kernel, sds((64, 32, 256)), 2, 2, name="spread")(
        mine, theirs, own.reshape(24, 32, 256), got.reshape(24, 32, 256))
    arrived = sent_col(spread.reshape(4, 16, 32, 256), q)
    head_cols = in_order(head_cols, across(head_cols, 1), head_far, across(head_far, 1), q)

    flags = jnp.stack([16 * child + r >= 2, q > 0]).astype(jnp.int32)
    rows = pl.BlockSpec((512, 512), lambda i: (i, 0))
    whole = pl.BlockSpec((512, 512), lambda i: (0, 0))
    narrow = pl.BlockSpec((512, 256), lambda i: (i, 0))
    fixed = pl.BlockSpec((512, 256), lambda i: (0, 0))
    root_factor, u_root, u_cols = pl.pallas_call(
        factor_kernel,
        out_shape=(sds((2048, 512)), sds((2048, 512), BF16), sds((512, 256), BF16)),
        grid=(4,),
        in_specs=[smem(), rows, whole, pl.BlockSpec((4, 4, 32, 256), lambda i: (0, 0, 0, 0))],
        out_specs=(rows, rows, fixed),
        scratch_shapes=[pltpu.VMEM((512, 256), F32)],
        compiler_params=VM,
        cost_estimate=pl.CostEstimate(flops=10**10, transcendentals=0, bytes_accessed=1 << 20),
        name="factor",
    )(flags, panel, inv_root, head_cols)
    arrived, u_root = lax.optimization_barrier((arrived, u_root))
    factor1 = after(factor1, u_root)
    factor1 = in_order(factor1, across(factor1, 1), far1, across(after(far1, u_root), 1), q)
    child_factor = jnp.concatenate([factor0, factor1], axis=3).transpose(1, 0, 2, 3).reshape(1, 256, 1024)
    trailing = pl.pallas_call(
        last_kernel,
        out_shape=sds((2048, 256)),
        grid=(4,),
        in_specs=[smem(), rows, fixed, narrow] + [pl.BlockSpec((4, 32, 256), lambda i: (i, 0, 0))] * 4,
        out_specs=narrow,
        compiler_params=VM,
        name="last",
    )(at, u_root, u_cols, root_front, *arrived)
    return (child_factor, root_factor, trailing)


def solution(mesh):
    return jax.shard_map(
        local,
        mesh=mesh,
        in_specs=(P("child", "row", "col"), P("col", ("child", "row")), P()),
        out_specs=(P("child", "row", None), P("col", None), P("col", ("child", "row"))),
        check_vma=False,
    )
```

profile of v0, /device:TPU:1, one launch (start us, length us, event | category | flops | bytes accessed | tf_op | source)
XLA Modules:
  0.0 349.1 jit_solution(2260980284217139333)
XLA Ops:
  7.2 1.2 slice.81
  8.8 1.0 slice_bitcast_fusion.1
  9.8 1.4 collective-permute-start
  11.2 1.4 collective-permute-start.1
  12.6 1.4 collective-permute-start.2
  14.2 1.3 fusion
  16.3 7.5 %all-to-all-start = ((f32[16,4,1536]{2,1,0:T(4,128)}), f32[16,4,1536]{2,1,0:T(4,128)S(1)}, u32[]{:S(2)}, u32[]{:S(2)}) async-start(f32[16,4,1536]{2,1,0:T(4,128)} %reshape.144), calls=%async_computation | async-start | bytes 786432 | tf_op jit(solution)/shard_map/all_to_all | solution.py:253
  23.9 7.9 %all-to-all-done = f32[16,4,1536]{2,1,0:T(4,128)S(1)} async-done(((f32[16,4,1536]{2,1,0:T(4,128)}), f32[16,4,1536]{2,1,0:T(4,128)S(1)}, u32[]{:S(2)}, u32[]{:S(2)}) %all-to-all-start) | async-done | bytes 393248 | tf_op jit(solution)/shard_map/all_to_all | solution.py:253
  32.4 16.6 %collective-permute-start.4 = (f32[2,4,512]{2,1,0:T(4,128)S(1)}, f32[2,4,512]{2,1,0:T(4,128)S(1)}, u32[]{:S(2)}, u32[]{:S(2)}) collective-permute-start(f32[2,4,512]{2,1,0:T(4,128)S(1)} %slice.113), channel_id=1, source_target_pairs={{0,2},{1,3},{2,0},{3,1},{4,6},{5,7},{6,4},{7,5},{8,10},{9,11},{10,... | collective-permute-start | bytes 49160 | tf_op jit(solution)/shard_map/ppermute | solution.py:269
  49.0 1.1 collective-permute-done.4
  50.1 2.4 collective-permute-start.5
  53.4 1.2 broadcast_in_dim.112
  54.6 3.7 %all-to-all-start.1 = ((f32[16,8,4,512]{3,2,1,0:T(4,128)}), f32[16,8,4,512]{3,2,1,0:T(4,128)S(1)}, u32[]{:S(2)}, u32[]{:S(2)}) async-start(f32[16,8,4,512]{3,2,1,0:T(4,128)} %broadcast_in_dim.112), calls=%async_computation.1 | async-start | bytes 2097152 | tf_op jit(solution)/shard_map/all_to_all | solution.py:253
  58.8 0.9 collective-permute-start.7
  60.5 2.7 collective-permute-start.10
  66.6 7.8 %all-to-all-done.1.d_ref = f32[16,8,4,512]{3,2,1,0:T(4,128)S(1)} async-done(((f32[16,8,4,512]{3,2,1,0:T(4,128)}), f32[16,8,4,512]{3,2,1,0:T(4,128)S(1)}, u32[]{:S(2)}, u32[]{:S(2)}) %all-to-all-start.1) | async-done | bytes 1048608 | tf_op jit(solution)/shard_map/all_to_all | solution.py:253
  74.4 2.0 broadcast_in_dim.113
  76.4 4.4 %all-to-all-start.2 = ((f32[16,9,4,1024]{3,2,1,0:T(4,128)}), f32[16,9,4,1024]{3,2,1,0:T(4,128)}, u32[]{:S(2)}, u32[]{:S(2)}) async-start(f32[16,9,4,1024]{3,2,1,0:T(4,128)} %broadcast_in_dim.113), calls=%async_computation.2 | async-start | bytes 4718592 | tf_op jit(solution)/shard_map/all_to_all | solution.py:253
  81.6 1.3 collective-permute-start.12
  83.8 1.2 fusion.2
  85.7 1.6 place_panel.1
  87.2 25.6 %collective-permute-done.12 = f32[512,128]{0,1:T(8,128)S(1)} collective-permute-done((f32[512,128]{0,1:T(8,128)}, f32[512,128]{0,1:T(8,128)S(1)}, u32[]{:S(2)}, u32[]{:S(2)}) %collective-permute-start.12) | collective-permute-done | bytes 262176 | tf_op jit(solution)/shard_map/ppermute | solution.py:357
  112.9 21.7 %head.1 = (f32[512,512]{1,0:T(8,128)}, f32[64,512]{1,0:T(8,128)}, bf16[64,512]{1,0:T(8,128)(2,1)}) custom-call(f32[16,8,4,512]{3,2,1,0:T(4,128)} %copy-done.3, f32[64,512]{1,0:T(8,128)} %get-tuple-element.177.c_ref), custom_call_target="tpu_custom_call" | custom-call | flops 20000000000 | bytes 1048576 | tf_op jit(solution)/shard_map/head/pallas_call | solution.py:360
  134.7 1.9 broadcast_in_dim.117
  136.6 14.7 %all-to-all-start.3 = ((bf16[16,2,32,512]{3,2,1,0:T(8,128)(2,1)}), bf16[16,2,32,512]{3,2,1,0:T(8,128)(2,1)S(1)}, u32[]{:S(2)}, u32[]{:S(2)}) async-start(bf16[16,2,32,512]{3,2,1,0:T(8,128)(2,1)} %broadcast_in_dim.117), calls=%async_computation.3 | async-start | bytes 2097152 | tf_op jit(solution)/shard_map/all_to_all | solution.py:253
  151.4 24.8 %second.1 = (f32[64,512]{1,0:T(8,128)}, bf16[64,512]{1,0:T(8,128)(2,1)}) custom-call(s32[1]{0:T(128)} %bitcast.mask_ref, f32[16,9,4,1024]{3,2,1,0:T(4,128)} %all-to-all-done.2.d_ref, f32[512,512]{1,0:T(8,128)} %get-tuple-element.80.inv0_ref, f32[64,512]{1,0:T(8,128)} %get-tuple-element.176.c_ref, bf16[64,512]{1,0:T(8,128)(2,1)} %get-tuple-element.78.u0_ref), custom_call_target="tpu_custom_call" | custom-call | flops 30000001024 | bytes 1048576 | tf_op jit(solution)/shard_map/second/pallas_call | solution.py:368
  176.2 2.0 broadcast_in_dim.119
  178.2 6.8 %all-to-all-start.4 = ((bf16[16,2,32,512]{3,2,1,0:T(8,128)(2,1)}), bf16[16,2,32,512]{3,2,1,0:T(8,128)(2,1)S(1)}, u32[]{:S(2)}, u32[]{:S(2)}) async-start(bf16[16,2,32,512]{3,2,1,0:T(8,128)(2,1)} %broadcast_in_dim.119), calls=%async_computation.4 | async-start | bytes 2097152 | tf_op jit(solution)/shard_map/all_to_all | solution.py:253
  186.2 0.9 pad_maximum_fusion.1.y_ref
  187.2 3.4 place.1
  190.7 17.0 %all-to-all-done.4 = bf16[16,2,32,512]{3,2,1,0:T(8,128)(2,1)S(1)} async-done(((bf16[16,2,32,512]{3,2,1,0:T(8,128)(2,1)}), bf16[16,2,32,512]{3,2,1,0:T(8,128)(2,1)S(1)}, u32[]{:S(2)}, u32[]{:S(2)}) %all-to-all-start.4) | async-done | bytes 1048608 | tf_op jit(solution)/shard_map/all_to_all | solution.py:253
  207.8 1.0 copy-done.1
  208.7 4.5 %all-to-all-start.5 = ((f32[16,64,512]{2,1,0:T(8,128)}), f32[16,64,512]{2,1,0:T(8,128)}, u32[]{:S(2)}, u32[]{:S(2)}) async-start(f32[16,64,512]{2,1,0:T(8,128)} %place.1), calls=%async_computation.5 | async-start | bytes 4194304 | tf_op jit(solution)/shard_map/all_to_all | solution.py:253
  214.0 2.4 select.17
  216.4 2.8 collective-permute-start.18
  219.2 1.1 collective-permute-start.17
  220.2 5.1 %collective-permute-done.18.c2 = bf16[4,32,1024]{2,1,0:T(8,128)(2,1)S(1)} collective-permute-done((bf16[4,32,1024]{2,1,0:T(8,128)(2,1)}, bf16[4,32,1024]{2,1,0:T(8,128)(2,1)S(1)}, u32[]{:S(2)}, u32[]{:S(2)}) %collective-permute-start.18) | collective-permute-done | bytes 262176 | tf_op jit(solution)/shard_map/ppermute | solution.py:269
  225.4 1.4 collective-permute-start.19
  226.8 2.8 collective-permute-start.20
  229.6 1.0 fusion.11
  232.3 4.0 %panel.1 = (f32[128,512]{1,0:T(8,128)}, f32[128,512]{1,0:T(8,128)}) custom-call(s32[1]{0:T(128)} %bitcast.41.q_ref, s32[4]{0:T(128)} %get-tuple-element.136.rows_ref, s32[4]{0:T(128)} %slice_bitcast_fusion.6.panel_ref, bf16[32,32,512]{2,1,0:T(8,128)(2,1)} %bitcast.150, bf16[32,32,512]{2,1,0:T(8,128)(2,1)} %bitcast.153, f32[32,32,512]{2,1,0:T(8,128)} %bitcast.157, ...), custom_call_target="tpu_custom_call" | custom-call | flops 1000000000 | bytes 1048576 | tf_op jit(solution)/shard_map/panel/pallas_call | solution.py:386
  236.6 1.0 dynamic-slice_bitcast_fusion.9
  238.4 2.8 collective-permute-start.22
  241.6 1.0 fusion.1
  242.6 1.5 collective-permute-start.24
  244.5 2.2 collective-permute-done.23
  247.7 3.4 collective-permute-done.24
  252.0 6.4 %collective-permute-done.30 = f32[128,512]{1,0:T(8,128)S(1)} collective-permute-done((f32[128,512]{1,0:T(8,128)S(1)}, f32[128,512]{1,0:T(8,128)S(1)}, u32[]{:S(2)}, u32[]{:S(2)}) %collective-permute-start.30) | collective-permute-done | bytes 262176 | tf_op jit(solution)/shard_map/ppermute | solution.py:300
  259.9 1.9 collective-permute-start.28
  261.8 4.7 %bulk.1 = (f32[768,256]{1,0:T(8,128)}, f32[768,256]{1,0:T(8,128)}, f32[4,32,256]{2,1,0:T(8,128)}, f32[4,32,256]{2,1,0:T(8,128)}) custom-call(s32[1]{0:T(128)} %bitcast.41.q_ref, s32[4]{0:T(128)} %slice_bitcast_fusion.6.panel_ref, bf16[32,32,512]{2,1,0:T(8,128)(2,1)} %bitcast.151, bf16[32,32,512]{2,1,0:T(8,128)(2,1)} %bitcast.154, ...), custom_call_target="tpu_custom_call" | custom-call | flops 2000000000 | bytes 1048576 | tf_op jit(solution)/shard_map/bulk/pallas_call | solution.py:400
  267.0 2.5 collective-permute-start.27
  270.5 0.9 add_add_fusion
  271.5 1.9 collective-permute-start.34
  273.4 2.5 collective-permute-start.38
  276.7 2.5 collective-permute-start.33
  279.2 20.9 %root.1.inv_ref = f32[512,512]{1,0:T(8,128)} custom-call(s32[1]{0:T(128)} %bitcast.41.q_ref, f32[4,32,512]{2,1,0:T(8,128)} %bitcast.167, f32[4,32,512]{2,1,0:T(8,128)} %copy-done.24, f32[4,32,512]{2,1,0:T(8,128)} %copy-done.23, f32[4,32,512]{2,1,0:T(8,128)} %copy-done.25), custom_call_target="tpu_custom_call" | custom-call | flops 20000000000 | bytes 1048576 | tf_op jit(solution)/shard_map/root/pallas_call | solution.py:407
  300.3 0.9 collective-permute-start.39
  301.3 3.7 %spread.1 = f32[64,32,256]{2,1,0:T(8,128)} custom-call(s32[64]{0:T(128)} %bitcast.179, s32[64]{0:T(128)} %get-tuple-element.191.theirs_ref, f32[24,32,256]{2,1,0:T(8,128)} %bitcast.161, f32[24,32,256]{2,1,0:T(8,128)} %bitcast.162), custom_call_target="tpu_custom_call" | custom-call | bytes 1048576 | tf_op jit(solution)/shard_map/spread/pallas_call | solution.py:409
  305.0 2.8 dynamic-slice_bitcast_fusion
  309.2 2.4 collective-permute-start.37
  312.4 11.4 %factor.1 = (f32[2048,512]{1,0:T(8,128)}, bf16[2048,512]{1,0:T(8,128)(2,1)}, bf16[512,256]{1,0:T(8,128)(2,1)}) custom-call(s32[2]{0:T(128)} %add_convert_fusion.flag_ref, f32[2048,512]{1,0:T(8,128)} %all-gather.4.cloned.1.call-done.panel_ref, f32[512,512]{1,0:T(8,128)} %root.1.inv_ref, f32[4,4,32,256]{3,2,1,0:T(8,128)} %pad_maximum_fusion.3.cp_ref), custom_call_target="tpu_custom_call" | custom-call | flops 10000000000 | bytes 1048576 | tf_op jit(solution)/shard_map/factor/pallas_call | solution.py:419
  323.9 10.9 %collective-permute-done.37.g3 = f32[16,32,256]{2,1,0:T(8,128)S(1)} collective-permute-done((f32[16,32,256]{2,1,0:T(8,128)S(1)}, f32[16,32,256]{2,1,0:T(8,128)S(1)}, u32[]{:S(2)}, u32[]{:S(2)}) %collective-permute-start.37) | collective-permute-done | bytes 524320 | tf_op jit(solution)/shard_map/ppermute | solution.py:269
  335.6 5.3 %last.1 = f32[2048,256]{1,0:T(8,128)} custom-call(s32[1]{0:T(128)} %bitcast.41.q_ref, bf16[2048,512]{1,0:T(8,128)(2,1)} %get-tuple-element.125.u_ref, bf16[512,256]{1,0:T(8,128)(2,1)} %get-tuple-element.130.ug_ref, f32[2048,256]{1,0:T(8,128)} %root_ref.1, f32[16,32,256]{2,1,0:T(8,128)} %get-tuple-element.131.g0, f32[16,32,256]{2,1,0:T(8,128)} %copy-done.5, ...), custom_call_target="tpu_custom_call" | custom-call | tf_op jit(solution)/shard_map/last/pallas_call | solution.py:434
  341.1 1.0 copy.22
  (162 shorter events, 24.7 us)
Async XLA Ops:
  9.8 14.0 %copy-start.19 = (s32[2,24]{1,0:T(2,128)S(1)}, s32[2,24]{1,0:T(2,128)}, u32[]{:S(2)}) copy-start(s32[2,24]{1,0:T(2,128)} %param.5) | copy-start | bytes 580
  9.8 4.4 %collective-permute-start = (f32[64,1536]{1,0:T(8,128)}, f32[64,1536]{1,0:T(8,128)}, u32[]{:S(2)}, u32[]{:S(2)}) collective-permute-start(f32[64,1536]{1,0:T(8,128)} %get-tuple-element.150), channel_id=1, source_target_pairs={{0,1},{4,5},{8,9},{12,13},{16,17},{20,21},{24,25},{28,29},{32,33},... | collective-permute-start | bytes 1179656 | tf_op jit(solution)/shard_map/ppermute | solution.py:282
  11.2 3.0 collective-permute-start.1
  12.6 1.5 collective-permute-start.2
  16.3 15.5 %all-to-all-start = ((f32[16,4,1536]{2,1,0:T(4,128)}), f32[16,4,1536]{2,1,0:T(4,128)S(1)}, u32[]{:S(2)}, u32[]{:S(2)}) async-start(f32[16,4,1536]{2,1,0:T(4,128)} %reshape.144), calls=%async_computation | async-start | bytes 786432 | tf_op jit(solution)/shard_map/all_to_all | solution.py:253
  32.4 17.7 %collective-permute-start.4 = (f32[2,4,512]{2,1,0:T(4,128)S(1)}, f32[2,4,512]{2,1,0:T(4,128)S(1)}, u32[]{:S(2)}, u32[]{:S(2)}) collective-permute-start(f32[2,4,512]{2,1,0:T(4,128)S(1)} %slice.113), channel_id=1, source_target_pairs={{0,2},{1,3},{2,0},{3,1},{4,6},{5,7},{6,4},{7,5},{8,10},{9,11},{10,... | collective-permute-start | bytes 49160 | tf_op jit(solution)/shard_map/ppermute | solution.py:269
  49.0 4.3 %collective-permute-start.3 = (f32[2,4,512]{2,1,0:T(4,128)S(1)}, f32[2,4,512]{2,1,0:T(4,128)S(1)}, u32[]{:S(2)}, u32[]{:S(2)}) collective-permute-start(f32[2,4,512]{2,1,0:T(4,128)S(1)} %slice.113), channel_id=1, source_target_pairs={{0,1},{1,0},{2,3},{3,2},{4,5},{5,4},{6,7},{7,6},{8,9},{9,8},{10,11... | collective-permute-start | bytes 49160 | tf_op jit(solution)/shard_map/ppermute | solution.py:269
  50.1 3.3 collective-permute-start.5
  54.6 19.7 %all-to-all-start.1 = ((f32[16,8,4,512]{3,2,1,0:T(4,128)}), f32[16,8,4,512]{3,2,1,0:T(4,128)S(1)}, u32[]{:S(2)}, u32[]{:S(2)}) async-start(f32[16,8,4,512]{3,2,1,0:T(4,128)} %broadcast_in_dim.112), calls=%async_computation.1 | async-start | bytes 2097152 | tf_op jit(solution)/shard_map/all_to_all | solution.py:253
  58.8 5.5 %collective-permute-start.7 = (f32[2,4,1024]{2,1,0:T(4,128)}, f32[2,4,1024]{2,1,0:T(4,128)S(1)}, u32[]{:S(2)}, u32[]{:S(2)}) collective-permute-start(f32[2,4,1024]{2,1,0:T(4,128)} %slice.114), channel_id=1, source_target_pairs={{0,2},{1,3},{2,0},{3,1},{4,6},{5,7},{6,4},{7,5},{8,10},{9,11},{10,... | collective-permute-start | bytes 98312 | tf_op jit(solution)/shard_map/ppermute | solution.py:269
  60.5 23.2 %collective-permute-start.10 = (f32[64,1024]{1,0:T(8,128)}, f32[64,1024]{1,0:T(8,128)}, u32[]{:S(2)}, u32[]{:S(2)}) collective-permute-start(f32[64,1024]{1,0:T(8,128)} %get-tuple-element.153), channel_id=1, source_target_pairs={{0,3},{1,2},{2,1},{3,0},{4,7},{5,6},{6,5},{7,4},{8,11},{9,10},{10,... | collective-permute-start | bytes 786440 | tf_op jit(solution)/shard_map/ppermute | solution.py:269
  63.1 20.6 %collective-permute-start.11 = (f32[64,1024]{1,0:T(8,128)S(1)}, f32[64,1024]{1,0:T(8,128)}, u32[]{:S(2)}, u32[]{:S(2)}) collective-permute-start(f32[64,1024]{1,0:T(8,128)S(1)} %get-tuple-element.152), channel_id=1, source_target_pairs={{0,2},{1,3},{2,0},{3,1},{4,6},{5,7},{6,4},{7,5},{8,10},{9,11},{10,... | collective-permute-start | bytes 786440 | tf_op jit(solution)/shard_map/ppermute | solution.py:269
  63.9 19.9 %collective-permute-start.9 = (f32[64,1024]{1,0:T(8,128)S(1)}, f32[64,1024]{1,0:T(8,128)}, u32[]{:S(2)}, u32[]{:S(2)}) collective-permute-start(f32[64,1024]{1,0:T(8,128)S(1)} %get-tuple-element.151), channel_id=1, source_target_pairs={{0,1},{1,0},{2,3},{3,2},{4,5},{5,4},{6,7},{7,6},{8,9},{9,8},{10,11... | collective-permute-start | bytes 786440 | tf_op jit(solution)/shard_map/ppermute | solution.py:269
  64.1 1.6 collective-permute-start.6
  64.4 1.4 collective-permute-start.8
  76.4 58.3 %all-to-all-start.2 = ((f32[16,9,4,1024]{3,2,1,0:T(4,128)}), f32[16,9,4,1024]{3,2,1,0:T(4,128)}, u32[]{:S(2)}, u32[]{:S(2)}) async-start(f32[16,9,4,1024]{3,2,1,0:T(4,128)} %broadcast_in_dim.113), calls=%async_computation.2 | async-start | bytes 4718592 | tf_op jit(solution)/shard_map/all_to_all | solution.py:253
  80.8 150.7 %all-gather.6.cloned.1.call-start = ((), (), s32[]{:S(2)}) async-start(), calls=%async_computation.7 | async-start | bytes 2228224 | tf_op jit(solution)/shard_map/all_gather | solution.py:362
  81.6 31.3 %collective-permute-start.12 = (f32[512,128]{0,1:T(8,128)}, f32[512,128]{0,1:T(8,128)S(1)}, u32[]{:S(2)}, u32[]{:S(2)}) collective-permute-start(f32[512,128]{0,1:T(8,128)} %get-tuple-element.167), channel_id=1, source_target_pairs={{0,0},{4,8},{8,16},{12,24},{16,32},{20,40},{24,48},{28,56},{32,1},... | collective-permute-start | bytes 786440 | tf_op jit(solution)/shard_map/ppermute | solution.py:357
  82.9 30.0 %collective-permute-start.13 = (f32[512,128]{0,1:T(8,128)}, f32[512,128]{0,1:T(8,128)S(1)}, u32[]{:S(2)}, u32[]{:S(2)}) collective-permute-start(f32[512,128]{0,1:T(8,128)} %get-tuple-element.166), channel_id=1, source_target_pairs={{0,4},{4,12},{8,20},{12,28},{16,36},{20,44},{24,52},{28,60},{32,5}... | collective-permute-start | bytes 786440 | tf_op jit(solution)/shard_map/ppermute | solution.py:357
  134.6 41.5 %collective-permute-start.14 = (f32[2,32,512]{2,1,0:T(8,128)}, f32[2,32,512]{2,1,0:T(8,128)S(1)}, u32[]{:S(2)}, u32[]{:S(2)}) collective-permute-start(f32[2,32,512]{2,1,0:T(8,128)} %bitcast.174), channel_id=1, source_target_pairs={{0,2},{1,3},{2,0},{3,1},{4,6},{5,7},{6,4},{7,5},{8,10},{9,11},{10,... | collective-permute-start | bytes 393224 | tf_op jit(solution)/shard_map/ppermute | solution.py:269
  136.6 39.6 %all-to-all-start.3 = ((bf16[16,2,32,512]{3,2,1,0:T(8,128)(2,1)}), bf16[16,2,32,512]{3,2,1,0:T(8,128)(2,1)S(1)}, u32[]{:S(2)}, u32[]{:S(2)}) async-start(bf16[16,2,32,512]{3,2,1,0:T(8,128)(2,1)} %broadcast_in_dim.117), calls=%async_computation.3 | async-start | bytes 2097152 | tf_op jit(solution)/shard_map/all_to_all | solution.py:253
  176.2 8.8 %copy-start.18 = (s32[1,64]{1,0:T(1,128)S(1)}, s32[1,64]{1,0:T(1,128)}, u32[]{:S(2)}) copy-start(s32[1,64]{1,0:T(1,128)} %get-tuple-element.192) | copy-start | bytes 772
  176.2 11.0 %copy-start = (bf16[16,2,32,512]{3,2,1,0:T(8,128)(2,1)}, bf16[16,2,32,512]{3,2,1,0:T(8,128)(2,1)S(1)}, u32[]{:S(2)}) copy-start(bf16[16,2,32,512]{3,2,1,0:T(8,128)(2,1)S(1)} %all-to-all-done.3) | copy-start | bytes 3145732
  178.2 29.5 %all-to-all-start.4 = ((bf16[16,2,32,512]{3,2,1,0:T(8,128)(2,1)}), bf16[16,2,32,512]{3,2,1,0:T(8,128)(2,1)S(1)}, u32[]{:S(2)}, u32[]{:S(2)}) async-start(bf16[16,2,32,512]{3,2,1,0:T(8,128)(2,1)} %broadcast_in_dim.119), calls=%async_computation.4 | async-start | bytes 2097152 | tf_op jit(solution)/shard_map/all_to_all | solution.py:253
  185.7 4.9 %collective-permute-start.15 = (f32[2,32,512]{2,1,0:T(8,128)}, f32[2,32,512]{2,1,0:T(8,128)S(1)}, u32[]{:S(2)}, u32[]{:S(2)}) collective-permute-start(f32[2,32,512]{2,1,0:T(8,128)} %bitcast.175), channel_id=1, source_target_pairs={{0,1},{1,0},{2,3},{3,2},{4,5},{5,4},{6,7},{7,6},{8,9},{9,8},{10,11... | collective-permute-start | bytes 393224 | tf_op jit(solution)/shard_map/ppermute | solution.py:269
  185.7 4.9 %collective-permute-start.16 = (f32[2,32,512]{2,1,0:T(8,128)}, f32[2,32,512]{2,1,0:T(8,128)S(1)}, u32[]{:S(2)}, u32[]{:S(2)}) collective-permute-start(f32[2,32,512]{2,1,0:T(8,128)} %copy-done.15), channel_id=1, source_target_pairs={{0,1},{1,0},{2,3},{3,2},{4,5},{5,4},{6,7},{7,6},{8,9},{9,8},{10,11... | collective-permute-start | bytes 393224 | tf_op jit(solution)/shard_map/ppermute | solution.py:269
  208.7 42.5 %all-to-all-start.5 = ((f32[16,64,512]{2,1,0:T(8,128)}), f32[16,64,512]{2,1,0:T(8,128)}, u32[]{:S(2)}, u32[]{:S(2)}) async-start(f32[16,64,512]{2,1,0:T(8,128)} %place.1), calls=%async_computation.5 | async-start | bytes 4194304 | tf_op jit(solution)/shard_map/all_to_all | solution.py:253
  213.2 99.2 %all-gather.4.cloned.1.call-start = ((), (), s32[]{:S(2)}) async-start(), calls=%async_computation.6 | async-start | bytes 4456448 | tf_op jit(solution)/shard_map/all_gather | solution.py:396
  216.4 9.0 %collective-permute-start.18 = (bf16[4,32,1024]{2,1,0:T(8,128)(2,1)}, bf16[4,32,1024]{2,1,0:T(8,128)(2,1)S(1)}, u32[]{:S(2)}, u32[]{:S(2)}) collective-permute-start(bf16[4,32,1024]{2,1,0:T(8,128)(2,1)} %get-tuple-element.93.c0), channel_id=1, source_target_pairs={{0,2},{1,3},{2,0},{3,1},{4,6},{5,7},{6,4},{7,5},{8,10},{9,11},{10,... | collective-permute-start | bytes 786440 | tf_op jit(solution)/shard_map/ppermute | solution.py:269
  219.2 12.3 %collective-permute-start.17 = (bf16[4,32,1024]{2,1,0:T(8,128)(2,1)}, bf16[4,32,1024]{2,1,0:T(8,128)(2,1)S(1)}, u32[]{:S(2)}, u32[]{:S(2)}) collective-permute-start(bf16[4,32,1024]{2,1,0:T(8,128)(2,1)} %get-tuple-element.93.c0), channel_id=1, source_target_pairs={{0,1},{1,0},{2,3},{3,2},{4,5},{5,4},{6,7},{7,6},{8,9},{9,8},{10,11... | collective-permute-start | bytes 786440 | tf_op jit(solution)/shard_map/ppermute | solution.py:269
  225.4 6.1 %collective-permute-start.19 = (bf16[4,32,1024]{2,1,0:T(8,128)(2,1)S(1)}, bf16[4,32,1024]{2,1,0:T(8,128)(2,1)S(1)}, u32[]{:S(2)}, u32[]{:S(2)}) collective-permute-start(bf16[4,32,1024]{2,1,0:T(8,128)(2,1)S(1)} %collective-permute-done.18.c2), channel_id=1, source_target_pairs={{0,1},{1,0},{2,3},{3,2},{4,5},{5,4},{6,7},{7,6},{8,9},{9,8},{10,11... | collective-permute-start | bytes 786440 | tf_op jit(solution)/shard_map/ppermute | solution.py:269
  226.8 9.8 %collective-permute-start.20 = (bf16[4,32,1024]{2,1,0:T(8,128)(2,1)}, bf16[4,32,1024]{2,1,0:T(8,128)(2,1)S(1)}, u32[]{:S(2)}, u32[]{:S(2)}) collective-permute-start(bf16[4,32,1024]{2,1,0:T(8,128)(2,1)} %get-tuple-element.104.c0), channel_id=1, source_target_pairs={{0,2},{1,3},{2,0},{3,1},{4,6},{5,7},{6,4},{7,5},{8,10},{9,11},{10,... | collective-permute-start | bytes 786440 | tf_op jit(solution)/shard_map/ppermute | solution.py:269
  230.7 20.4 %collective-permute-start.25 = (bf16[4,32,1024]{2,1,0:T(8,128)(2,1)}, bf16[4,32,1024]{2,1,0:T(8,128)(2,1)S(1)}, u32[]{:S(2)}, u32[]{:S(2)}) collective-permute-start(bf16[4,32,1024]{2,1,0:T(8,128)(2,1)} %get-tuple-element.104.c0), channel_id=1, source_target_pairs={{0,1},{1,0},{2,3},{3,2},{4,5},{5,4},{6,7},{7,6},{8,9},{9,8},{10,11... | collective-permute-start | bytes 786440 | tf_op jit(solution)/shard_map/ppermute | solution.py:269
  236.6 22.6 %copy-start.20 = (bf16[4,32,1024]{2,1,0:T(8,128)(2,1)}, bf16[4,32,1024]{2,1,0:T(8,128)(2,1)S(1)}, u32[]{:S(2)}) copy-start(bf16[4,32,1024]{2,1,0:T(8,128)(2,1)S(1)} %collective-permute-done.20.c2) | copy-start | bytes 786436
  237.6 6.5 %collective-permute-start.21 = (f32[32,512]{1,0:T(8,128)S(1)}, f32[32,512]{1,0:T(8,128)S(1)}, u32[]{:S(2)}, u32[]{:S(2)}) collective-permute-start(f32[32,512]{1,0:T(8,128)S(1)} %get-tuple-element.180), channel_id=1, source_target_pairs={{0,1},{1,0},{2,3},{3,2},{4,5},{5,4},{6,7},{7,6},{8,9},{9,8},{10,11... | collective-permute-start | bytes 196616 | tf_op jit(solution)/shard_map/ppermute | solution.py:269
  238.4 6.1 %collective-permute-start.22 = (f32[32,512]{1,0:T(8,128)S(1)}, f32[32,512]{1,0:T(8,128)S(1)}, u32[]{:S(2)}, u32[]{:S(2)}) collective-permute-start(f32[32,512]{1,0:T(8,128)S(1)} %get-tuple-element.182), channel_id=1, source_target_pairs={{0,2},{1,3},{2,0},{3,1},{4,6},{5,7},{6,4},{7,5},{8,10},{9,11},{10,... | collective-permute-start | bytes 196616 | tf_op jit(solution)/shard_map/ppermute | solution.py:269
  241.2 5.6 %collective-permute-start.23 = (f32[32,512]{1,0:T(8,128)S(1)}, f32[32,512]{1,0:T(8,128)S(1)}, u32[]{:S(2)}, u32[]{:S(2)}) collective-permute-start(f32[32,512]{1,0:T(8,128)S(1)} %get-tuple-element.181), channel_id=1, source_target_pairs={{0,3},{1,2},{2,1},{3,0},{4,7},{5,6},{6,5},{7,4},{8,11},{9,10},{10,... | collective-permute-start | bytes 196616 | tf_op jit(solution)/shard_map/ppermute | solution.py:269
  242.6 8.5 %collective-permute-start.24 = (f32[128,512]{1,0:T(8,128)S(1)}, f32[128,512]{1,0:T(8,128)S(1)}, u32[]{:S(2)}, u32[]{:S(2)}) collective-permute-start(f32[128,512]{1,0:T(8,128)S(1)} %fusion.1), channel_id=1, source_target_pairs={{0,64},{64,0},{1,65},{65,1},{2,66},{66,2},{3,67},{67,3},{4,68},{68... | collective-permute-start | bytes 786440 | tf_op jit(solution)/shard_map/ppermute | solution.py:300
  244.1 7.1 %collective-permute-start.26 = (bf16[4,32,1024]{2,1,0:T(8,128)(2,1)S(1)}, bf16[4,32,1024]{2,1,0:T(8,128)(2,1)S(1)}, u32[]{:S(2)}, u32[]{:S(2)}) collective-permute-start(bf16[4,32,1024]{2,1,0:T(8,128)(2,1)S(1)} %collective-permute-done.20.c2), channel_id=1, source_target_pairs={{0,1},{1,0},{2,3},{3,2},{4,5},{5,4},{6,7},{7,6},{8,9},{9,8},{10,11... | collective-permute-start | bytes 786440 | tf_op jit(solution)/shard_map/ppermute | solution.py:269
  251.1 15.8 %copy-start.8 = (f32[128,512]{1,0:T(8,128)}, f32[128,512]{1,0:T(8,128)S(1)}, u32[]{:S(2)}) copy-start(f32[128,512]{1,0:T(8,128)S(1)} %add.166) | copy-start | bytes 786436
  251.2 10.7 %copy-start.21 = (bf16[4,32,1024]{2,1,0:T(8,128)(2,1)}, bf16[4,32,1024]{2,1,0:T(8,128)(2,1)S(1)}, u32[]{:S(2)}) copy-start(bf16[4,32,1024]{2,1,0:T(8,128)(2,1)S(1)} %collective-permute-done.25.c1) | copy-start | bytes 786436
  251.2 10.6 %copy-start.22 = (bf16[4,32,1024]{2,1,0:T(8,128)(2,1)}, bf16[4,32,1024]{2,1,0:T(8,128)(2,1)S(1)}, u32[]{:S(2)}) copy-start(bf16[4,32,1024]{2,1,0:T(8,128)(2,1)S(1)} %collective-permute-done.26.c3) | copy-start | bytes 786436
  251.2 7.2 %collective-permute-start.30 = (f32[128,512]{1,0:T(8,128)S(1)}, f32[128,512]{1,0:T(8,128)S(1)}, u32[]{:S(2)}, u32[]{:S(2)}) collective-permute-start(f32[128,512]{1,0:T(8,128)S(1)} %bitcast_add_fusion), channel_id=1, source_target_pairs={{0,64},{64,0},{1,65},{65,1},{2,66},{66,2},{3,67},{67,3},{4,68},{68... | collective-permute-start | bytes 786440 | tf_op jit(solution)/shard_map/ppermute | solution.py:300
  259.9 16.8 %copy-start.12 = (f32[64,512]{1,0:T(8,128)S(1)}, f32[64,512]{1,0:T(8,128)}, u32[]{:S(2)}) copy-start(f32[64,512]{1,0:T(8,128)} %get-tuple-element.89) | copy-start | bytes 393220
  259.9 9.6 %collective-permute-start.28 = (f32[4,32,512]{2,1,0:T(8,128)S(1)}, f32[4,32,512]{2,1,0:T(8,128)S(1)}, u32[]{:S(2)}, u32[]{:S(2)}) collective-permute-start(f32[4,32,512]{2,1,0:T(8,128)S(1)} %bitcast.165), channel_id=1, source_target_pairs={{0,2},{1,3},{2,0},{3,1},{4,6},{5,7},{6,4},{7,5},{8,10},{9,11},{10,... | collective-permute-start | bytes 786440 | tf_op jit(solution)/shard_map/ppermute | solution.py:269
  266.5 4.0 %collective-permute-start.31 = (f32[4,32,256]{2,1,0:T(8,128)}, f32[4,32,256]{2,1,0:T(8,128)S(1)}, u32[]{:S(2)}, u32[]{:S(2)}) collective-permute-start(f32[4,32,256]{2,1,0:T(8,128)} %get-tuple-element.113), channel_id=1, source_target_pairs={{0,64},{64,0},{1,65},{65,1},{2,66},{66,2},{3,67},{67,3},{4,68},{68... | collective-permute-start | bytes 393224 | tf_op jit(solution)/shard_map/ppermute | solution.py:300
  267.0 4.5 %collective-permute-start.27 = (f32[4,32,512]{2,1,0:T(8,128)S(1)}, f32[4,32,512]{2,1,0:T(8,128)S(1)}, u32[]{:S(2)}, u32[]{:S(2)}) collective-permute-start(f32[4,32,512]{2,1,0:T(8,128)S(1)} %bitcast.166), channel_id=1, source_target_pairs={{0,1},{1,0},{2,3},{3,2},{4,5},{5,4},{6,7},{7,6},{8,9},{9,8},{10,11... | collective-permute-start | bytes 786440 | tf_op jit(solution)/shard_map/ppermute | solution.py:269
  269.5 9.7 %copy-start.23 = (f32[4,32,512]{2,1,0:T(8,128)}, f32[4,32,512]{2,1,0:T(8,128)S(1)}, u32[]{:S(2)}) copy-start(f32[4,32,512]{2,1,0:T(8,128)S(1)} %collective-permute-done.28.t2) | copy-start | bytes 786436
  269.5 2.0 collective-permute-start.29
  271.5 7.7 %copy-start.24 = (f32[4,32,512]{2,1,0:T(8,128)}, f32[4,32,512]{2,1,0:T(8,128)S(1)}, u32[]{:S(2)}) copy-start(f32[4,32,512]{2,1,0:T(8,128)S(1)} %collective-permute-done.27.t1) | copy-start | bytes 786436
  271.5 7.7 %copy-start.25 = (f32[4,32,512]{2,1,0:T(8,128)}, f32[4,32,512]{2,1,0:T(8,128)S(1)}, u32[]{:S(2)}) copy-start(f32[4,32,512]{2,1,0:T(8,128)S(1)} %collective-permute-done.29.t3) | copy-start | bytes 786436
  271.5 28.8 %collective-permute-start.34 = (f32[4,32,256]{2,1,0:T(8,128)S(1)}, f32[4,32,256]{2,1,0:T(8,128)S(1)}, u32[]{:S(2)}, u32[]{:S(2)}) collective-permute-start(f32[4,32,256]{2,1,0:T(8,128)S(1)} %add_add_fusion), channel_id=1, source_target_pairs={{0,2},{1,3},{2,0},{3,1},{4,6},{5,7},{6,4},{7,5},{8,10},{9,11},{10,... | collective-permute-start | bytes 393224 | tf_op jit(solution)/shard_map/ppermute | solution.py:269
  273.4 38.1 %collective-permute-start.38 = (f32[4,32,256]{2,1,0:T(8,128)S(1)}, f32[4,32,256]{2,1,0:T(8,128)S(1)}, u32[]{:S(2)}, u32[]{:S(2)}) collective-permute-start(f32[4,32,256]{2,1,0:T(8,128)S(1)} %add_add_fusion), channel_id=1, source_target_pairs={{0,1},{1,0},{2,3},{3,2},{4,5},{5,4},{6,7},{7,6},{8,9},{9,8},{10,11... | collective-permute-start | bytes 393224 | tf_op jit(solution)/shard_map/ppermute | solution.py:269
  275.9 24.4 %collective-permute-start.32 = (f32[768,256]{1,0:T(8,128)}, f32[768,256]{1,0:T(8,128)S(1)}, u32[]{:S(2)}, u32[]{:S(2)}) collective-permute-start(f32[768,256]{1,0:T(8,128)} %get-tuple-element.114), channel_id=1, source_target_pairs={{0,64},{64,0},{1,65},{65,1},{2,66},{66,2},{3,67},{67,3},{4,68},{68... | collective-permute-start | bytes 2359304 | tf_op jit(solution)/shard_map/ppermute | solution.py:300
  276.7 23.6 %collective-permute-start.33 = (f32[2,32,512]{2,1,0:T(8,128)S(1)}, f32[2,32,512]{2,1,0:T(8,128)S(1)}, u32[]{:S(2)}, u32[]{:S(2)}) collective-permute-start(f32[2,32,512]{2,1,0:T(8,128)S(1)} %bitcast.171), channel_id=1, source_target_pairs={{0,2},{1,3},{2,0},{3,1},{4,6},{5,7},{6,4},{7,5},{8,10},{9,11},{10,... | collective-permute-start | bytes 393224 | tf_op jit(solution)/shard_map/ppermute | solution.py:269
  300.3 11.2 %collective-permute-start.39 = (f32[4,32,256]{2,1,0:T(8,128)S(1)}, f32[4,32,256]{2,1,0:T(8,128)S(1)}, u32[]{:S(2)}, u32[]{:S(2)}) collective-permute-start(f32[4,32,256]{2,1,0:T(8,128)S(1)} %collective-permute-done.34), channel_id=1, source_target_pairs={{0,1},{1,0},{2,3},{3,2},{4,5},{5,4},{6,7},{7,6},{8,9},{9,8},{10,11... | collective-permute-start | bytes 393224 | tf_op jit(solution)/shard_map/ppermute | solution.py:269
  307.8 16.1 %collective-permute-start.35 = (f32[16,32,256]{2,1,0:T(8,128)}, f32[16,32,256]{2,1,0:T(8,128)S(1)}, u32[]{:S(2)}, u32[]{:S(2)}) collective-permute-start(f32[16,32,256]{2,1,0:T(8,128)} %get-tuple-element.143), channel_id=1, source_target_pairs={{0,1},{1,0},{2,3},{3,2},{4,5},{5,4},{6,7},{7,6},{8,9},{9,8},{10,11... | collective-permute-start | bytes 1572872 | tf_op jit(solution)/shard_map/ppermute | solution.py:269
  308.4 15.5 %collective-permute-start.36 = (f32[16,32,256]{2,1,0:T(8,128)S(1)}, f32[16,32,256]{2,1,0:T(8,128)S(1)}, u32[]{:S(2)}, u32[]{:S(2)}) collective-permute-start(f32[16,32,256]{2,1,0:T(8,128)S(1)} %get-tuple-element.142), channel_id=1, source_target_pairs={{0,2},{1,3},{2,0},{3,1},{4,6},{5,7},{6,4},{7,5},{8,10},{9,11},{10,... | collective-permute-start | bytes 1572872 | tf_op jit(solution)/shard_map/ppermute | solution.py:269
  309.2 25.6 %collective-permute-start.37 = (f32[16,32,256]{2,1,0:T(8,128)S(1)}, f32[16,32,256]{2,1,0:T(8,128)S(1)}, u32[]{:S(2)}, u32[]{:S(2)}) collective-permute-start(f32[16,32,256]{2,1,0:T(8,128)S(1)} %get-tuple-element.141), channel_id=1, source_target_pairs={{0,3},{1,2},{2,1},{3,0},{4,7},{5,6},{6,5},{7,4},{8,11},{9,10},{10,... | collective-permute-start | bytes 1572872 | tf_op jit(solution)/shard_map/ppermute | solution.py:269
  312.4 22.6 %copy-start.13 = (f32[64,512]{1,0:T(8,128)S(1)}, f32[64,512]{1,0:T(8,128)}, u32[]{:S(2)}) copy-start(f32[64,512]{1,0:T(8,128)} %get-tuple-element.89) | copy-start | bytes 393220
  323.9 11.4 %copy-start.5 = (f32[16,32,256]{2,1,0:T(8,128)}, f32[16,32,256]{2,1,0:T(8,128)S(1)}, u32[]{:S(2)}) copy-start(f32[16,32,256]{2,1,0:T(8,128)S(1)} %collective-permute-done.35.g1) | copy-start | bytes 1572868
  323.9 11.4 %copy-start.6 = (f32[16,32,256]{2,1,0:T(8,128)}, f32[16,32,256]{2,1,0:T(8,128)S(1)}, u32[]{:S(2)}) copy-start(f32[16,32,256]{2,1,0:T(8,128)S(1)} %collective-permute-done.36.g2) | copy-start | bytes 1572868
  334.8 6.1 %collective-permute-start.41 = (f32[2,32,512]{2,1,0:T(8,128)S(1)}, f32[2,32,512]{2,1,0:T(8,128)S(1)}, u32[]{:S(2)}, u32[]{:S(2)}) collective-permute-start(f32[2,32,512]{2,1,0:T(8,128)S(1)} %collective-permute-done.33), channel_id=1, source_target_pairs={{0,1},{1,0},{2,3},{3,2},{4,5},{5,4},{6,7},{7,6},{8,9},{9,8},{10,11... | collective-permute-start | bytes 393224 | tf_op jit(solution)/shard_map/ppermute | solution.py:269
  335.1 5.8 %collective-permute-start.40 = (f32[2,32,512]{2,1,0:T(8,128)S(1)}, f32[2,32,512]{2,1,0:T(8,128)S(1)}, u32[]{:S(2)}, u32[]{:S(2)}) collective-permute-start(f32[2,32,512]{2,1,0:T(8,128)S(1)} %bitcast.172), channel_id=1, source_target_pairs={{0,1},{1,0},{2,3},{3,2},{4,5},{5,4},{6,7},{7,6},{8,9},{9,8},{10,11... | collective-permute-start | bytes 393224 | tf_op jit(solution)/shard_map/ppermute | solution.py:269
  (12 other events, 29.5 us)
Sparse Core Ops, SparseCore 0:
  134.8 67.6 all-gather.5
  259.3 52.8 all-gather.3
where the time goes:
time: 355 us; the launch traced here: 349 us
  starting transfers between devices  107 us (30%)
  Pallas kernels  104 us (29%)
  waiting for transfers between devices  88.7 us (25%)
  local copies, waits for them, and re-layouts  22.8 us (6%)
  between operations  14.9 us (4%)
  other arithmetic  12.1 us (3%)
    ppermute x33, starting transfers between devices, across(): return lax.ppermute(x, 'col', [(i, i ^ k) for i in range(4)])  55.2 us
    all_to_all x6, starting transfers between devices, exchange(): return lax.all_to_all(x, axis, split_axis=0, concat_axis=0, tiled=True)  41.5 us
    all_to_all x6, waiting for transfers between devices, exchange(): return lax.all_to_all(x, axis, split_axis=0, concat_axis=0, tiled=True)  32.7 us
    ppermute x2, waiting for transfers between devices, local(): lax.ppermute(tile_top[:, 128 * j:128 * j + 128], ('child', 'row', 'col'),...  25.6 us
    pallas_call x1, Pallas kernels, local(): call(second_kernel, (sds((64, 512)), sds((64, 512), BF16)), 1, 4, [pltpu....  24.8 us
    pallas_call x1, Pallas kernels, local(): call(head_kernel, (sds((512, 512)), sds((64, 512)), sds((64, 512), BF16))...  21.7 us
    pallas_call x1, Pallas kernels, local(): call(root_kernel, sds((512, 512)), 1, 4, CHOL, 2 * 10 ** 10, 'root')  20.9 us
    ppermute x33, waiting for transfers between devices, across(): return lax.ppermute(x, 'col', [(i, i ^ k) for i in range(4)])  20 us
  transfers between devices with their start and end apart: 50, of which 15 were waited for; matrix products, arithmetic and copies ran while one was open for 7% of the time, Pallas kernels for 30%

commit v1 on v0

--- a/solution.py
+++ b/solution.py
@@ -162,17 +162,18 @@
         out[...] = f - dot16(jnp.concatenate([u0, u1], axis=1), upan, 1, 1)
 
 
-def bulk_kernel(q_ref, panel_ref, u0_ref, u1_ref, f_ref, c0, c1, c2, c3, own_ref, other_ref, first_ref, send_ref):
-    ubulk = columns_of((c0, c1, c2, c3), q_ref)
+def corner_kernel(q_ref, panel_ref, u0_ref, u1_ref, f_ref, c0, c1, c2, c3, first_ref, send_ref):
+    f, u0, u1 = [jnp.concatenate([picked(panel_ref[i], x) for i in range(4)], axis=0) for x in (f_ref, u0_ref, u1_ref)]
+    s = f - dot16(jnp.concatenate([u0, u1], axis=1), columns_of((c0, c1, c2, c3), q_ref), 1, 1)
+    first_ref[...] = s[:, 0:256]
+    send_ref[...] = s[:, 256:512]
+
+
+def bulk_kernel(q_ref, u0_ref, u1_ref, f_ref, c0, c1, c2, c3, own_ref, other_ref):
     rows = jnp.concatenate([u0_ref[8:32].reshape(768, 512), u1_ref[8:32].reshape(768, 512)], axis=1)
-    s = f_ref[8:32].reshape(768, 512) - dot16(rows, ubulk, 1, 1)
+    s = f_ref[8:32].reshape(768, 512) - dot16(rows, columns_of((c0, c1, c2, c3), q_ref), 1, 1)
     own_ref[...] = s[:, 0:256]
     other_ref[...] = s[:, 256:512]
-    for m in range(4):
-        b = panel_ref[m]
-        rows = pl.ds(pl.multiple_of(32 * jnp.maximum(b, 0), 32), 32)
-        first_ref[m] = jnp.where(b >= 0, own_ref[rows, :], 0.0)
-        send_ref[m] = jnp.where(b >= 0, other_ref[rows, :], 0.0)
 
 
 def root_kernel(q_ref, t0, t1, t2, t3, inv_ref, a, g):
@@ -347,16 +348,7 @@
     panel_y = y[1][:, 0:512]
     placed_panel = call(place_panel_kernel, sds((64, 512)), 1, 1, name="place_panel")(panel_idx, panel_y)
 
-    raw_rows = 0.0
-    tile_top = after(root_front[0:512], pack)
-    for j in range(2):
-        pairs = []
-        for g in range(32):
-            m = 2 * g + j
-            pairs.append((4 * g, (m // 32 * 16 + m % 16) * 4 + m // 16))
-        raw_rows += lax.ppermute(tile_top[:, 128 * j:128 * j + 128], ("child", "row", "col"), pairs)
-    d00, placed_panel, raw_rows = lax.optimization_barrier((d00, placed_panel, raw_rows))
-    raw_rows = raw_rows.T
+    d00, placed_panel = lax.optimization_barrier((d00, placed_panel))
     inv0, p0, u0 = call(
         head_kernel, (sds((512, 512)), sds((64, 512)), sds((64, 512), BF16)), 0, 2, CHOL, 2 * 10**10, "head")(d00, left)
     f_panel = lax.all_gather(placed_panel, "row").reshape(32, 32, 512)
@@ -375,7 +367,16 @@
     placed = call(place_kernel, sds((16, 64, 512)), 1, 1, name="place")(bulk_idx, wide)
     factor0 = after(factor0, u1)
     factor0 = in_order(factor0, across(factor0, 1), far0, across(far0, 1), q)
-    u1_all, placed, factor0 = lax.optimization_barrier((u1_all, placed, factor0))
+    raw_rows = 0.0
+    tile_top = after(root_front[0:512], u1)
+    for j in range(2):
+        pairs = []
+        for g in range(32):
+            m = 2 * g + j
+            pairs.append((4 * g, (m // 32 * 16 + m % 16) * 4 + m // 16))
+        raw_rows += lax.ppermute(tile_top[:, 128 * j:128 * j + 128], ("child", "row", "col"), pairs)
+    u1_all, placed, factor0, raw_rows = lax.optimization_barrier((u1_all, placed, factor0, raw_rows))
+    raw_rows = raw_rows.T
     f_bulk = exchange(placed, "row").reshape(32, 32, 512)
 
     some = sds((4, 32, 1024), BF16)
@@ -396,10 +397,12 @@
     panel = lax.all_gather(z, "row", tiled=True)
     t_all = around(t.reshape(4, 32, 512))
 
-    half, block = sds((768, 256)), sds((4, 32, 256))
-    own, other, first, sent = call(bulk_kernel, (half, half, block, block), 2, 7, flops=2 * 10**9, name="bulk")(
+    half, block = sds((768, 256)), sds((128, 256))
+    first, sent = call(corner_kernel, (block, block), 2, 7, flops=10**9, name="corner")(
         at, panel_idx, u0_all, u1_all, f_bulk, *u_bulk)
-    head_cols = top.reshape(4, 32, 256) + first + swap_child(sent)
+    own, other = call(bulk_kernel, (half, half), 1, 7, flops=4 * 10**9, name="bulk")(
+        at, u0_all, u1_all, after(f_bulk, sent), *u_bulk)
+    head_cols = (top + first + swap_child(sent)).reshape(4, 32, 256)
     t_all, z, other, head_cols = lax.optimization_barrier((t_all, z, other, head_cols))
     factor1 = p1.reshape(2, 32, 512)
     far1 = across(after(factor1, other), 2)

time: 355 us -> 331 us (0.932)
  waiting for transfers between devices: 88.7 us -> 67.4 us
  starting transfers between devices: 107 us -> 101 us
  Pallas kernels: 104 us -> 108 us
    all_to_all x6, waiting for transfers between devices: 32.7 us -> 12.5 us  [exchange(): return lax.all_to_all(x, axis, split_axis=0, concat_axis=0, tiled=True)]
    ppermute x2, waiting for transfers between devices: 25.6 us -> 10.8 us  [local(): lax.ppermute(tile_top[:, 128 * j:128 * j + 128], ('child', 'row', 'col'),...]
    ppermute x33, waiting for transfers between devices: 20 us -> 30.5 us  [across(): return lax.ppermute(x, 'col', [(i, i ^ k) for i in range(4)])]
    pallas_call x1 -> x2, Pallas kernels: 4.69 us -> 8.43 us  [the longest x1 4.77 us: local(): call(bulk_kernel, (half, half), 1, 7, flops=4 * 10 ** 9, name='bulk')]
  transfers between devices with their start and end apart: 50 -> 50, of which waited for: 15 -> 14; matrix products, arithmetic and copies ran while one was open for 7% -> 7% of each run, Pallas kernels for 30% -> 33%
where the time goes in v1:
time: 331 us; the launch traced here: 326 us
  Pallas kernels  108 us (33%)
  starting transfers between devices  101 us (31%)
  waiting for transfers between devices  67.4 us (20%)
  local copies, waits for them, and re-layouts  22.3 us (7%)
  between operations  14.9 us (5%)
  other arithmetic  12.3 us (4%)
    ppermute x33, starting transfers between devices, across(): return lax.ppermute(x, 'col', [(i, i ^ k) for i in range(4)])  53 us
    all_to_all x6, starting transfers between devices, exchange(): return lax.all_to_all(x, axis, split_axis=0, concat_axis=0, tiled=True)  39.4 us
    ppermute x33, waiting for transfers between devices, across(): return lax.ppermute(x, 'col', [(i, i ^ k) for i in range(4)])  30.5 us
    pallas_call x1, Pallas kernels, local(): call(second_kernel, (sds((64, 512)), sds((64, 512), BF16)), 1, 4, [pltpu....  24.8 us
    pallas_call x1, Pallas kernels, local(): call(head_kernel, (sds((512, 512)), sds((64, 512)), sds((64, 512), BF16))...  21.7 us
    pallas_call x1, Pallas kernels, local(): call(root_kernel, sds((512, 512)), 1, 4, CHOL, 2 * 10 ** 10, 'root')  20.9 us
    ppermute x4, waiting for transfers between devices, swap_child(): return lax.ppermute(x, 'child', [(0, 1), (1, 0)])  13.3 us
    all_to_all x6, waiting for transfers between devices, exchange(): return lax.all_to_all(x, axis, split_axis=0, concat_axis=0, tiled=True)  12.5 us
  transfers between devices with their start and end apart: 50, of which 14 were waited for; matrix products, arithmetic and copies ran while one was open for 7% of the time, Pallas kernels for 33%

profile of v1, /device:TPU:1, one launch (start us, length us, event | category | flops | bytes accessed | tf_op | source)
XLA Modules:
  0.0 325.5 jit_solution(8320201722554434253)
XLA Ops:
  7.2 1.2 slice.81
  8.8 1.0 slice_bitcast_fusion.1
  9.7 1.4 collective-permute-start
  11.2 1.4 collective-permute-start.1
  12.6 1.4 collective-permute-start.2
  14.1 1.3 fusion
  16.3 7.5 %all-to-all-start = ((f32[16,4,1536]{2,1,0:T(4,128)}), f32[16,4,1536]{2,1,0:T(4,128)S(1)}, u32[]{:S(2)}, u32[]{:S(2)}) async-start(f32[16,4,1536]{2,1,0:T(4,128)} %reshape.144), calls=%async_computation | async-start | bytes 786432 | tf_op jit(solution)/shard_map/all_to_all | solution.py:254
  23.8 8.0 %all-to-all-done = f32[16,4,1536]{2,1,0:T(4,128)S(1)} async-done(((f32[16,4,1536]{2,1,0:T(4,128)}), f32[16,4,1536]{2,1,0:T(4,128)S(1)}, u32[]{:S(2)}, u32[]{:S(2)}) %all-to-all-start) | async-done | bytes 393248 | tf_op jit(solution)/shard_map/all_to_all | solution.py:254
  31.7 16.6 %collective-permute-start.4 = (f32[2,4,512]{2,1,0:T(4,128)S(1)}, f32[2,4,512]{2,1,0:T(4,128)S(1)}, u32[]{:S(2)}, u32[]{:S(2)}) collective-permute-start(f32[2,4,512]{2,1,0:T(4,128)S(1)} %slice.113), channel_id=1, source_target_pairs={{0,2},{1,3},{2,0},{3,1},{4,6},{5,7},{6,4},{7,5},{8,10},{9,11},{10,... | collective-permute-start | bytes 49160 | tf_op jit(solution)/shard_map/ppermute | solution.py:270
  48.6 0.9 collective-permute-done.4
  49.5 2.4 collective-permute-start.5
  52.8 1.2 broadcast_in_dim.112
  54.0 3.7 %all-to-all-start.1 = ((f32[16,8,4,512]{3,2,1,0:T(4,128)}), f32[16,8,4,512]{3,2,1,0:T(4,128)S(1)}, u32[]{:S(2)}, u32[]{:S(2)}) async-start(f32[16,8,4,512]{3,2,1,0:T(4,128)} %broadcast_in_dim.112), calls=%async_computation.1 | async-start | bytes 2097152 | tf_op jit(solution)/shard_map/all_to_all | solution.py:254
  58.7 0.9 collective-permute-start.7
  60.1 3.2 collective-permute-done.7
  63.3 1.3 collective-permute-start.8
  66.0 2.3 collective-permute-start.11
  69.2 4.6 %all-to-all-done.1.d_ref = f32[16,8,4,512]{3,2,1,0:T(4,128)S(1)} async-done(((f32[16,8,4,512]{3,2,1,0:T(4,128)}), f32[16,8,4,512]{3,2,1,0:T(4,128)S(1)}, u32[]{:S(2)}, u32[]{:S(2)}) %all-to-all-start.1) | async-done | bytes 1048608 | tf_op jit(solution)/shard_map/all_to_all | solution.py:254
  73.7 2.0 broadcast_in_dim.113
  75.7 4.5 %all-to-all-start.2 = ((f32[16,9,4,1024]{3,2,1,0:T(4,128)}), f32[16,9,4,1024]{3,2,1,0:T(4,128)}, u32[]{:S(2)}, u32[]{:S(2)}) async-start(f32[16,9,4,1024]{3,2,1,0:T(4,128)} %broadcast_in_dim.113), calls=%async_computation.2 | async-start | bytes 4718592 | tf_op jit(solution)/shard_map/all_to_all | solution.py:254
  81.2 2.0 fusion.2
  84.6 1.6 place_panel.1
  86.2 21.7 %head.1 = (f32[512,512]{1,0:T(8,128)}, f32[64,512]{1,0:T(8,128)}, bf16[64,512]{1,0:T(8,128)(2,1)}) custom-call(f32[16,8,4,512]{3,2,1,0:T(4,128)} %copy-done.4, f32[64,512]{1,0:T(8,128)} %get-tuple-element.179.c_ref), custom_call_target="tpu_custom_call" | custom-call | flops 20000000000 | bytes 1048576 | tf_op jit(solution)/shard_map/head/pallas_call | solution.py:352
  108.0 1.8 collective-permute-start.12
  109.8 1.9 broadcast_in_dim.117
  111.8 6.8 %all-to-all-start.3 = ((bf16[16,2,32,512]{3,2,1,0:T(8,128)(2,1)}), bf16[16,2,32,512]{3,2,1,0:T(8,128)(2,1)S(1)}, u32[]{:S(2)}, u32[]{:S(2)}) async-start(bf16[16,2,32,512]{3,2,1,0:T(8,128)(2,1)} %broadcast_in_dim.117), calls=%async_computation.3 | async-start | bytes 2097152 | tf_op jit(solution)/shard_map/all_to_all | solution.py:254
  118.5 24.8 %second.1 = (f32[64,512]{1,0:T(8,128)}, bf16[64,512]{1,0:T(8,128)(2,1)}) custom-call(s32[1]{0:T(128)} %bitcast.mask_ref, f32[16,9,4,1024]{3,2,1,0:T(4,128)} %all-to-all-done.2.d_ref, f32[512,512]{1,0:T(8,128)} %get-tuple-element.80.inv0_ref, f32[64,512]{1,0:T(8,128)} %get-tuple-element.178.c_ref, bf16[64,512]{1,0:T(8,128)(2,1)} %get-tuple-element.78.u0_ref), custom_call_target="tpu_custom_call" | custom-call | flops 30000001024 | bytes 1048576 | tf_op jit(solution)/shard_map/second/pallas_call | solution.py:360
  143.3 2.0 broadcast_in_dim.119
  145.4 6.8 %all-to-all-start.4 = ((bf16[16,2,32,512]{3,2,1,0:T(8,128)(2,1)}), bf16[16,2,32,512]{3,2,1,0:T(8,128)(2,1)S(1)}, u32[]{:S(2)}, u32[]{:S(2)}) async-start(bf16[16,2,32,512]{3,2,1,0:T(8,128)(2,1)} %broadcast_in_dim.119), calls=%async_computation.4 | async-start | bytes 2097152 | tf_op jit(solution)/shard_map/all_to_all | solution.py:254
  153.0 2.1 pad_maximum_fusion.1.y_ref
  155.1 3.1 collective-permute-start.13
  158.4 1.3 collective-permute-start.15
  160.4 3.4 %place.1 = f32[16,64,512]{2,1,0:T(8,128)} custom-call(s32[64]{0:T(128)} %select_reduce_fusion.bulk_ref, f32[64,3072]{1,0:T(8,128)} %pad_maximum_fusion.1.y_ref), custom_call_target="tpu_custom_call" | custom-call | bytes 1048576 | tf_op jit(solution)/shard_map/place/pallas_call | solution.py:367
  163.9 10.8 %collective-permute-done.15 = f32[512,128]{0,1:T(8,128)S(1)} collective-permute-done((f32[512,128]{0,1:T(8,128)S(1)}, f32[512,128]{0,1:T(8,128)S(1)}, u32[]{:S(2)}, u32[]{:S(2)}) %collective-permute-start.15) | collective-permute-done | bytes 262176 | tf_op jit(solution)/shard_map/ppermute | solution.py:377
  174.7 1.0 copy-done.1
  175.7 10.4 %all-to-all-start.5 = ((f32[16,64,512]{2,1,0:T(8,128)}), f32[16,64,512]{2,1,0:T(8,128)}, u32[]{:S(2)}, u32[]{:S(2)}) async-start(f32[16,64,512]{2,1,0:T(8,128)} %place.1), calls=%async_computation.5 | async-start | bytes 4194304 | tf_op jit(solution)/shard_map/all_to_all | solution.py:254
  186.9 2.4 select.17
  189.3 9.8 %collective-permute-done.18.c2 = bf16[4,32,1024]{2,1,0:T(8,128)(2,1)S(1)} collective-permute-done((bf16[4,32,1024]{2,1,0:T(8,128)(2,1)}, bf16[4,32,1024]{2,1,0:T(8,128)(2,1)S(1)}, u32[]{:S(2)}, u32[]{:S(2)}) %collective-permute-start.18) | collective-permute-done | bytes 262176 | tf_op jit(solution)/shard_map/ppermute | solution.py:270
  199.7 1.0 fusion.12
  200.8 1.0 collective-permute-start.25
  202.6 4.0 %panel.1 = (f32[128,512]{1,0:T(8,128)}, f32[128,512]{1,0:T(8,128)}) custom-call(s32[1]{0:T(128)} %bitcast.41.q_ref, s32[4]{0:T(128)} %get-tuple-element.138.rows_ref, s32[4]{0:T(128)} %slice_bitcast_fusion.6.panel_ref, bf16[32,32,512]{2,1,0:T(8,128)(2,1)} %bitcast.147, bf16[32,32,512]{2,1,0:T(8,128)(2,1)} %bitcast.151, f32[32,32,512]{2,1,0:T(8,128)} %bitcast.159, ...), custom_call_target="tpu_custom_call" | custom-call | flops 1000000000 | bytes 1048576 | tf_op jit(solution)/shard_map/panel/pallas_call | solution.py:387
  206.6 2.9 collective-permute-done.20.c2
  209.5 1.0 dynamic-slice_bitcast_fusion.9
  211.3 3.2 collective-permute-start.23
  214.5 1.0 fusion.1
  215.5 1.9 collective-permute-start.24
  218.9 6.4 %collective-permute-done.24 = f32[128,512]{1,0:T(8,128)S(1)} collective-permute-done((f32[128,512]{1,0:T(8,128)S(1)}, f32[128,512]{1,0:T(8,128)S(1)}, u32[]{:S(2)}, u32[]{:S(2)}) %collective-permute-start.24) | collective-permute-done | bytes 262176 | tf_op jit(solution)/shard_map/ppermute | solution.py:301
  225.5 6.9 %collective-permute-done.30 = f32[128,512]{1,0:T(8,128)S(1)} collective-permute-done((f32[128,512]{1,0:T(8,128)S(1)}, f32[128,512]{1,0:T(8,128)S(1)}, u32[]{:S(2)}, u32[]{:S(2)}) %collective-permute-start.30) | collective-permute-done | bytes 262176 | tf_op jit(solution)/shard_map/ppermute | solution.py:301
  233.8 2.7 collective-permute-start.28
  236.6 3.7 %corner.1 = (f32[128,256]{1,0:T(8,128)}, f32[128,256]{1,0:T(8,128)}) custom-call(s32[1]{0:T(128)} %bitcast.41.q_ref, s32[4]{0:T(128)} %slice_bitcast_fusion.6.panel_ref, bf16[32,32,512]{2,1,0:T(8,128)(2,1)} %bitcast.148, bf16[32,32,512]{2,1,0:T(8,128)(2,1)} %bitcast.152, f32[32,32,512]{2,1,0:T(8,128)} %bitcast.54.f_ref, ...), custom_call_target="tpu_custom_call" | custom-call | flops 1000000000 | bytes 1048576 | tf_op jit(solution)/shard_map/corner/pallas_call | solution.py:401
  240.3 2.4 collective-permute-start.27
  242.8 2.2 collective-permute-start.29
  245.0 4.8 %bulk.1 = (f32[768,256]{1,0:T(8,128)}, f32[768,256]{1,0:T(8,128)}) custom-call(s32[1]{0:T(128)} %bitcast.41.q_ref, bf16[32,32,512]{2,1,0:T(8,128)(2,1)} %bitcast.149, bf16[32,32,512]{2,1,0:T(8,128)(2,1)} %bitcast.153, f32[32,32,512]{2,1,0:T(8,128)} %bitcast.54.f_ref, bf16[4,32,1024]{2,1,0:T(8,128)(2,1)} %get-tuple-element.105.c0, ...), custom_call_target="tpu_custom_call" | custom-call | flops 4000000000 | bytes 1048576 | tf_op jit(solution)/shard_map/bulk/pallas_call | solution.py:403
  249.8 3.3 %collective-permute-start.34 = (f32[4,32,256]{2,1,0:T(8,128)S(1)}, f32[4,32,256]{2,1,0:T(8,128)S(1)}, u32[]{:S(2)}, u32[]{:S(2)}) collective-permute-start(f32[4,32,256]{2,1,0:T(8,128)S(1)} %bitcast.165), channel_id=1, source_target_pairs={{0,2},{1,3},{2,0},{3,1},{4,6},{5,7},{6,4},{7,5},{8,10},{9,11},{10,... | collective-permute-start | bytes 393224 | tf_op jit(solution)/shard_map/ppermute | solution.py:270
  253.7 20.9 %root.1.inv_ref = f32[512,512]{1,0:T(8,128)} custom-call(s32[1]{0:T(128)} %bitcast.41.q_ref, f32[4,32,512]{2,1,0:T(8,128)} %bitcast.171, f32[4,32,512]{2,1,0:T(8,128)} %copy-done.29, f32[4,32,512]{2,1,0:T(8,128)} %copy-done.28, f32[4,32,512]{2,1,0:T(8,128)} %copy-done.30), custom_call_target="tpu_custom_call" | custom-call | flops 20000000000 | bytes 1048576 | tf_op jit(solution)/shard_map/root/pallas_call | solution.py:410
  274.7 1.9 collective-permute-done.33
  276.6 0.9 collective-permute-start.39
  277.5 3.7 %spread.1 = f32[64,32,256]{2,1,0:T(8,128)} custom-call(s32[64]{0:T(128)} %bitcast.185, s32[64]{0:T(128)} %get-tuple-element.193.theirs_ref, f32[24,32,256]{2,1,0:T(8,128)} %bitcast.163, f32[24,32,256]{2,1,0:T(8,128)} %bitcast.164), custom_call_target="tpu_custom_call" | custom-call | bytes 1048576 | tf_op jit(solution)/shard_map/spread/pallas_call | solution.py:412
  281.2 2.9 dynamic-slice_bitcast_fusion
  284.7 3.0 collective-permute-start.36
  288.8 11.5 %factor.1 = (f32[2048,512]{1,0:T(8,128)}, bf16[2048,512]{1,0:T(8,128)(2,1)}, bf16[512,256]{1,0:T(8,128)(2,1)}) custom-call(s32[2]{0:T(128)} %add_convert_fusion.flag_ref, f32[2048,512]{1,0:T(8,128)} %all-gather.4.cloned.1.call-done.panel_ref, f32[512,512]{1,0:T(8,128)} %root.1.inv_ref, f32[4,4,32,256]{3,2,1,0:T(8,128)} %pad_maximum_fusion.3.cp_ref), custom_call_target="tpu_custom_call" | custom-call | flops 10000000000 | bytes 1048576 | tf_op jit(solution)/shard_map/factor/pallas_call | solution.py:422
  300.3 10.8 %collective-permute-done.37.g3 = f32[16,32,256]{2,1,0:T(8,128)S(1)} collective-permute-done((f32[16,32,256]{2,1,0:T(8,128)S(1)}, f32[16,32,256]{2,1,0:T(8,128)S(1)}, u32[]{:S(2)}, u32[]{:S(2)}) %collective-permute-start.37) | collective-permute-done | bytes 524320 | tf_op jit(solution)/shard_map/ppermute | solution.py:270
  311.9 5.4 %last.1 = f32[2048,256]{1,0:T(8,128)} custom-call(s32[1]{0:T(128)} %bitcast.41.q_ref, bf16[2048,512]{1,0:T(8,128)(2,1)} %get-tuple-element.127.u_ref, bf16[512,256]{1,0:T(8,128)(2,1)} %get-tuple-element.132.ug_ref, f32[2048,256]{1,0:T(8,128)} %root_ref.1, f32[16,32,256]{2,1,0:T(8,128)} %get-tuple-element.133.g0, f32[16,32,256]{2,1,0:T(8,128)} %copy-done.6, ...), custom_call_target="tpu_custom_call" | custom-call | tf_op jit(solution)/shard_map/last/pallas_call | solution.py:437
  317.5 1.0 copy.22
  (172 shorter events, 20.2 us)
Async XLA Ops:
  9.7 38.6 %copy-start.27 = (s32[2,24]{1,0:T(2,128)S(1)}, s32[2,24]{1,0:T(2,128)}, u32[]{:S(2)}) copy-start(s32[2,24]{1,0:T(2,128)} %param.5) | copy-start | bytes 580
  9.7 4.4 %collective-permute-start = (f32[64,1536]{1,0:T(8,128)}, f32[64,1536]{1,0:T(8,128)}, u32[]{:S(2)}, u32[]{:S(2)}) collective-permute-start(f32[64,1536]{1,0:T(8,128)} %get-tuple-element.152), channel_id=1, source_target_pairs={{0,1},{4,5},{8,9},{12,13},{16,17},{20,21},{24,25},{28,29},{32,33},... | collective-permute-start | bytes 1179656 | tf_op jit(solution)/shard_map/ppermute | solution.py:283
  11.2 3.0 collective-permute-start.1
  12.6 1.5 collective-permute-start.2
  16.3 15.4 %all-to-all-start = ((f32[16,4,1536]{2,1,0:T(4,128)}), f32[16,4,1536]{2,1,0:T(4,128)S(1)}, u32[]{:S(2)}, u32[]{:S(2)}) async-start(f32[16,4,1536]{2,1,0:T(4,128)} %reshape.144), calls=%async_computation | async-start | bytes 786432 | tf_op jit(solution)/shard_map/all_to_all | solution.py:254
  31.7 17.8 %collective-permute-start.4 = (f32[2,4,512]{2,1,0:T(4,128)S(1)}, f32[2,4,512]{2,1,0:T(4,128)S(1)}, u32[]{:S(2)}, u32[]{:S(2)}) collective-permute-start(f32[2,4,512]{2,1,0:T(4,128)S(1)} %slice.113), channel_id=1, source_target_pairs={{0,2},{1,3},{2,0},{3,1},{4,6},{5,7},{6,4},{7,5},{8,10},{9,11},{10,... | collective-permute-start | bytes 49160 | tf_op jit(solution)/shard_map/ppermute | solution.py:270
  48.5 3.5 %collective-permute-start.3 = (f32[2,4,512]{2,1,0:T(4,128)S(1)}, f32[2,4,512]{2,1,0:T(4,128)S(1)}, u32[]{:S(2)}, u32[]{:S(2)}) collective-permute-start(f32[2,4,512]{2,1,0:T(4,128)S(1)} %slice.113), channel_id=1, source_target_pairs={{0,1},{1,0},{2,3},{3,2},{4,5},{5,4},{6,7},{7,6},{8,9},{9,8},{10,11... | collective-permute-start | bytes 49160 | tf_op jit(solution)/shard_map/ppermute | solution.py:270
  49.5 3.3 %collective-permute-start.5 = (f32[2,4,512]{2,1,0:T(4,128)S(1)}, f32[2,4,512]{2,1,0:T(4,128)S(1)}, u32[]{:S(2)}, u32[]{:S(2)}) collective-permute-start(f32[2,4,512]{2,1,0:T(4,128)S(1)} %collective-permute-done.4), channel_id=1, source_target_pairs={{0,1},{1,0},{2,3},{3,2},{4,5},{5,4},{6,7},{7,6},{8,9},{9,8},{10,11... | collective-permute-start | bytes 49160 | tf_op jit(solution)/shard_map/ppermute | solution.py:270
  54.0 19.7 %all-to-all-start.1 = ((f32[16,8,4,512]{3,2,1,0:T(4,128)}), f32[16,8,4,512]{3,2,1,0:T(4,128)S(1)}, u32[]{:S(2)}, u32[]{:S(2)}) async-start(f32[16,8,4,512]{3,2,1,0:T(4,128)} %broadcast_in_dim.112), calls=%async_computation.1 | async-start | bytes 2097152 | tf_op jit(solution)/shard_map/all_to_all | solution.py:254
  58.2 128.0 %copy-start.26 = (s32[1,64]{1,0:T(1,128)}, s32[1,64]{1,0:T(1,128)S(1)}, u32[]{:S(2)}) copy-start(s32[1,64]{1,0:T(1,128)S(1)} %get-tuple-element.194) | copy-start | bytes 772
  58.7 4.6 %collective-permute-start.7 = (f32[2,4,1024]{2,1,0:T(4,128)S(1)}, f32[2,4,1024]{2,1,0:T(4,128)S(1)}, u32[]{:S(2)}, u32[]{:S(2)}) collective-permute-start(f32[2,4,1024]{2,1,0:T(4,128)S(1)} %slice.114), channel_id=1, source_target_pairs={{0,2},{1,3},{2,0},{3,1},{4,6},{5,7},{6,4},{7,5},{8,10},{9,11},{10,... | collective-permute-start | bytes 98312 | tf_op jit(solution)/shard_map/ppermute | solution.py:270
  59.6 9.4 %collective-permute-start.6 = (f32[2,4,1024]{2,1,0:T(4,128)S(1)}, f32[2,4,1024]{2,1,0:T(4,128)S(1)}, u32[]{:S(2)}, u32[]{:S(2)}) collective-permute-start(f32[2,4,1024]{2,1,0:T(4,128)S(1)} %slice.114), channel_id=1, source_target_pairs={{0,1},{1,0},{2,3},{3,2},{4,5},{5,4},{6,7},{7,6},{8,9},{9,8},{10,11... | collective-permute-start | bytes 98312 | tf_op jit(solution)/shard_map/ppermute | solution.py:270
  63.3 5.8 %collective-permute-start.8 = (f32[2,4,1024]{2,1,0:T(4,128)S(1)}, f32[2,4,1024]{2,1,0:T(4,128)S(1)}, u32[]{:S(2)}, u32[]{:S(2)}) collective-permute-start(f32[2,4,1024]{2,1,0:T(4,128)S(1)} %collective-permute-done.7), channel_id=1, source_target_pairs={{0,1},{1,0},{2,3},{3,2},{4,5},{5,4},{6,7},{7,6},{8,9},{9,8},{10,11... | collective-permute-start | bytes 98312 | tf_op jit(solution)/shard_map/ppermute | solution.py:270
  65.4 15.8 %collective-permute-start.10 = (f32[64,1024]{1,0:T(8,128)}, f32[64,1024]{1,0:T(8,128)}, u32[]{:S(2)}, u32[]{:S(2)}) collective-permute-start(f32[64,1024]{1,0:T(8,128)} %get-tuple-element.155), channel_id=1, source_target_pairs={{0,3},{1,2},{2,1},{3,0},{4,7},{5,6},{6,5},{7,4},{8,11},{9,10},{10,... | collective-permute-start | bytes 786440 | tf_op jit(solution)/shard_map/ppermute | solution.py:270
  66.0 15.2 %collective-permute-start.11 = (f32[64,1024]{1,0:T(8,128)}, f32[64,1024]{1,0:T(8,128)}, u32[]{:S(2)}, u32[]{:S(2)}) collective-permute-start(f32[64,1024]{1,0:T(8,128)} %get-tuple-element.154), channel_id=1, source_target_pairs={{0,2},{1,3},{2,0},{3,1},{4,6},{5,7},{6,4},{7,5},{8,10},{9,11},{10,... | collective-permute-start | bytes 786440 | tf_op jit(solution)/shard_map/ppermute | solution.py:270
  68.3 12.9 %collective-permute-start.9 = (f32[64,1024]{1,0:T(8,128)S(1)}, f32[64,1024]{1,0:T(8,128)}, u32[]{:S(2)}, u32[]{:S(2)}) collective-permute-start(f32[64,1024]{1,0:T(8,128)S(1)} %get-tuple-element.153), channel_id=1, source_target_pairs={{0,1},{1,0},{2,3},{3,2},{4,5},{5,4},{6,7},{7,6},{8,9},{9,8},{10,11... | collective-permute-start | bytes 786440 | tf_op jit(solution)/shard_map/ppermute | solution.py:270
  75.7 34.1 %all-to-all-start.2 = ((f32[16,9,4,1024]{3,2,1,0:T(4,128)}), f32[16,9,4,1024]{3,2,1,0:T(4,128)}, u32[]{:S(2)}, u32[]{:S(2)}) async-start(f32[16,9,4,1024]{3,2,1,0:T(4,128)} %broadcast_in_dim.113), calls=%async_computation.2 | async-start | bytes 4718592 | tf_op jit(solution)/shard_map/all_to_all | solution.py:254
  80.2 121.6 %all-gather.6.cloned.1.call-start = ((), (), s32[]{:S(2)}) async-start(), calls=%async_computation.7 | async-start | bytes 2228224 | tf_op jit(solution)/shard_map/all_gather | solution.py:354
  108.0 35.4 %collective-permute-start.12 = (f32[2,32,512]{2,1,0:T(8,128)}, f32[2,32,512]{2,1,0:T(8,128)S(1)}, u32[]{:S(2)}, u32[]{:S(2)}) collective-permute-start(f32[2,32,512]{2,1,0:T(8,128)} %bitcast.178), channel_id=1, source_target_pairs={{0,2},{1,3},{2,0},{3,1},{4,6},{5,7},{6,4},{7,5},{8,10},{9,11},{10,... | collective-permute-start | bytes 393224 | tf_op jit(solution)/shard_map/ppermute | solution.py:270
  111.8 31.6 %all-to-all-start.3 = ((bf16[16,2,32,512]{3,2,1,0:T(8,128)(2,1)}), bf16[16,2,32,512]{3,2,1,0:T(8,128)(2,1)S(1)}, u32[]{:S(2)}, u32[]{:S(2)}) async-start(bf16[16,2,32,512]{3,2,1,0:T(8,128)(2,1)} %broadcast_in_dim.117), calls=%async_computation.3 | async-start | bytes 2097152 | tf_op jit(solution)/shard_map/all_to_all | solution.py:254
  143.3 9.7 %copy-start = (bf16[16,2,32,512]{3,2,1,0:T(8,128)(2,1)}, bf16[16,2,32,512]{3,2,1,0:T(8,128)(2,1)S(1)}, u32[]{:S(2)}) copy-start(bf16[16,2,32,512]{3,2,1,0:T(8,128)(2,1)S(1)} %all-to-all-done.3) | copy-start | bytes 3145732
  145.4 29.4 %all-to-all-start.4 = ((bf16[16,2,32,512]{3,2,1,0:T(8,128)(2,1)}), bf16[16,2,32,512]{3,2,1,0:T(8,128)(2,1)S(1)}, u32[]{:S(2)}, u32[]{:S(2)}) async-start(bf16[16,2,32,512]{3,2,1,0:T(8,128)(2,1)} %broadcast_in_dim.119), calls=%async_computation.4 | async-start | bytes 2097152 | tf_op jit(solution)/shard_map/all_to_all | solution.py:254
  155.1 8.6 %copy-start.24 = (f32[2,32,512]{2,1,0:T(8,128)S(1)}, f32[2,32,512]{2,1,0:T(8,128)}, u32[]{:S(2)}) copy-start(f32[2,32,512]{2,1,0:T(8,128)} %copy-done.23) | copy-start | bytes 393220
  155.1 8.6 %collective-permute-start.13 = (f32[2,32,512]{2,1,0:T(8,128)}, f32[2,32,512]{2,1,0:T(8,128)S(1)}, u32[]{:S(2)}, u32[]{:S(2)}) collective-permute-start(f32[2,32,512]{2,1,0:T(8,128)} %bitcast.179), channel_id=1, source_target_pairs={{0,1},{1,0},{2,3},{3,2},{4,5},{5,4},{6,7},{7,6},{8,9},{9,8},{10,11... | collective-permute-start | bytes 393224 | tf_op jit(solution)/shard_map/ppermute | solution.py:270
  158.3 5.5 %collective-permute-start.14 = (f32[2,32,512]{2,1,0:T(8,128)}, f32[2,32,512]{2,1,0:T(8,128)S(1)}, u32[]{:S(2)}, u32[]{:S(2)}) collective-permute-start(f32[2,32,512]{2,1,0:T(8,128)} %copy-done.23), channel_id=1, source_target_pairs={{0,1},{1,0},{2,3},{3,2},{4,5},{5,4},{6,7},{7,6},{8,9},{9,8},{10,11... | collective-permute-start | bytes 393224 | tf_op jit(solution)/shard_map/ppermute | solution.py:270
  158.4 16.3 %collective-permute-start.15 = (f32[512,128]{0,1:T(8,128)S(1)}, f32[512,128]{0,1:T(8,128)S(1)}, u32[]{:S(2)}, u32[]{:S(2)}) collective-permute-start(f32[512,128]{0,1:T(8,128)S(1)} %get-tuple-element.165), channel_id=1, source_target_pairs={{0,0},{4,8},{8,16},{12,24},{16,32},{20,40},{24,48},{28,56},{32,1},... | collective-permute-start | bytes 786440 | tf_op jit(solution)/shard_map/ppermute | solution.py:377
  159.7 15.0 %collective-permute-start.16 = (f32[512,128]{0,1:T(8,128)S(1)}, f32[512,128]{0,1:T(8,128)S(1)}, u32[]{:S(2)}, u32[]{:S(2)}) collective-permute-start(f32[512,128]{0,1:T(8,128)S(1)} %get-tuple-element.164), channel_id=1, source_target_pairs={{0,4},{4,12},{8,20},{12,28},{16,36},{20,44},{24,52},{28,60},{32,5}... | collective-permute-start | bytes 786440 | tf_op jit(solution)/shard_map/ppermute | solution.py:377
  175.7 49.7 %all-to-all-start.5 = ((f32[16,64,512]{2,1,0:T(8,128)}), f32[16,64,512]{2,1,0:T(8,128)}, u32[]{:S(2)}, u32[]{:S(2)}) async-start(f32[16,64,512]{2,1,0:T(8,128)} %place.1), calls=%async_computation.5 | async-start | bytes 4194304 | tf_op jit(solution)/shard_map/all_to_all | solution.py:254
  186.1 102.7 %all-gather.4.cloned.1.call-start = ((), (), s32[]{:S(2)}) async-start(), calls=%async_computation.6 | async-start | bytes 4456448 | tf_op jit(solution)/shard_map/all_gather | solution.py:397
  189.3 9.8 %collective-permute-start.18 = (bf16[4,32,1024]{2,1,0:T(8,128)(2,1)}, bf16[4,32,1024]{2,1,0:T(8,128)(2,1)S(1)}, u32[]{:S(2)}, u32[]{:S(2)}) collective-permute-start(bf16[4,32,1024]{2,1,0:T(8,128)(2,1)} %get-tuple-element.94.c0), channel_id=1, source_target_pairs={{0,2},{1,3},{2,0},{3,1},{4,6},{5,7},{6,4},{7,5},{8,10},{9,11},{10,... | collective-permute-start | bytes 786440 | tf_op jit(solution)/shard_map/ppermute | solution.py:270
  189.3 12.5 %collective-permute-start.17 = (bf16[4,32,1024]{2,1,0:T(8,128)(2,1)}, bf16[4,32,1024]{2,1,0:T(8,128)(2,1)S(1)}, u32[]{:S(2)}, u32[]{:S(2)}) collective-permute-start(bf16[4,32,1024]{2,1,0:T(8,128)(2,1)} %get-tuple-element.94.c0), channel_id=1, source_target_pairs={{0,1},{1,0},{2,3},{3,2},{4,5},{5,4},{6,7},{7,6},{8,9},{9,8},{10,11... | collective-permute-start | bytes 786440 | tf_op jit(solution)/shard_map/ppermute | solution.py:270
  199.1 2.7 collective-permute-start.19
  199.7 9.8 %collective-permute-start.20 = (bf16[4,32,1024]{2,1,0:T(8,128)(2,1)}, bf16[4,32,1024]{2,1,0:T(8,128)(2,1)S(1)}, u32[]{:S(2)}, u32[]{:S(2)}) collective-permute-start(bf16[4,32,1024]{2,1,0:T(8,128)(2,1)} %get-tuple-element.105.c0), channel_id=1, source_target_pairs={{0,2},{1,3},{2,0},{3,1},{4,6},{5,7},{6,4},{7,5},{8,10},{9,11},{10,... | collective-permute-start | bytes 786440 | tf_op jit(solution)/shard_map/ppermute | solution.py:270
  200.8 24.5 %collective-permute-start.25 = (bf16[4,32,1024]{2,1,0:T(8,128)(2,1)}, bf16[4,32,1024]{2,1,0:T(8,128)(2,1)S(1)}, u32[]{:S(2)}, u32[]{:S(2)}) collective-permute-start(bf16[4,32,1024]{2,1,0:T(8,128)(2,1)} %get-tuple-element.105.c0), channel_id=1, source_target_pairs={{0,1},{1,0},{2,3},{3,2},{4,5},{5,4},{6,7},{7,6},{8,9},{9,8},{10,11... | collective-permute-start | bytes 786440 | tf_op jit(solution)/shard_map/ppermute | solution.py:270
  209.5 23.7 %copy-start.9 = (bf16[4,32,1024]{2,1,0:T(8,128)(2,1)}, bf16[4,32,1024]{2,1,0:T(8,128)(2,1)S(1)}, u32[]{:S(2)}) copy-start(bf16[4,32,1024]{2,1,0:T(8,128)(2,1)S(1)} %collective-permute-done.20.c2) | copy-start | bytes 786436
  210.5 6.9 %collective-permute-start.21 = (f32[32,512]{1,0:T(8,128)S(1)}, f32[32,512]{1,0:T(8,128)S(1)}, u32[]{:S(2)}, u32[]{:S(2)}) collective-permute-start(f32[32,512]{1,0:T(8,128)S(1)} %get-tuple-element.182), channel_id=1, source_target_pairs={{0,1},{1,0},{2,3},{3,2},{4,5},{5,4},{6,7},{7,6},{8,9},{9,8},{10,11... | collective-permute-start | bytes 196616 | tf_op jit(solution)/shard_map/ppermute | solution.py:270
  211.2 6.6 %collective-permute-start.22 = (f32[32,512]{1,0:T(8,128)S(1)}, f32[32,512]{1,0:T(8,128)S(1)}, u32[]{:S(2)}, u32[]{:S(2)}) collective-permute-start(f32[32,512]{1,0:T(8,128)S(1)} %get-tuple-element.184), channel_id=1, source_target_pairs={{0,2},{1,3},{2,0},{3,1},{4,6},{5,7},{6,4},{7,5},{8,10},{9,11},{10,... | collective-permute-start | bytes 196616 | tf_op jit(solution)/shard_map/ppermute | solution.py:270
  211.3 6.7 %collective-permute-start.23 = (f32[32,512]{1,0:T(8,128)S(1)}, f32[32,512]{1,0:T(8,128)S(1)}, u32[]{:S(2)}, u32[]{:S(2)}) collective-permute-start(f32[32,512]{1,0:T(8,128)S(1)} %get-tuple-element.183), channel_id=1, source_target_pairs={{0,3},{1,2},{2,1},{3,0},{4,7},{5,6},{6,5},{7,4},{8,11},{9,10},{10,... | collective-permute-start | bytes 196616 | tf_op jit(solution)/shard_map/ppermute | solution.py:270
  215.5 9.8 %collective-permute-start.24 = (f32[128,512]{1,0:T(8,128)S(1)}, f32[128,512]{1,0:T(8,128)S(1)}, u32[]{:S(2)}, u32[]{:S(2)}) collective-permute-start(f32[128,512]{1,0:T(8,128)S(1)} %fusion.1), channel_id=1, source_target_pairs={{0,64},{64,0},{1,65},{65,1},{2,66},{66,2},{3,67},{67,3},{4,68},{68... | collective-permute-start | bytes 786440 | tf_op jit(solution)/shard_map/ppermute | solution.py:301
  217.4 8.0 %collective-permute-start.26 = (bf16[4,32,1024]{2,1,0:T(8,128)(2,1)S(1)}, bf16[4,32,1024]{2,1,0:T(8,128)(2,1)S(1)}, u32[]{:S(2)}, u32[]{:S(2)}) collective-permute-start(bf16[4,32,1024]{2,1,0:T(8,128)(2,1)S(1)} %collective-permute-done.20.c2), channel_id=1, source_target_pairs={{0,1},{1,0},{2,3},{3,2},{4,5},{5,4},{6,7},{7,6},{8,9},{9,8},{10,11... | collective-permute-start | bytes 786440 | tf_op jit(solution)/shard_map/ppermute | solution.py:270
  225.3 15.0 %copy-start.11 = (f32[128,512]{1,0:T(8,128)}, f32[128,512]{1,0:T(8,128)S(1)}, u32[]{:S(2)}) copy-start(f32[128,512]{1,0:T(8,128)S(1)} %add.166) | copy-start | bytes 786436
  225.4 11.2 %copy-start.10 = (bf16[4,32,1024]{2,1,0:T(8,128)(2,1)}, bf16[4,32,1024]{2,1,0:T(8,128)(2,1)S(1)}, u32[]{:S(2)}) copy-start(bf16[4,32,1024]{2,1,0:T(8,128)(2,1)S(1)} %collective-permute-done.25.c1) | copy-start | bytes 786436
  225.4 11.2 %copy-start.12 = (bf16[4,32,1024]{2,1,0:T(8,128)(2,1)}, bf16[4,32,1024]{2,1,0:T(8,128)(2,1)S(1)}, u32[]{:S(2)}) copy-start(bf16[4,32,1024]{2,1,0:T(8,128)(2,1)S(1)} %collective-permute-done.26.c3) | copy-start | bytes 786436
  225.4 7.0 %collective-permute-start.30 = (f32[128,512]{1,0:T(8,128)S(1)}, f32[128,512]{1,0:T(8,128)S(1)}, u32[]{:S(2)}, u32[]{:S(2)}) collective-permute-start(f32[128,512]{1,0:T(8,128)S(1)} %bitcast_add_fusion), channel_id=1, source_target_pairs={{0,64},{64,0},{1,65},{65,1},{2,66},{66,2},{3,67},{67,3},{4,68},{68... | collective-permute-start | bytes 786440 | tf_op jit(solution)/shard_map/ppermute | solution.py:301
  233.8 8.9 %collective-permute-start.28 = (f32[4,32,512]{2,1,0:T(8,128)S(1)}, f32[4,32,512]{2,1,0:T(8,128)S(1)}, u32[]{:S(2)}, u32[]{:S(2)}) collective-permute-start(f32[4,32,512]{2,1,0:T(8,128)S(1)} %bitcast.169), channel_id=1, source_target_pairs={{0,2},{1,3},{2,0},{3,1},{4,6},{5,7},{6,4},{7,5},{8,10},{9,11},{10,... | collective-permute-start | bytes 786440 | tf_op jit(solution)/shard_map/ppermute | solution.py:270
  240.2 9.5 %copy-start.25 = (f32[128,256]{1,0:T(8,128)S(1)}, f32[128,256]{1,0:T(8,128)}, u32[]{:S(2)}) copy-start(f32[128,256]{1,0:T(8,128)} %get-tuple-element.115) | copy-start | bytes 393220
  240.2 13.3 %copy-start.16 = (f32[64,512]{1,0:T(8,128)S(1)}, f32[64,512]{1,0:T(8,128)}, u32[]{:S(2)}) copy-start(f32[64,512]{1,0:T(8,128)} %get-tuple-element.90) | copy-start | bytes 393220
  240.2 9.5 %collective-permute-start.31 = (f32[128,256]{1,0:T(8,128)}, f32[128,256]{1,0:T(8,128)S(1)}, u32[]{:S(2)}, u32[]{:S(2)}) collective-permute-start(f32[128,256]{1,0:T(8,128)} %get-tuple-element.109), channel_id=1, source_target_pairs={{0,64},{64,0},{1,65},{65,1},{2,66},{66,2},{3,67},{67,3},{4,68},{68... | collective-permute-start | bytes 393224 | tf_op jit(solution)/shard_map/ppermute | solution.py:301
  240.3 9.5 %collective-permute-start.27 = (f32[4,32,512]{2,1,0:T(8,128)S(1)}, f32[4,32,512]{2,1,0:T(8,128)S(1)}, u32[]{:S(2)}, u32[]{:S(2)}) collective-permute-start(f32[4,32,512]{2,1,0:T(8,128)S(1)} %bitcast.170), channel_id=1, source_target_pairs={{0,1},{1,0},{2,3},{3,2},{4,5},{5,4},{6,7},{7,6},{8,9},{9,8},{10,11... | collective-permute-start | bytes 786440 | tf_op jit(solution)/shard_map/ppermute | solution.py:270
  242.8 7.1 %collective-permute-start.29 = (f32[4,32,512]{2,1,0:T(8,128)S(1)}, f32[4,32,512]{2,1,0:T(8,128)S(1)}, u32[]{:S(2)}, u32[]{:S(2)}) collective-permute-start(f32[4,32,512]{2,1,0:T(8,128)S(1)} %collective-permute-done.28.t2), channel_id=1, source_target_pairs={{0,1},{1,0},{2,3},{3,2},{4,5},{5,4},{6,7},{7,6},{8,9},{9,8},{10,11... | collective-permute-start | bytes 786440 | tf_op jit(solution)/shard_map/ppermute | solution.py:270
  249.8 26.7 %collective-permute-start.34 = (f32[4,32,256]{2,1,0:T(8,128)S(1)}, f32[4,32,256]{2,1,0:T(8,128)S(1)}, u32[]{:S(2)}, u32[]{:S(2)}) collective-permute-start(f32[4,32,256]{2,1,0:T(8,128)S(1)} %bitcast.165), channel_id=1, source_target_pairs={{0,2},{1,3},{2,0},{3,1},{4,6},{5,7},{6,4},{7,5},{8,10},{9,11},{10,... | collective-permute-start | bytes 393224 | tf_op jit(solution)/shard_map/ppermute | solution.py:270
  253.1 34.8 %collective-permute-start.38 = (f32[4,32,256]{2,1,0:T(8,128)S(1)}, f32[4,32,256]{2,1,0:T(8,128)S(1)}, u32[]{:S(2)}, u32[]{:S(2)}) collective-permute-start(f32[4,32,256]{2,1,0:T(8,128)S(1)} %bitcast.166), channel_id=1, source_target_pairs={{0,1},{1,0},{2,3},{3,2},{4,5},{5,4},{6,7},{7,6},{8,9},{9,8},{10,11... | collective-permute-start | bytes 393224 | tf_op jit(solution)/shard_map/ppermute | solution.py:270
  253.5 23.0 %collective-permute-start.32 = (f32[768,256]{1,0:T(8,128)}, f32[768,256]{1,0:T(8,128)S(1)}, u32[]{:S(2)}, u32[]{:S(2)}) collective-permute-start(f32[768,256]{1,0:T(8,128)} %get-tuple-element.116), channel_id=1, source_target_pairs={{0,64},{64,0},{1,65},{65,1},{2,66},{66,2},{3,67},{67,3},{4,68},{68... | collective-permute-start | bytes 2359304 | tf_op jit(solution)/shard_map/ppermute | solution.py:301
  253.6 23.0 %collective-permute-start.33 = (f32[2,32,512]{2,1,0:T(8,128)S(1)}, f32[2,32,512]{2,1,0:T(8,128)S(1)}, u32[]{:S(2)}, u32[]{:S(2)}) collective-permute-start(f32[2,32,512]{2,1,0:T(8,128)S(1)} %bitcast.175), channel_id=1, source_target_pairs={{0,2},{1,3},{2,0},{3,1},{4,6},{5,7},{6,4},{7,5},{8,10},{9,11},{10,... | collective-permute-start | bytes 393224 | tf_op jit(solution)/shard_map/ppermute | solution.py:270
  276.6 11.4 %collective-permute-start.39 = (f32[4,32,256]{2,1,0:T(8,128)S(1)}, f32[4,32,256]{2,1,0:T(8,128)S(1)}, u32[]{:S(2)}, u32[]{:S(2)}) collective-permute-start(f32[4,32,256]{2,1,0:T(8,128)S(1)} %collective-permute-done.34), channel_id=1, source_target_pairs={{0,1},{1,0},{2,3},{3,2},{4,5},{5,4},{6,7},{7,6},{8,9},{9,8},{10,11... | collective-permute-start | bytes 393224 | tf_op jit(solution)/shard_map/ppermute | solution.py:270
  284.1 16.2 %collective-permute-start.35 = (f32[16,32,256]{2,1,0:T(8,128)}, f32[16,32,256]{2,1,0:T(8,128)S(1)}, u32[]{:S(2)}, u32[]{:S(2)}) collective-permute-start(f32[16,32,256]{2,1,0:T(8,128)} %get-tuple-element.145), channel_id=1, source_target_pairs={{0,1},{1,0},{2,3},{3,2},{4,5},{5,4},{6,7},{7,6},{8,9},{9,8},{10,11... | collective-permute-start | bytes 1572872 | tf_op jit(solution)/shard_map/ppermute | solution.py:270
  284.7 15.6 %collective-permute-start.36 = (f32[16,32,256]{2,1,0:T(8,128)S(1)}, f32[16,32,256]{2,1,0:T(8,128)S(1)}, u32[]{:S(2)}, u32[]{:S(2)}) collective-permute-start(f32[16,32,256]{2,1,0:T(8,128)S(1)} %get-tuple-element.144), channel_id=1, source_target_pairs={{0,2},{1,3},{2,0},{3,1},{4,6},{5,7},{6,4},{7,5},{8,10},{9,11},{10,... | collective-permute-start | bytes 1572872 | tf_op jit(solution)/shard_map/ppermute | solution.py:270
  287.7 23.4 %collective-permute-start.37 = (f32[16,32,256]{2,1,0:T(8,128)S(1)}, f32[16,32,256]{2,1,0:T(8,128)S(1)}, u32[]{:S(2)}, u32[]{:S(2)}) collective-permute-start(f32[16,32,256]{2,1,0:T(8,128)S(1)} %get-tuple-element.143), channel_id=1, source_target_pairs={{0,3},{1,2},{2,1},{3,0},{4,7},{5,6},{6,5},{7,4},{8,11},{9,10},{10,... | collective-permute-start | bytes 1572872 | tf_op jit(solution)/shard_map/ppermute | solution.py:270
  288.8 22.3 %copy-start.20 = (f32[2,32,512]{2,1,0:T(8,128)S(1)}, f32[2,32,512]{2,1,0:T(8,128)}, u32[]{:S(2)}) copy-start(f32[2,32,512]{2,1,0:T(8,128)} %copy-done.19) | copy-start | bytes 393220
  288.8 22.5 %copy-start.17 = (f32[64,512]{1,0:T(8,128)S(1)}, f32[64,512]{1,0:T(8,128)}, u32[]{:S(2)}) copy-start(f32[64,512]{1,0:T(8,128)} %get-tuple-element.90) | copy-start | bytes 393220
  300.3 11.3 %copy-start.6 = (f32[16,32,256]{2,1,0:T(8,128)}, f32[16,32,256]{2,1,0:T(8,128)S(1)}, u32[]{:S(2)}) copy-start(f32[16,32,256]{2,1,0:T(8,128)S(1)} %collective-permute-done.35.g1) | copy-start | bytes 1572868
  300.3 11.3 %copy-start.7 = (f32[16,32,256]{2,1,0:T(8,128)}, f32[16,32,256]{2,1,0:T(8,128)S(1)}, u32[]{:S(2)}) copy-start(f32[16,32,256]{2,1,0:T(8,128)S(1)} %collective-permute-done.36.g2) | copy-start | bytes 1572868
  311.1 6.2 %collective-permute-start.41 = (f32[2,32,512]{2,1,0:T(8,128)S(1)}, f32[2,32,512]{2,1,0:T(8,128)S(1)}, u32[]{:S(2)}, u32[]{:S(2)}) collective-permute-start(f32[2,32,512]{2,1,0:T(8,128)S(1)} %copy-done.20), channel_id=1, source_target_pairs={{0,1},{1,0},{2,3},{3,2},{4,5},{5,4},{6,7},{7,6},{8,9},{9,8},{10,11... | collective-permute-start | bytes 393224 | tf_op jit(solution)/shard_map/ppermute | solution.py:270
  311.4 5.9 %collective-permute-start.40 = (f32[2,32,512]{2,1,0:T(8,128)S(1)}, f32[2,32,512]{2,1,0:T(8,128)S(1)}, u32[]{:S(2)}, u32[]{:S(2)}) collective-permute-start(f32[2,32,512]{2,1,0:T(8,128)S(1)} %bitcast.176), channel_id=1, source_target_pairs={{0,1},{1,0},{2,3},{3,2},{4,5},{5,4},{6,7},{7,6},{8,9},{9,8},{10,11... | collective-permute-start | bytes 393224 | tf_op jit(solution)/shard_map/ppermute | solution.py:270
  (17 other events, 54.8 us)
Sparse Core Ops, SparseCore 0:
  109.9 54.9 all-gather.5
  233.3 53.5 all-gather.3

commit v2 on v1

--- a/solution.py
+++ b/solution.py
@@ -94,7 +94,7 @@
     inverse_factor512(a, inv_ref, g)
     p = dot(c_ref[...], inv_ref[...], 1, 1)
     p_ref[...] = p
-    u_ref[...] = p.astype(BF16)
+    u_ref[...] = jnp.broadcast_to(p.astype(BF16)[None], u_ref.shape)
 
 
 def second_kernel(mask_ref, d_ref, inv0_ref, c_ref, u0_ref, p_ref, u_ref, d10, inv1, a, g):
@@ -103,11 +103,11 @@
         a[o:o + 4, :] = d_ref[s, i, :, 512:1024]
     u10 = dot(d10[...], inv0_ref[...], 1, 1).astype(BF16)
     a[...] = a[...] - dot16(u10, u10, 1, 1)
-    c1 = c_ref[...] - dot16(u0_ref[...], u10, 1, 1)
+    c1 = c_ref[...] - dot16(u0_ref[0], u10, 1, 1)
     inverse_factor512(a, inv1, g)
     p1 = dot(c1, inv1[...], 1, 1)
     p_ref[...] = jnp.where(mask_ref[0] > 0, p1, 0.0)
-    u_ref[...] = p1.astype(BF16)
+    u_ref[...] = jnp.broadcast_to(p1.astype(BF16)[None], u_ref.shape)
 
 
 def place(b, y_ref):
@@ -350,19 +350,18 @@
 
     d00, placed_panel = lax.optimization_barrier((d00, placed_panel))
     inv0, p0, u0 = call(
-        head_kernel, (sds((512, 512)), sds((64, 512)), sds((64, 512), BF16)), 0, 2, CHOL, 2 * 10**10, "head")(d00, left)
+        head_kernel, (sds((512, 512)), sds((64, 512)), sds((ROWS, 64, 512), BF16)), 0, 2, CHOL, 2 * 10**10, "head")(d00, left)
     f_panel = lax.all_gather(placed_panel, "row").reshape(32, 32, 512)
-    u0_all = jnp.broadcast_to(u0.reshape(1, 2, 32, 512), (ROWS, 2, 32, 512))
-    d1, u0_all = lax.optimization_barrier((d1, u0_all))
-    u0_all = exchange(u0_all, "row").reshape(32, 32, 512)
+    d1, u0 = lax.optimization_barrier((d1, u0))
+    u0_all = exchange(u0, "row").reshape(32, 32, 512)
 
     below = (r >= 2).astype(jnp.int32)[None]
     p1, u1 = call(
-        second_kernel, (sds((64, 512)), sds((64, 512), BF16)), 1, 4,
+        second_kernel, (sds((64, 512)), sds((ROWS, 64, 512), BF16)), 1, 4,
         [pltpu.VMEM((512, 512), F32)] * 2 + CHOL, 3 * 10**10, "second")(below, d1, inv0, pack[:, 512:1024], u0)
     factor0 = p0.reshape(2, 32, 512)
     u1, u0_all, far0 = lax.optimization_barrier((u1, u0_all, across(factor0, 2)))
-    u1_all = gather(u1.reshape(2, 32, 512), "row", ROWS).reshape(32, 32, 512)
+    u1_all = exchange(u1, "row").reshape(32, 32, 512)
     wide = after(jnp.concatenate([y[1], y[2], y[3]], axis=1), u1)
     placed = call(place_kernel, sds((16, 64, 512)), 1, 1, name="place")(bulk_idx, wide)
     factor0 = after(factor0, u1)
@@ -391,17 +390,18 @@
     t = t + swap_child(t)
     u_bulk = [u_bulk, across(u_bulk, 1), bulk_far, across(bulk_far, 1)]
     z = exchange_col(z.reshape(4, 32, 512), q).reshape(128, 512) + raw_rows
+    half, block = sds((768, 256)), sds((128, 256))
     z, t, u_bulk, f_bulk = lax.optimization_barrier((z, t, u_bulk, f_bulk))
+    first, sent = call(corner_kernel, (block, block), 2, 7, flops=10**9, name="corner")(
+        at, panel_idx, u0_all, u1_all, f_bulk, *u_bulk)
     z_swapped = swap_child(z)
+    own, other = call(bulk_kernel, (half, half), 1, 7, flops=4 * 10**9, name="bulk")(
+        at, u0_all, u1_all, after(f_bulk, sent), *u_bulk)
+    z_swapped, own, other = lax.optimization_barrier((z_swapped, own, other))
     z = z + z_swapped
     panel = lax.all_gather(z, "row", tiled=True)
+
     t_all = around(t.reshape(4, 32, 512))
-
-    half, block = sds((768, 256)), sds((128, 256))
-    first, sent = call(corner_kernel, (block, block), 2, 7, flops=10**9, name="corner")(
-        at, panel_idx, u0_all, u1_all, f_bulk, *u_bulk)
-    own, other = call(bulk_kernel, (half, half), 1, 7, flops=4 * 10**9, name="bulk")(
-        at, u0_all, u1_all, after(f_bulk, sent), *u_bulk)
     head_cols = (top + first + swap_child(sent)).reshape(4, 32, 256)
     t_all, z, other, head_cols = lax.optimization_barrier((t_all, z, other, head_cols))
     factor1 = p1.reshape(2, 32, 512)

time: 331 us -> 333 us (level)
  waiting for transfers between devices: 67.4 us -> 64 us
    ppermute x4, waiting for transfers between devices: 13.3 us -> 8.05 us  [swap_child(): return lax.ppermute(x, 'child', [(0, 1), (1, 0)])]
  transfers between devices with their start and end apart: 50 -> 50, of which waited for: 14 -> 16; matrix products, arithmetic and copies ran while one was open for 7% -> 7% of each run, Pallas kernels for 33% -> 32%
where the time goes in v2:
time: 333 us; the launch traced here: 327 us
  Pallas kernels  109 us (33%)
  starting transfers between devices  104 us (31%)
  waiting for transfers between devices  64 us (19%)
  local copies, waits for them, and re-layouts  21.6 us (6%)
  between operations  14.8 us (4%)
  other arithmetic  13.8 us (4%)
    ppermute x33, starting transfers between devices, across(): return lax.ppermute(x, 'col', [(i, i ^ k) for i in range(4)])  52.9 us
    all_to_all x6, starting transfers between devices, exchange(): return lax.all_to_all(x, axis, split_axis=0, concat_axis=0, tiled=True)  40.8 us
    ppermute x33, waiting for transfers between devices, across(): return lax.ppermute(x, 'col', [(i, i ^ k) for i in range(4)])  31.7 us
    pallas_call x1, Pallas kernels, local(): call(second_kernel, (sds((64, 512)), sds((ROWS, 64, 512), BF16)), 1, 4, [...  25.5 us
    pallas_call x1, Pallas kernels, local(): call(head_kernel, (sds((512, 512)), sds((64, 512)), sds((ROWS, 64, 512),...  22.2 us
    pallas_call x1, Pallas kernels, local(): call(root_kernel, sds((512, 512)), 1, 4, CHOL, 2 * 10 ** 10, 'root')  20.9 us
    all_to_all x6, waiting for transfers between devices, exchange(): return lax.all_to_all(x, axis, split_axis=0, concat_axis=0, tiled=True)  12.6 us
    pallas_call x1, Pallas kernels, local(): pl.pallas_call(factor_kernel, out_shape=(sds((2048, 512)), sds((2048, 512...  11.4 us
  transfers between devices with their start and end apart: 50, of which 16 were waited for; matrix products, arithmetic and copies ran while one was open for 7% of the time, Pallas kernels for 32%

profile of v2, /device:TPU:1, one launch (start us, length us, event | category | flops | bytes accessed | tf_op | source)
XLA Modules:
  0.0 327.3 jit_solution(11956157859251920494)
XLA Ops:
  7.2 1.2 slice.81
  8.8 1.0 slice_bitcast_fusion.1
  9.8 1.4 collective-permute-start
  11.2 1.4 collective-permute-start.1
  12.6 1.4 collective-permute-start.2
  14.1 1.3 fusion
  16.3 7.4 %all-to-all-start = ((f32[16,4,1536]{2,1,0:T(4,128)}), f32[16,4,1536]{2,1,0:T(4,128)S(1)}, u32[]{:S(2)}, u32[]{:S(2)}) async-start(f32[16,4,1536]{2,1,0:T(4,128)} %reshape.141), calls=%async_computation | async-start | bytes 786432 | tf_op jit(solution)/shard_map/all_to_all | solution.py:254
  23.8 8.0 %all-to-all-done = f32[16,4,1536]{2,1,0:T(4,128)S(1)} async-done(((f32[16,4,1536]{2,1,0:T(4,128)}), f32[16,4,1536]{2,1,0:T(4,128)S(1)}, u32[]{:S(2)}, u32[]{:S(2)}) %all-to-all-start) | async-done | bytes 393248 | tf_op jit(solution)/shard_map/all_to_all | solution.py:254
  31.8 16.6 %collective-permute-start.4 = (f32[2,4,512]{2,1,0:T(4,128)S(1)}, f32[2,4,512]{2,1,0:T(4,128)S(1)}, u32[]{:S(2)}, u32[]{:S(2)}) collective-permute-start(f32[2,4,512]{2,1,0:T(4,128)S(1)} %slice.113), channel_id=1, source_target_pairs={{0,2},{1,3},{2,0},{3,1},{4,6},{5,7},{6,4},{7,5},{8,10},{9,11},{10,... | collective-permute-start | bytes 49160 | tf_op jit(solution)/shard_map/ppermute | solution.py:270
  48.6 0.9 collective-permute-done.4
  49.5 2.4 collective-permute-start.5
  52.8 1.2 broadcast_in_dim.98
  54.0 3.7 %all-to-all-start.1 = ((f32[16,8,4,512]{3,2,1,0:T(4,128)}), f32[16,8,4,512]{3,2,1,0:T(4,128)S(1)}, u32[]{:S(2)}, u32[]{:S(2)}) async-start(f32[16,8,4,512]{3,2,1,0:T(4,128)} %broadcast_in_dim.98), calls=%async_computation.1 | async-start | bytes 2097152 | tf_op jit(solution)/shard_map/all_to_all | solution.py:254
  58.7 0.9 collective-permute-start.7
  60.1 3.2 collective-permute-done.7
  63.3 1.3 collective-permute-start.8
  66.0 2.3 collective-permute-start.11
  69.2 4.6 %all-to-all-done.1.d_ref = f32[16,8,4,512]{3,2,1,0:T(4,128)S(1)} async-done(((f32[16,8,4,512]{3,2,1,0:T(4,128)}), f32[16,8,4,512]{3,2,1,0:T(4,128)S(1)}, u32[]{:S(2)}, u32[]{:S(2)}) %all-to-all-start.1) | async-done | bytes 1048608 | tf_op jit(solution)/shard_map/all_to_all | solution.py:254
  73.8 2.0 broadcast_in_dim.99
  75.8 4.4 %all-to-all-start.2 = ((f32[16,9,4,1024]{3,2,1,0:T(4,128)}), f32[16,9,4,1024]{3,2,1,0:T(4,128)}, u32[]{:S(2)}, u32[]{:S(2)}) async-start(f32[16,9,4,1024]{3,2,1,0:T(4,128)} %broadcast_in_dim.99), calls=%async_computation.2 | async-start | bytes 4718592 | tf_op jit(solution)/shard_map/all_to_all | solution.py:254
  81.2 2.0 fusion.2
  84.6 1.6 place_panel.1
  86.1 22.2 %head.1 = (f32[512,512]{1,0:T(8,128)}, f32[64,512]{1,0:T(8,128)}, bf16[16,64,512]{2,1,0:T(8,128)(2,1)}) custom-call(f32[16,8,4,512]{3,2,1,0:T(4,128)} %copy-done.7, f32[64,512]{1,0:T(8,128)} %get-tuple-element.185.c_ref), custom_call_target="tpu_custom_call" | custom-call | flops 20000000000 | bytes 1048576 | tf_op jit(solution)/shard_map/head/pallas_call | solution.py:352
  108.3 1.8 collective-permute-start.12
  110.2 6.8 %all-to-all-start.3 = ((bf16[16,64,512]{2,1,0:T(8,128)(2,1)}), bf16[16,64,512]{2,1,0:T(8,128)(2,1)S(1)}, u32[]{:S(2)}, u32[]{:S(2)}) async-start(bf16[16,64,512]{2,1,0:T(8,128)(2,1)} %get-tuple-element.84.u0_ref), calls=%async_computation.3 | async-start | bytes 2097152 | tf_op jit(solution)/shard_map/all_to_all | solution.py:254
  116.9 25.5 %second.1 = (f32[64,512]{1,0:T(8,128)}, bf16[16,64,512]{2,1,0:T(8,128)(2,1)}) custom-call(s32[1]{0:T(128)} %bitcast.mask_ref, f32[16,9,4,1024]{3,2,1,0:T(4,128)} %all-to-all-done.2.d_ref, f32[512,512]{1,0:T(8,128)} %get-tuple-element.83.inv0_ref, f32[64,512]{1,0:T(8,128)} %get-tuple-element.184.c_ref, bf16[16,64,512]{2,1,0:T(8,128)(2,1)} %get-tuple-element.84.u0_ref), custom_call_target="tpu_custom_call" | custom-call | flops 30000001024 | bytes 1048576 | tf_op jit(solution)/shard_map/second/pallas_call | solution.py:359
  142.5 6.8 %all-to-all-start.4 = ((bf16[16,64,512]{2,1,0:T(8,128)(2,1)}), bf16[16,64,512]{2,1,0:T(8,128)(2,1)S(1)}, u32[]{:S(2)}, u32[]{:S(2)}) async-start(bf16[16,64,512]{2,1,0:T(8,128)(2,1)} %get-tuple-element.87), calls=%async_computation.4 | async-start | bytes 2097152 | tf_op jit(solution)/shard_map/all_to_all | solution.py:254
  150.1 2.1 pad_maximum_fusion.1.y_ref
  152.2 3.2 collective-permute-start.13
  155.5 1.3 collective-permute-start.15
  157.5 3.4 %place.1 = f32[16,64,512]{2,1,0:T(8,128)} custom-call(s32[64]{0:T(128)} %select_reduce_fusion.bulk_ref, f32[64,3072]{1,0:T(8,128)} %pad_maximum_fusion.1.y_ref), custom_call_target="tpu_custom_call" | custom-call | bytes 1048576 | tf_op jit(solution)/shard_map/place/pallas_call | solution.py:366
  160.9 0.9 pad_maximum_fusion.2
  161.8 10.8 %collective-permute-done.15 = f32[512,128]{0,1:T(8,128)S(1)} collective-permute-done((f32[512,128]{0,1:T(8,128)S(1)}, f32[512,128]{0,1:T(8,128)S(1)}, u32[]{:S(2)}, u32[]{:S(2)}) %collective-permute-start.15) | collective-permute-done | bytes 262176 | tf_op jit(solution)/shard_map/ppermute | solution.py:376
  173.3 1.0 copy-done.1
  174.3 11.7 %all-to-all-start.5 = ((f32[16,64,512]{2,1,0:T(8,128)}), f32[16,64,512]{2,1,0:T(8,128)S(1)}, u32[]{:S(2)}, u32[]{:S(2)}) async-start(f32[16,64,512]{2,1,0:T(8,128)} %place.1), calls=%async_computation.5 | async-start | bytes 4194304 | tf_op jit(solution)/shard_map/all_to_all | solution.py:254
  186.9 2.4 select.17
  189.3 9.9 %collective-permute-done.18.c2 = bf16[4,32,1024]{2,1,0:T(8,128)(2,1)S(1)} collective-permute-done((bf16[4,32,1024]{2,1,0:T(8,128)(2,1)}, bf16[4,32,1024]{2,1,0:T(8,128)(2,1)S(1)}, u32[]{:S(2)}, u32[]{:S(2)}) %collective-permute-start.18) | collective-permute-done | bytes 262176 | tf_op jit(solution)/shard_map/ppermute | solution.py:270
  199.7 1.0 fusion.12
  204.5 4.0 %panel.1 = (f32[128,512]{1,0:T(8,128)}, f32[128,512]{1,0:T(8,128)}) custom-call(s32[1]{0:T(128)} %bitcast.39.q_ref, s32[4]{0:T(128)} %get-tuple-element.144.rows_ref, s32[4]{0:T(128)} %slice_bitcast_fusion.6.panel_ref, bf16[32,32,512]{2,1,0:T(8,128)(2,1)} %bitcast.145, bf16[32,32,512]{2,1,0:T(8,128)(2,1)} %bitcast.149, f32[32,32,512]{2,1,0:T(8,128)} %bitcast.159, ...), custom_call_target="tpu_custom_call" | custom-call | flops 1000000000 | bytes 1048576 | tf_op jit(solution)/shard_map/panel/pallas_call | solution.py:386
  209.3 1.0 dynamic-slice_bitcast_fusion.9
  211.2 1.7 collective-permute-start.22
  213.0 1.5 collective-permute-start.23
  214.5 1.0 fusion.1
  215.4 3.3 %collective-permute-start.24 = (f32[128,512]{1,0:T(8,128)S(1)}, f32[128,512]{1,0:T(8,128)S(1)}, u32[]{:S(2)}, u32[]{:S(2)}) collective-permute-start(f32[128,512]{1,0:T(8,128)S(1)} %fusion.1), channel_id=1, source_target_pairs={{0,64},{64,0},{1,65},{65,1},{2,66},{66,2},{3,67},{67,3},{4,68},{68... | collective-permute-start | bytes 786440 | tf_op jit(solution)/shard_map/ppermute | solution.py:301
  219.8 6.1 %collective-permute-done.24 = f32[128,512]{1,0:T(8,128)S(1)} collective-permute-done((f32[128,512]{1,0:T(8,128)S(1)}, f32[128,512]{1,0:T(8,128)S(1)}, u32[]{:S(2)}, u32[]{:S(2)}) %collective-permute-start.24) | collective-permute-done | bytes 262176 | tf_op jit(solution)/shard_map/ppermute | solution.py:301
  227.4 3.7 %corner.1 = (f32[128,256]{1,0:T(8,128)}, f32[128,256]{1,0:T(8,128)}) custom-call(s32[1]{0:T(128)} %bitcast.39.q_ref, s32[4]{0:T(128)} %slice_bitcast_fusion.6.panel_ref, bf16[32,32,512]{2,1,0:T(8,128)(2,1)} %bitcast.146, bf16[32,32,512]{2,1,0:T(8,128)(2,1)} %bitcast.150, f32[32,32,512]{2,1,0:T(8,128)} %bitcast.155, ...), custom_call_target="tpu_custom_call" | custom-call | flops 1000000000 | bytes 1048576 | tf_op jit(solution)/shard_map/corner/pallas_call | solution.py:395
  231.1 1.0 collective-permute-start.27
  232.1 4.6 %bulk.1 = (f32[768,256]{1,0:T(8,128)}, f32[768,256]{1,0:T(8,128)}) custom-call(s32[1]{0:T(128)} %bitcast.39.q_ref, bf16[32,32,512]{2,1,0:T(8,128)(2,1)} %bitcast.147, bf16[32,32,512]{2,1,0:T(8,128)(2,1)} %bitcast.151, f32[32,32,512]{2,1,0:T(8,128)} %bitcast.156, bf16[4,32,1024]{2,1,0:T(8,128)(2,1)} %get-tuple-element.109.c0, ...), custom_call_target="tpu_custom_call" | custom-call | flops 4000000000 | bytes 1048576 | tf_op jit(solution)/shard_map/bulk/pallas_call | solution.py:398
  236.7 2.0 collective-permute-done.27
  240.8 2.3 collective-permute-start.28
  243.1 4.5 %collective-permute-done.29.t2 = f32[4,32,512]{2,1,0:T(8,128)S(1)} collective-permute-done((f32[4,32,512]{2,1,0:T(8,128)S(1)}, f32[4,32,512]{2,1,0:T(8,128)S(1)}, u32[]{:S(2)}, u32[]{:S(2)}) %collective-permute-start.29) | collective-permute-done | bytes 262176 | tf_op jit(solution)/shard_map/ppermute | solution.py:270
  247.6 3.6 %collective-permute-start.30 = (f32[4,32,512]{2,1,0:T(8,128)S(1)}, f32[4,32,512]{2,1,0:T(8,128)S(1)}, u32[]{:S(2)}, u32[]{:S(2)}) collective-permute-start(f32[4,32,512]{2,1,0:T(8,128)S(1)} %collective-permute-done.29.t2), channel_id=1, source_target_pairs={{0,1},{1,0},{2,3},{3,2},{4,5},{5,4},{6,7},{7,6},{8,9},{9,8},{10,11... | collective-permute-start | bytes 786440 | tf_op jit(solution)/shard_map/ppermute | solution.py:270
  251.2 1.1 collective-permute-done.30.t3
  252.9 1.2 collective-permute-start.38
  254.1 2.9 collective-permute-start.33
  257.1 20.9 %root.1.inv_ref = f32[512,512]{1,0:T(8,128)} custom-call(s32[1]{0:T(128)} %bitcast.39.q_ref, f32[4,32,512]{2,1,0:T(8,128)} %bitcast.171, f32[4,32,512]{2,1,0:T(8,128)} %copy-done.29, f32[4,32,512]{2,1,0:T(8,128)} %copy-done.28, f32[4,32,512]{2,1,0:T(8,128)} %copy-done.30), custom_call_target="tpu_custom_call" | custom-call | flops 20000000000 | bytes 1048576 | tf_op jit(solution)/shard_map/root/pallas_call | solution.py:410
  278.2 1.4 collective-permute-start.39
  279.6 3.7 %spread.1 = f32[64,32,256]{2,1,0:T(8,128)} custom-call(s32[64]{0:T(128)} %bitcast.183, s32[64]{0:T(128)} %get-tuple-element.199.theirs_ref, f32[24,32,256]{2,1,0:T(8,128)} %bitcast.163, f32[24,32,256]{2,1,0:T(8,128)} %bitcast.164), custom_call_target="tpu_custom_call" | custom-call | bytes 1048576 | tf_op jit(solution)/shard_map/spread/pallas_call | solution.py:412
  283.3 2.5 dynamic-slice_bitcast_fusion
  287.1 2.5 collective-permute-start.37
  291.2 11.4 %factor.1 = (f32[2048,512]{1,0:T(8,128)}, bf16[2048,512]{1,0:T(8,128)(2,1)}, bf16[512,256]{1,0:T(8,128)(2,1)}) custom-call(s32[2]{0:T(128)} %add_convert_fusion.flag_ref, f32[2048,512]{1,0:T(8,128)} %all-gather.4.cloned.1.call-done.panel_ref, f32[512,512]{1,0:T(8,128)} %root.1.inv_ref, f32[4,4,32,256]{3,2,1,0:T(8,128)} %pad_maximum_fusion.3.cp_ref), custom_call_target="tpu_custom_call" | custom-call | flops 10000000000 | bytes 1048576 | tf_op jit(solution)/shard_map/factor/pallas_call | solution.py:422
  302.6 10.3 %collective-permute-done.37.g3 = f32[16,32,256]{2,1,0:T(8,128)S(1)} collective-permute-done((f32[16,32,256]{2,1,0:T(8,128)S(1)}, f32[16,32,256]{2,1,0:T(8,128)S(1)}, u32[]{:S(2)}, u32[]{:S(2)}) %collective-permute-start.37) | collective-permute-done | bytes 524320 | tf_op jit(solution)/shard_map/ppermute | solution.py:270
  313.7 5.4 %last.1 = f32[2048,256]{1,0:T(8,128)} custom-call(s32[1]{0:T(128)} %bitcast.39.q_ref, bf16[2048,512]{1,0:T(8,128)(2,1)} %get-tuple-element.133.u_ref, bf16[512,256]{1,0:T(8,128)(2,1)} %get-tuple-element.138.ug_ref, f32[2048,256]{1,0:T(8,128)} %root_ref.1, f32[16,32,256]{2,1,0:T(8,128)} %get-tuple-element.139.g0, f32[16,32,256]{2,1,0:T(8,128)} %copy-done.9, ...), custom_call_target="tpu_custom_call" | custom-call | tf_op jit(solution)/shard_map/last/pallas_call | solution.py:437
  319.3 1.0 copy.22
  (172 shorter events, 27.3 us)
Async XLA Ops:
  9.8 38.6 %copy-start.27 = (s32[2,24]{1,0:T(2,128)S(1)}, s32[2,24]{1,0:T(2,128)}, u32[]{:S(2)}) copy-start(s32[2,24]{1,0:T(2,128)} %param.5) | copy-start | bytes 580
  9.8 4.4 %collective-permute-start = (f32[64,1536]{1,0:T(8,128)}, f32[64,1536]{1,0:T(8,128)}, u32[]{:S(2)}, u32[]{:S(2)}) collective-permute-start(f32[64,1536]{1,0:T(8,128)} %get-tuple-element.158), channel_id=1, source_target_pairs={{0,1},{4,5},{8,9},{12,13},{16,17},{20,21},{24,25},{28,29},{32,33},... | collective-permute-start | bytes 1179656 | tf_op jit(solution)/shard_map/ppermute | solution.py:283
  11.2 3.0 collective-permute-start.1
  12.6 1.6 collective-permute-start.2
  16.3 15.4 %all-to-all-start = ((f32[16,4,1536]{2,1,0:T(4,128)}), f32[16,4,1536]{2,1,0:T(4,128)S(1)}, u32[]{:S(2)}, u32[]{:S(2)}) async-start(f32[16,4,1536]{2,1,0:T(4,128)} %reshape.141), calls=%async_computation | async-start | bytes 786432 | tf_op jit(solution)/shard_map/all_to_all | solution.py:254
  31.8 17.8 %collective-permute-start.4 = (f32[2,4,512]{2,1,0:T(4,128)S(1)}, f32[2,4,512]{2,1,0:T(4,128)S(1)}, u32[]{:S(2)}, u32[]{:S(2)}) collective-permute-start(f32[2,4,512]{2,1,0:T(4,128)S(1)} %slice.113), channel_id=1, source_target_pairs={{0,2},{1,3},{2,0},{3,1},{4,6},{5,7},{6,4},{7,5},{8,10},{9,11},{10,... | collective-permute-start | bytes 49160 | tf_op jit(solution)/shard_map/ppermute | solution.py:270
  48.5 3.5 %collective-permute-start.3 = (f32[2,4,512]{2,1,0:T(4,128)S(1)}, f32[2,4,512]{2,1,0:T(4,128)S(1)}, u32[]{:S(2)}, u32[]{:S(2)}) collective-permute-start(f32[2,4,512]{2,1,0:T(4,128)S(1)} %slice.113), channel_id=1, source_target_pairs={{0,1},{1,0},{2,3},{3,2},{4,5},{5,4},{6,7},{7,6},{8,9},{9,8},{10,11... | collective-permute-start | bytes 49160 | tf_op jit(solution)/shard_map/ppermute | solution.py:270
  49.5 3.3 collective-permute-start.5
  54.0 19.7 %all-to-all-start.1 = ((f32[16,8,4,512]{3,2,1,0:T(4,128)}), f32[16,8,4,512]{3,2,1,0:T(4,128)S(1)}, u32[]{:S(2)}, u32[]{:S(2)}) async-start(f32[16,8,4,512]{3,2,1,0:T(4,128)} %broadcast_in_dim.98), calls=%async_computation.1 | async-start | bytes 2097152 | tf_op jit(solution)/shard_map/all_to_all | solution.py:254
  58.2 127.9 %copy-start.26 = (s32[1,64]{1,0:T(1,128)}, s32[1,64]{1,0:T(1,128)S(1)}, u32[]{:S(2)}) copy-start(s32[1,64]{1,0:T(1,128)S(1)} %get-tuple-element.200) | copy-start | bytes 772
  58.7 4.6 %collective-permute-start.7 = (f32[2,4,1024]{2,1,0:T(4,128)S(1)}, f32[2,4,1024]{2,1,0:T(4,128)S(1)}, u32[]{:S(2)}, u32[]{:S(2)}) collective-permute-start(f32[2,4,1024]{2,1,0:T(4,128)S(1)} %slice.114), channel_id=1, source_target_pairs={{0,2},{1,3},{2,0},{3,1},{4,6},{5,7},{6,4},{7,5},{8,10},{9,11},{10,... | collective-permute-start | bytes 98312 | tf_op jit(solution)/shard_map/ppermute | solution.py:270
  59.6 9.4 %collective-permute-start.6 = (f32[2,4,1024]{2,1,0:T(4,128)S(1)}, f32[2,4,1024]{2,1,0:T(4,128)S(1)}, u32[]{:S(2)}, u32[]{:S(2)}) collective-permute-start(f32[2,4,1024]{2,1,0:T(4,128)S(1)} %slice.114), channel_id=1, source_target_pairs={{0,1},{1,0},{2,3},{3,2},{4,5},{5,4},{6,7},{7,6},{8,9},{9,8},{10,11... | collective-permute-start | bytes 98312 | tf_op jit(solution)/shard_map/ppermute | solution.py:270
  63.3 5.8 %collective-permute-start.8 = (f32[2,4,1024]{2,1,0:T(4,128)S(1)}, f32[2,4,1024]{2,1,0:T(4,128)S(1)}, u32[]{:S(2)}, u32[]{:S(2)}) collective-permute-start(f32[2,4,1024]{2,1,0:T(4,128)S(1)} %collective-permute-done.7), channel_id=1, source_target_pairs={{0,1},{1,0},{2,3},{3,2},{4,5},{5,4},{6,7},{7,6},{8,9},{9,8},{10,11... | collective-permute-start | bytes 98312 | tf_op jit(solution)/shard_map/ppermute | solution.py:270
  65.4 15.8 %collective-permute-start.10 = (f32[64,1024]{1,0:T(8,128)}, f32[64,1024]{1,0:T(8,128)}, u32[]{:S(2)}, u32[]{:S(2)}) collective-permute-start(f32[64,1024]{1,0:T(8,128)} %get-tuple-element.161), channel_id=1, source_target_pairs={{0,3},{1,2},{2,1},{3,0},{4,7},{5,6},{6,5},{7,4},{8,11},{9,10},{10,... | collective-permute-start | bytes 786440 | tf_op jit(solution)/shard_map/ppermute | solution.py:270
  66.0 15.2 %collective-permute-start.11 = (f32[64,1024]{1,0:T(8,128)}, f32[64,1024]{1,0:T(8,128)}, u32[]{:S(2)}, u32[]{:S(2)}) collective-permute-start(f32[64,1024]{1,0:T(8,128)} %get-tuple-element.160), channel_id=1, source_target_pairs={{0,2},{1,3},{2,0},{3,1},{4,6},{5,7},{6,4},{7,5},{8,10},{9,11},{10,... | collective-permute-start | bytes 786440 | tf_op jit(solution)/shard_map/ppermute | solution.py:270
  68.2 12.9 %collective-permute-start.9 = (f32[64,1024]{1,0:T(8,128)S(1)}, f32[64,1024]{1,0:T(8,128)}, u32[]{:S(2)}, u32[]{:S(2)}) collective-permute-start(f32[64,1024]{1,0:T(8,128)S(1)} %get-tuple-element.159), channel_id=1, source_target_pairs={{0,1},{1,0},{2,3},{3,2},{4,5},{5,4},{6,7},{7,6},{8,9},{9,8},{10,11... | collective-permute-start | bytes 786440 | tf_op jit(solution)/shard_map/ppermute | solution.py:270
  75.8 34.4 %all-to-all-start.2 = ((f32[16,9,4,1024]{3,2,1,0:T(4,128)}), f32[16,9,4,1024]{3,2,1,0:T(4,128)}, u32[]{:S(2)}, u32[]{:S(2)}) async-start(f32[16,9,4,1024]{3,2,1,0:T(4,128)} %broadcast_in_dim.99), calls=%async_computation.2 | async-start | bytes 4718592 | tf_op jit(solution)/shard_map/all_to_all | solution.py:254
  80.2 123.6 %all-gather.6.cloned.1.call-start = ((), (), s32[]{:S(2)}) async-start(), calls=%async_computation.7 | async-start | bytes 2228224 | tf_op jit(solution)/shard_map/all_gather | solution.py:354
  108.3 34.2 %collective-permute-start.12 = (f32[2,32,512]{2,1,0:T(8,128)}, f32[2,32,512]{2,1,0:T(8,128)S(1)}, u32[]{:S(2)}, u32[]{:S(2)}) collective-permute-start(f32[2,32,512]{2,1,0:T(8,128)} %bitcast.178), channel_id=1, source_target_pairs={{0,2},{1,3},{2,0},{3,1},{4,6},{5,7},{6,4},{7,5},{8,10},{9,11},{10,... | collective-permute-start | bytes 393224 | tf_op jit(solution)/shard_map/ppermute | solution.py:270
  110.2 32.3 %all-to-all-start.3 = ((bf16[16,64,512]{2,1,0:T(8,128)(2,1)}), bf16[16,64,512]{2,1,0:T(8,128)(2,1)S(1)}, u32[]{:S(2)}, u32[]{:S(2)}) async-start(bf16[16,64,512]{2,1,0:T(8,128)(2,1)} %get-tuple-element.84.u0_ref), calls=%async_computation.3 | async-start | bytes 2097152 | tf_op jit(solution)/shard_map/all_to_all | solution.py:254
  142.5 9.7 %copy-start = (bf16[16,64,512]{2,1,0:T(8,128)(2,1)}, bf16[16,64,512]{2,1,0:T(8,128)(2,1)S(1)}, u32[]{:S(2)}) copy-start(bf16[16,64,512]{2,1,0:T(8,128)(2,1)S(1)} %all-to-all-done.3) | copy-start | bytes 3145732
  142.5 30.9 %all-to-all-start.4 = ((bf16[16,64,512]{2,1,0:T(8,128)(2,1)}), bf16[16,64,512]{2,1,0:T(8,128)(2,1)S(1)}, u32[]{:S(2)}, u32[]{:S(2)}) async-start(bf16[16,64,512]{2,1,0:T(8,128)(2,1)} %get-tuple-element.87), calls=%async_computation.4 | async-start | bytes 2097152 | tf_op jit(solution)/shard_map/all_to_all | solution.py:254
  152.2 8.6 %collective-permute-start.13 = (f32[2,32,512]{2,1,0:T(8,128)}, f32[2,32,512]{2,1,0:T(8,128)S(1)}, u32[]{:S(2)}, u32[]{:S(2)}) collective-permute-start(f32[2,32,512]{2,1,0:T(8,128)} %bitcast.179), channel_id=1, source_target_pairs={{0,1},{1,0},{2,3},{3,2},{4,5},{5,4},{6,7},{7,6},{8,9},{9,8},{10,11... | collective-permute-start | bytes 393224 | tf_op jit(solution)/shard_map/ppermute | solution.py:270
  155.3 5.5 %collective-permute-start.14 = (f32[2,32,512]{2,1,0:T(8,128)}, f32[2,32,512]{2,1,0:T(8,128)S(1)}, u32[]{:S(2)}, u32[]{:S(2)}) collective-permute-start(f32[2,32,512]{2,1,0:T(8,128)} %copy-done.23), channel_id=1, source_target_pairs={{0,1},{1,0},{2,3},{3,2},{4,5},{5,4},{6,7},{7,6},{8,9},{9,8},{10,11... | collective-permute-start | bytes 393224 | tf_op jit(solution)/shard_map/ppermute | solution.py:270
  155.5 17.1 %collective-permute-start.15 = (f32[512,128]{0,1:T(8,128)S(1)}, f32[512,128]{0,1:T(8,128)S(1)}, u32[]{:S(2)}, u32[]{:S(2)}) collective-permute-start(f32[512,128]{0,1:T(8,128)S(1)} %get-tuple-element.171), channel_id=1, source_target_pairs={{0,0},{4,8},{8,16},{12,24},{16,32},{20,40},{24,48},{28,56},{32,1},... | collective-permute-start | bytes 786440 | tf_op jit(solution)/shard_map/ppermute | solution.py:376
  156.8 15.8 %collective-permute-start.16 = (f32[512,128]{0,1:T(8,128)S(1)}, f32[512,128]{0,1:T(8,128)S(1)}, u32[]{:S(2)}, u32[]{:S(2)}) collective-permute-start(f32[512,128]{0,1:T(8,128)S(1)} %get-tuple-element.170), channel_id=1, source_target_pairs={{0,4},{4,12},{8,20},{12,28},{16,36},{20,44},{24,52},{28,60},{32,5}... | collective-permute-start | bytes 786440 | tf_op jit(solution)/shard_map/ppermute | solution.py:376
  174.3 51.7 %all-to-all-start.5 = ((f32[16,64,512]{2,1,0:T(8,128)}), f32[16,64,512]{2,1,0:T(8,128)S(1)}, u32[]{:S(2)}, u32[]{:S(2)}) async-start(f32[16,64,512]{2,1,0:T(8,128)} %place.1), calls=%async_computation.5 | async-start | bytes 4194304 | tf_op jit(solution)/shard_map/all_to_all | solution.py:254
  186.0 105.1 %all-gather.4.cloned.1.call-start = ((), (), s32[]{:S(2)}) async-start(), calls=%async_computation.6 | async-start | bytes 4456448 | tf_op jit(solution)/shard_map/all_gather | solution.py:402
  189.2 9.9 %collective-permute-start.18 = (bf16[4,32,1024]{2,1,0:T(8,128)(2,1)}, bf16[4,32,1024]{2,1,0:T(8,128)(2,1)S(1)}, u32[]{:S(2)}, u32[]{:S(2)}) collective-permute-start(bf16[4,32,1024]{2,1,0:T(8,128)(2,1)} %get-tuple-element.97.c0), channel_id=1, source_target_pairs={{0,2},{1,3},{2,0},{3,1},{4,6},{5,7},{6,4},{7,5},{8,10},{9,11},{10,... | collective-permute-start | bytes 786440 | tf_op jit(solution)/shard_map/ppermute | solution.py:270
  189.2 14.6 %collective-permute-start.17 = (bf16[4,32,1024]{2,1,0:T(8,128)(2,1)}, bf16[4,32,1024]{2,1,0:T(8,128)(2,1)S(1)}, u32[]{:S(2)}, u32[]{:S(2)}) collective-permute-start(bf16[4,32,1024]{2,1,0:T(8,128)(2,1)} %get-tuple-element.97.c0), channel_id=1, source_target_pairs={{0,1},{1,0},{2,3},{3,2},{4,5},{5,4},{6,7},{7,6},{8,9},{9,8},{10,11... | collective-permute-start | bytes 786440 | tf_op jit(solution)/shard_map/ppermute | solution.py:270
  199.1 4.7 %collective-permute-start.19 = (bf16[4,32,1024]{2,1,0:T(8,128)(2,1)S(1)}, bf16[4,32,1024]{2,1,0:T(8,128)(2,1)}, u32[]{:S(2)}, u32[]{:S(2)}) collective-permute-start(bf16[4,32,1024]{2,1,0:T(8,128)(2,1)S(1)} %collective-permute-done.18.c2), channel_id=1, source_target_pairs={{0,1},{1,0},{2,3},{3,2},{4,5},{5,4},{6,7},{7,6},{8,9},{9,8},{10,11... | collective-permute-start | bytes 786440 | tf_op jit(solution)/shard_map/ppermute | solution.py:270
  199.7 9.7 %collective-permute-start.20 = (bf16[4,32,1024]{2,1,0:T(8,128)(2,1)}, bf16[4,32,1024]{2,1,0:T(8,128)(2,1)S(1)}, u32[]{:S(2)}, u32[]{:S(2)}) collective-permute-start(bf16[4,32,1024]{2,1,0:T(8,128)(2,1)} %get-tuple-element.109.c0), channel_id=1, source_target_pairs={{0,2},{1,3},{2,0},{3,1},{4,6},{5,7},{6,4},{7,5},{8,10},{9,11},{10,... | collective-permute-start | bytes 786440 | tf_op jit(solution)/shard_map/ppermute | solution.py:270
  203.2 22.8 %collective-permute-start.25 = (bf16[4,32,1024]{2,1,0:T(8,128)(2,1)}, bf16[4,32,1024]{2,1,0:T(8,128)(2,1)S(1)}, u32[]{:S(2)}, u32[]{:S(2)}) collective-permute-start(bf16[4,32,1024]{2,1,0:T(8,128)(2,1)} %get-tuple-element.109.c0), channel_id=1, source_target_pairs={{0,1},{1,0},{2,3},{3,2},{4,5},{5,4},{6,7},{7,6},{8,9},{9,8},{10,11... | collective-permute-start | bytes 786440 | tf_op jit(solution)/shard_map/ppermute | solution.py:270
  204.5 9.9 %copy-start.17 = (f32[64,256]{1,0:T(8,128)S(1)}, f32[64,256]{1,0:T(8,128)}, u32[]{:S(2)}) copy-start(f32[64,256]{1,0:T(8,128)} %concatenate.41) | copy-start | bytes 196612
  204.5 9.9 %copy-start.18 = (f32[64,256]{1,0:T(8,128)S(1)}, f32[64,256]{1,0:T(8,128)}, u32[]{:S(2)}) copy-start(f32[64,256]{1,0:T(8,128)} %concatenate.42) | copy-start | bytes 196612
  204.5 9.9 %copy-start.19 = (f32[64,256]{1,0:T(8,128)S(1)}, f32[64,256]{1,0:T(8,128)}, u32[]{:S(2)}) copy-start(f32[64,256]{1,0:T(8,128)} %concatenate.44) | copy-start | bytes 196612
  204.5 9.9 %copy-start.20 = (f32[64,256]{1,0:T(8,128)S(1)}, f32[64,256]{1,0:T(8,128)}, u32[]{:S(2)}) copy-start(f32[64,256]{1,0:T(8,128)} %concatenate.45) | copy-start | bytes 196612
  208.6 11.2 %copy-start.5 = (f32[512,128]{0,1:T(8,128)S(1)}, f32[512,128]{0,1:T(8,128)}, u32[]{:S(2)}) copy-start(f32[512,128]{0,1:T(8,128)} %add.157) | copy-start | bytes 786436
  209.3 16.7 %copy-start.12 = (bf16[4,32,1024]{2,1,0:T(8,128)(2,1)}, bf16[4,32,1024]{2,1,0:T(8,128)(2,1)S(1)}, u32[]{:S(2)}) copy-start(bf16[4,32,1024]{2,1,0:T(8,128)(2,1)S(1)} %collective-permute-done.20.c2) | copy-start | bytes 786436
  210.3 8.4 %collective-permute-start.21 = (f32[32,512]{1,0:T(8,128)S(1)}, f32[32,512]{1,0:T(8,128)S(1)}, u32[]{:S(2)}, u32[]{:S(2)}) collective-permute-start(f32[32,512]{1,0:T(8,128)S(1)} %get-tuple-element.188), channel_id=1, source_target_pairs={{0,1},{1,0},{2,3},{3,2},{4,5},{5,4},{6,7},{7,6},{8,9},{9,8},{10,11... | collective-permute-start | bytes 196616 | tf_op jit(solution)/shard_map/ppermute | solution.py:270
  211.2 7.7 %collective-permute-start.22 = (f32[32,512]{1,0:T(8,128)S(1)}, f32[32,512]{1,0:T(8,128)S(1)}, u32[]{:S(2)}, u32[]{:S(2)}) collective-permute-start(f32[32,512]{1,0:T(8,128)S(1)} %get-tuple-element.190), channel_id=1, source_target_pairs={{0,2},{1,3},{2,0},{3,1},{4,6},{5,7},{6,4},{7,5},{8,10},{9,11},{10,... | collective-permute-start | bytes 196616 | tf_op jit(solution)/shard_map/ppermute | solution.py:270
  213.0 5.9 %collective-permute-start.23 = (f32[32,512]{1,0:T(8,128)S(1)}, f32[32,512]{1,0:T(8,128)S(1)}, u32[]{:S(2)}, u32[]{:S(2)}) collective-permute-start(f32[32,512]{1,0:T(8,128)S(1)} %get-tuple-element.189), channel_id=1, source_target_pairs={{0,3},{1,2},{2,1},{3,0},{4,7},{5,6},{6,5},{7,4},{8,11},{9,10},{10,... | collective-permute-start | bytes 196616 | tf_op jit(solution)/shard_map/ppermute | solution.py:270
  215.4 10.5 %collective-permute-start.24 = (f32[128,512]{1,0:T(8,128)S(1)}, f32[128,512]{1,0:T(8,128)S(1)}, u32[]{:S(2)}, u32[]{:S(2)}) collective-permute-start(f32[128,512]{1,0:T(8,128)S(1)} %fusion.1), channel_id=1, source_target_pairs={{0,64},{64,0},{1,65},{65,1},{2,66},{66,2},{3,67},{67,3},{4,68},{68... | collective-permute-start | bytes 786440 | tf_op jit(solution)/shard_map/ppermute | solution.py:301
  218.8 7.2 %collective-permute-start.26 = (bf16[4,32,1024]{2,1,0:T(8,128)(2,1)S(1)}, bf16[4,32,1024]{2,1,0:T(8,128)(2,1)}, u32[]{:S(2)}, u32[]{:S(2)}) collective-permute-start(bf16[4,32,1024]{2,1,0:T(8,128)(2,1)S(1)} %collective-permute-done.20.c2), channel_id=1, source_target_pairs={{0,1},{1,0},{2,3},{3,2},{4,5},{5,4},{6,7},{7,6},{8,9},{9,8},{10,11... | collective-permute-start | bytes 786440 | tf_op jit(solution)/shard_map/ppermute | solution.py:270
  226.0 14.8 %copy-start.14 = (f32[128,512]{1,0:T(8,128)}, f32[128,512]{1,0:T(8,128)S(1)}, u32[]{:S(2)}) copy-start(f32[128,512]{1,0:T(8,128)S(1)} %add.166) | copy-start | bytes 786436
  231.1 20.1 %copy-start.25 = (f32[128,256]{1,0:T(8,128)S(1)}, f32[128,256]{1,0:T(8,128)}, u32[]{:S(2)}) copy-start(f32[128,256]{1,0:T(8,128)} %get-tuple-element.121) | copy-start | bytes 393220
  231.1 23.1 %copy-start.21 = (f32[64,512]{1,0:T(8,128)S(1)}, f32[64,512]{1,0:T(8,128)}, u32[]{:S(2)}) copy-start(f32[64,512]{1,0:T(8,128)} %get-tuple-element.93) | copy-start | bytes 393220
  231.1 7.6 %collective-permute-start.27 = (f32[128,512]{1,0:T(8,128)S(1)}, f32[128,512]{1,0:T(8,128)S(1)}, u32[]{:S(2)}, u32[]{:S(2)}) collective-permute-start(f32[128,512]{1,0:T(8,128)S(1)} %bitcast_add_fusion), channel_id=1, source_target_pairs={{0,64},{64,0},{1,65},{65,1},{2,66},{66,2},{3,67},{67,3},{4,68},{68... | collective-permute-start | bytes 786440 | tf_op jit(solution)/shard_map/ppermute | solution.py:301
  239.4 8.2 %collective-permute-start.29 = (f32[4,32,512]{2,1,0:T(8,128)S(1)}, f32[4,32,512]{2,1,0:T(8,128)S(1)}, u32[]{:S(2)}, u32[]{:S(2)}) collective-permute-start(f32[4,32,512]{2,1,0:T(8,128)S(1)} %bitcast.169), channel_id=1, source_target_pairs={{0,2},{1,3},{2,0},{3,1},{4,6},{5,7},{6,4},{7,5},{8,10},{9,11},{10,... | collective-permute-start | bytes 786440 | tf_op jit(solution)/shard_map/ppermute | solution.py:270
  240.8 10.4 %collective-permute-start.31 = (f32[128,256]{1,0:T(8,128)S(1)}, f32[128,256]{1,0:T(8,128)S(1)}, u32[]{:S(2)}, u32[]{:S(2)}) collective-permute-start(f32[128,256]{1,0:T(8,128)S(1)} %copy-done.31), channel_id=1, source_target_pairs={{0,64},{64,0},{1,65},{65,1},{2,66},{66,2},{3,67},{67,3},{4,68},{68... | collective-permute-start | bytes 393224 | tf_op jit(solution)/shard_map/ppermute | solution.py:301
  240.8 10.4 %collective-permute-start.28 = (f32[4,32,512]{2,1,0:T(8,128)S(1)}, f32[4,32,512]{2,1,0:T(8,128)S(1)}, u32[]{:S(2)}, u32[]{:S(2)}) collective-permute-start(f32[4,32,512]{2,1,0:T(8,128)S(1)} %bitcast.170), channel_id=1, source_target_pairs={{0,1},{1,0},{2,3},{3,2},{4,5},{5,4},{6,7},{7,6},{8,9},{9,8},{10,11... | collective-permute-start | bytes 786440 | tf_op jit(solution)/shard_map/ppermute | solution.py:270
  247.6 4.7 %collective-permute-start.30 = (f32[4,32,512]{2,1,0:T(8,128)S(1)}, f32[4,32,512]{2,1,0:T(8,128)S(1)}, u32[]{:S(2)}, u32[]{:S(2)}) collective-permute-start(f32[4,32,512]{2,1,0:T(8,128)S(1)} %collective-permute-done.29.t2), channel_id=1, source_target_pairs={{0,1},{1,0},{2,3},{3,2},{4,5},{5,4},{6,7},{7,6},{8,9},{9,8},{10,11... | collective-permute-start | bytes 786440 | tf_op jit(solution)/shard_map/ppermute | solution.py:270
  252.3 25.9 %collective-permute-start.34 = (f32[4,32,256]{2,1,0:T(8,128)S(1)}, f32[4,32,256]{2,1,0:T(8,128)S(1)}, u32[]{:S(2)}, u32[]{:S(2)}) collective-permute-start(f32[4,32,256]{2,1,0:T(8,128)S(1)} %bitcast.165), channel_id=1, source_target_pairs={{0,2},{1,3},{2,0},{3,1},{4,6},{5,7},{6,4},{7,5},{8,10},{9,11},{10,... | collective-permute-start | bytes 393224 | tf_op jit(solution)/shard_map/ppermute | solution.py:270
  252.9 36.7 %collective-permute-start.38 = (f32[4,32,256]{2,1,0:T(8,128)S(1)}, f32[4,32,256]{2,1,0:T(8,128)S(1)}, u32[]{:S(2)}, u32[]{:S(2)}) collective-permute-start(f32[4,32,256]{2,1,0:T(8,128)S(1)} %bitcast.166), channel_id=1, source_target_pairs={{0,1},{1,0},{2,3},{3,2},{4,5},{5,4},{6,7},{7,6},{8,9},{9,8},{10,11... | collective-permute-start | bytes 393224 | tf_op jit(solution)/shard_map/ppermute | solution.py:270
  254.1 24.1 %collective-permute-start.32 = (f32[768,256]{1,0:T(8,128)}, f32[768,256]{1,0:T(8,128)S(1)}, u32[]{:S(2)}, u32[]{:S(2)}) collective-permute-start(f32[768,256]{1,0:T(8,128)} %get-tuple-element.122), channel_id=1, source_target_pairs={{0,64},{64,0},{1,65},{65,1},{2,66},{66,2},{3,67},{67,3},{4,68},{68... | collective-permute-start | bytes 2359304 | tf_op jit(solution)/shard_map/ppermute | solution.py:301
  254.1 24.1 %collective-permute-start.33 = (f32[2,32,512]{2,1,0:T(8,128)S(1)}, f32[2,32,512]{2,1,0:T(8,128)S(1)}, u32[]{:S(2)}, u32[]{:S(2)}) collective-permute-start(f32[2,32,512]{2,1,0:T(8,128)S(1)} %bitcast.175), channel_id=1, source_target_pairs={{0,2},{1,3},{2,0},{3,1},{4,6},{5,7},{6,4},{7,5},{8,10},{9,11},{10,... | collective-permute-start | bytes 393224 | tf_op jit(solution)/shard_map/ppermute | solution.py:270
  278.2 11.4 %collective-permute-start.39 = (f32[4,32,256]{2,1,0:T(8,128)S(1)}, f32[4,32,256]{2,1,0:T(8,128)S(1)}, u32[]{:S(2)}, u32[]{:S(2)}) collective-permute-start(f32[4,32,256]{2,1,0:T(8,128)S(1)} %collective-permute-done.34), channel_id=1, source_target_pairs={{0,1},{1,0},{2,3},{3,2},{4,5},{5,4},{6,7},{7,6},{8,9},{9,8},{10,11... | collective-permute-start | bytes 393224 | tf_op jit(solution)/shard_map/ppermute | solution.py:270
  285.9 16.7 %collective-permute-start.35 = (f32[16,32,256]{2,1,0:T(8,128)S(1)}, f32[16,32,256]{2,1,0:T(8,128)S(1)}, u32[]{:S(2)}, u32[]{:S(2)}) collective-permute-start(f32[16,32,256]{2,1,0:T(8,128)S(1)} %get-tuple-element.151), channel_id=1, source_target_pairs={{0,1},{1,0},{2,3},{3,2},{4,5},{5,4},{6,7},{7,6},{8,9},{9,8},{10,11... | collective-permute-start | bytes 1572872 | tf_op jit(solution)/shard_map/ppermute | solution.py:270
  286.5 16.1 %collective-permute-start.36 = (f32[16,32,256]{2,1,0:T(8,128)S(1)}, f32[16,32,256]{2,1,0:T(8,128)S(1)}, u32[]{:S(2)}, u32[]{:S(2)}) collective-permute-start(f32[16,32,256]{2,1,0:T(8,128)S(1)} %get-tuple-element.150), channel_id=1, source_target_pairs={{0,2},{1,3},{2,0},{3,1},{4,6},{5,7},{6,4},{7,5},{8,10},{9,11},{10,... | collective-permute-start | bytes 1572872 | tf_op jit(solution)/shard_map/ppermute | solution.py:270
  287.1 25.8 %collective-permute-start.37 = (f32[16,32,256]{2,1,0:T(8,128)S(1)}, f32[16,32,256]{2,1,0:T(8,128)S(1)}, u32[]{:S(2)}, u32[]{:S(2)}) collective-permute-start(f32[16,32,256]{2,1,0:T(8,128)S(1)} %get-tuple-element.149), channel_id=1, source_target_pairs={{0,3},{1,2},{2,1},{3,0},{4,7},{5,6},{6,5},{7,4},{8,11},{9,10},{10,... | collective-permute-start | bytes 1572872 | tf_op jit(solution)/shard_map/ppermute | solution.py:270
  302.6 10.8 %copy-start.9 = (f32[16,32,256]{2,1,0:T(8,128)}, f32[16,32,256]{2,1,0:T(8,128)S(1)}, u32[]{:S(2)}) copy-start(f32[16,32,256]{2,1,0:T(8,128)S(1)} %collective-permute-done.35.g1) | copy-start | bytes 1572868
  302.6 10.8 %copy-start.10 = (f32[16,32,256]{2,1,0:T(8,128)}, f32[16,32,256]{2,1,0:T(8,128)S(1)}, u32[]{:S(2)}) copy-start(f32[16,32,256]{2,1,0:T(8,128)S(1)} %collective-permute-done.36.g2) | copy-start | bytes 1572868
  312.9 6.2 %collective-permute-start.41 = (f32[2,32,512]{2,1,0:T(8,128)S(1)}, f32[2,32,512]{2,1,0:T(8,128)S(1)}, u32[]{:S(2)}, u32[]{:S(2)}) collective-permute-start(f32[2,32,512]{2,1,0:T(8,128)S(1)} %collective-permute-done.33), channel_id=1, source_target_pairs={{0,1},{1,0},{2,3},{3,2},{4,5},{5,4},{6,7},{7,6},{8,9},{9,8},{10,11... | collective-permute-start | bytes 393224 | tf_op jit(solution)/shard_map/ppermute | solution.py:270
  313.2 5.9 %collective-permute-start.40 = (f32[2,32,512]{2,1,0:T(8,128)S(1)}, f32[2,32,512]{2,1,0:T(8,128)S(1)}, u32[]{:S(2)}, u32[]{:S(2)}) collective-permute-start(f32[2,32,512]{2,1,0:T(8,128)S(1)} %bitcast.176), channel_id=1, source_target_pairs={{0,1},{1,0},{2,3},{3,2},{4,5},{5,4},{6,7},{7,6},{8,9},{9,8},{10,11... | collective-permute-start | bytes 393224 | tf_op jit(solution)/shard_map/ppermute | solution.py:270
  (18 other events, 74.3 us)
Sparse Core Ops, SparseCore 0:
  110.3 55.4 all-gather.5
  239.5 51.5 all-gather.3

commit v3 on v2

--- a/solution.py
+++ b/solution.py
@@ -162,18 +162,16 @@
         out[...] = f - dot16(jnp.concatenate([u0, u1], axis=1), upan, 1, 1)
 
 
-def corner_kernel(q_ref, panel_ref, u0_ref, u1_ref, f_ref, c0, c1, c2, c3, first_ref, send_ref):
-    f, u0, u1 = [jnp.concatenate([picked(panel_ref[i], x) for i in range(4)], axis=0) for x in (f_ref, u0_ref, u1_ref)]
-    s = f - dot16(jnp.concatenate([u0, u1], axis=1), columns_of((c0, c1, c2, c3), q_ref), 1, 1)
-    first_ref[...] = s[:, 0:256]
-    send_ref[...] = s[:, 256:512]
-
-
-def bulk_kernel(q_ref, u0_ref, u1_ref, f_ref, c0, c1, c2, c3, own_ref, other_ref):
+def bulk_kernel(q_ref, panel_ref, u0_ref, u1_ref, f_ref, c0, c1, c2, c3, own_ref, other_ref, first_ref, send_ref):
     rows = jnp.concatenate([u0_ref[8:32].reshape(768, 512), u1_ref[8:32].reshape(768, 512)], axis=1)
     s = f_ref[8:32].reshape(768, 512) - dot16(rows, columns_of((c0, c1, c2, c3), q_ref), 1, 1)
     own_ref[...] = s[:, 0:256]
     other_ref[...] = s[:, 256:512]
+    for m in range(4):
+        b = panel_ref[m]
+        rows = pl.ds(pl.multiple_of(32 * jnp.maximum(b, 0), 32), 32)
+        first_ref[32 * m:32 * m + 32, :] = jnp.where(b >= 0, own_ref[rows, :], 0.0)
+        send_ref[32 * m:32 * m + 32, :] = jnp.where(b >= 0, other_ref[rows, :], 0.0)
 
 
 def root_kernel(q_ref, t0, t1, t2, t3, inv_ref, a, g):
@@ -374,7 +372,9 @@
             m = 2 * g + j
             pairs.append((4 * g, (m // 32 * 16 + m % 16) * 4 + m // 16))
         raw_rows += lax.ppermute(tile_top[:, 128 * j:128 * j + 128], ("child", "row", "col"), pairs)
-    u1_all, placed, factor0, raw_rows = lax.optimization_barrier((u1_all, placed, factor0, raw_rows))
+    factor1 = p1.reshape(2, 32, 512)
+    u1_all, placed, factor0, raw_rows, far1 = lax.optimization_barrier(
+        (u1_all, placed, factor0, raw_rows, across(after(factor1, u1), 2)))
     raw_rows = raw_rows.T
     f_bulk = exchange(placed, "row").reshape(32, 32, 512)
 
@@ -392,23 +392,22 @@
     z = exchange_col(z.reshape(4, 32, 512), q).reshape(128, 512) + raw_rows
     half, block = sds((768, 256)), sds((128, 256))
     z, t, u_bulk, f_bulk = lax.optimization_barrier((z, t, u_bulk, f_bulk))
-    first, sent = call(corner_kernel, (block, block), 2, 7, flops=10**9, name="corner")(
+    z_swapped = swap_child(z)
+    t = t.reshape(4, 32, 512)
+    t_far = across(t, 2)
+    own, other, first, sent = call(
+        bulk_kernel, (half, half, block, block), 2, 7, flops=4 * 10**9, name="bulk")(
         at, panel_idx, u0_all, u1_all, f_bulk, *u_bulk)
-    z_swapped = swap_child(z)
-    own, other = call(bulk_kernel, (half, half), 1, 7, flops=4 * 10**9, name="bulk")(
-        at, u0_all, u1_all, after(f_bulk, sent), *u_bulk)
-    z_swapped, own, other = lax.optimization_barrier((z_swapped, own, other))
+    z_swapped, own, other, t_far = lax.optimization_barrier((z_swapped, own, other, t_far))
     z = z + z_swapped
     panel = lax.all_gather(z, "row", tiled=True)
 
-    t_all = around(t.reshape(4, 32, 512))
+    t_all = [t, across(t, 1), t_far, across(t_far, 1)]
     head_cols = (top + first + swap_child(sent)).reshape(4, 32, 256)
     t_all, z, other, head_cols = lax.optimization_barrier((t_all, z, other, head_cols))
-    factor1 = p1.reshape(2, 32, 512)
-    far1 = across(after(factor1, other), 2)
     head_far = across(head_cols, 2)
     inv_root = call(root_kernel, sds((512, 512)), 1, 4, CHOL, 2 * 10**10, "root")(at, *t_all)
-    got, inv_root, far1, head_far = lax.optimization_barrier((swap_child(other), inv_root, far1, head_far))
+    got, inv_root, head_far = lax.optimization_barrier((swap_child(other), inv_root, head_far))
     spread = call(spread_kernel, sds((64, 32, 256)), 2, 2, name="spread")(
         mine, theirs, own.reshape(24, 32, 256), got.reshape(24, 32, 256))
     arrived = sent_col(spread.reshape(4, 16, 32, 256), q)

time: 333 us -> 327 us (0.982)
  Pallas kernels: 109 us -> 105 us
  starting transfers between devices: 104 us -> 100 us
    all_gather x1, waiting for transfers between devices: 0.64 us -> 8 us  [local(): panel = lax.all_gather(z, 'row', tiled=True)]
    ppermute x33, waiting for transfers between devices: 31.7 us -> 25.6 us  [across(): return lax.ppermute(x, 'col', [(i, i ^ k) for i in range(4)])]
    ppermute x33, starting transfers between devices: 52.9 us -> 49.2 us  [across(): return lax.ppermute(x, 'col', [(i, i ^ k) for i in range(4)])]
    pallas_call x2 -> x1, Pallas kernels: 8.32 us -> 4.72 us  [local(): call(bulk_kernel, (half, half, block, block), 2, 7, flops=4 * 10 ** 9, na...]
  transfers between devices with their start and end apart: 50 -> 50, of which waited for: 16 -> 16; matrix products, arithmetic and copies ran while one was open for 7% -> 7% of each run, Pallas kernels for 32% -> 33%
where the time goes in v3:
time: 327 us; the launch traced here: 322 us
  Pallas kernels  105 us (32%)
  starting transfers between devices  100 us (31%)
  waiting for transfers between devices  66 us (20%)
  local copies, waits for them, and re-layouts  19.8 us (6%)
  other arithmetic  15.8 us (5%)
  between operations  14.8 us (5%)
    ppermute x33, starting transfers between devices, across(): return lax.ppermute(x, 'col', [(i, i ^ k) for i in range(4)])  49.2 us
    all_to_all x6, starting transfers between devices, exchange(): return lax.all_to_all(x, axis, split_axis=0, concat_axis=0, tiled=True)  40.8 us
    ppermute x33, waiting for transfers between devices, across(): return lax.ppermute(x, 'col', [(i, i ^ k) for i in range(4)])  25.6 us
    pallas_call x1, Pallas kernels, local(): call(second_kernel, (sds((64, 512)), sds((ROWS, 64, 512), BF16)), 1, 4, [...  25.5 us
    pallas_call x1, Pallas kernels, local(): call(head_kernel, (sds((512, 512)), sds((64, 512)), sds((ROWS, 64, 512),...  22.2 us
    pallas_call x1, Pallas kernels, local(): call(root_kernel, sds((512, 512)), 1, 4, CHOL, 2 * 10 ** 10, 'root')  20.9 us
    all_to_all x6, waiting for transfers between devices, exchange(): return lax.all_to_all(x, axis, split_axis=0, concat_axis=0, tiled=True)  12.6 us
    pallas_call x1, Pallas kernels, local(): pl.pallas_call(factor_kernel, out_shape=(sds((2048, 512)), sds((2048, 512...  11.4 us
  transfers between devices with their start and end apart: 50, of which 16 were waited for; matrix products, arithmetic and copies ran while one was open for 7% of the time, Pallas kernels for 33%

profile of v3, /device:TPU:1, one launch (start us, length us, event | category | flops | bytes accessed | tf_op | source)
XLA Modules:
  0.0 321.9 jit_solution(8840079765995644434)
XLA Ops:
  7.2 1.2 slice.81
  8.8 1.0 slice_bitcast_fusion.1
  9.8 1.4 collective-permute-start
  11.2 1.4 collective-permute-start.1
  12.6 1.4 collective-permute-start.2
  14.1 1.3 fusion
  16.3 7.5 %all-to-all-start = ((f32[16,4,1536]{2,1,0:T(4,128)}), f32[16,4,1536]{2,1,0:T(4,128)S(1)}, u32[]{:S(2)}, u32[]{:S(2)}) async-start(f32[16,4,1536]{2,1,0:T(4,128)} %reshape.141), calls=%async_computation | async-start | bytes 786432 | tf_op jit(solution)/shard_map/all_to_all | solution.py:252
  23.8 8.0 %all-to-all-done = f32[16,4,1536]{2,1,0:T(4,128)S(1)} async-done(((f32[16,4,1536]{2,1,0:T(4,128)}), f32[16,4,1536]{2,1,0:T(4,128)S(1)}, u32[]{:S(2)}, u32[]{:S(2)}) %all-to-all-start) | async-done | bytes 393248 | tf_op jit(solution)/shard_map/all_to_all | solution.py:252
  31.8 16.7 %collective-permute-start.4 = (f32[2,4,512]{2,1,0:T(4,128)S(1)}, f32[2,4,512]{2,1,0:T(4,128)S(1)}, u32[]{:S(2)}, u32[]{:S(2)}) collective-permute-start(f32[2,4,512]{2,1,0:T(4,128)S(1)} %slice.113), channel_id=1, source_target_pairs={{0,2},{1,3},{2,0},{3,1},{4,6},{5,7},{6,4},{7,5},{8,10},{9,11},{10,... | collective-permute-start | bytes 49160 | tf_op jit(solution)/shard_map/ppermute | solution.py:268
  48.6 0.9 collective-permute-done.4
  49.6 2.4 collective-permute-start.5
  52.9 1.2 broadcast_in_dim.98
  54.0 3.7 %all-to-all-start.1 = ((f32[16,8,4,512]{3,2,1,0:T(4,128)}), f32[16,8,4,512]{3,2,1,0:T(4,128)S(1)}, u32[]{:S(2)}, u32[]{:S(2)}) async-start(f32[16,8,4,512]{3,2,1,0:T(4,128)} %broadcast_in_dim.98), calls=%async_computation.1 | async-start | bytes 2097152 | tf_op jit(solution)/shard_map/all_to_all | solution.py:252
  60.1 3.2 collective-permute-done.7
  63.3 1.3 collective-permute-start.8
  66.0 2.3 collective-permute-start.11
  69.2 4.6 %all-to-all-done.1.d_ref = f32[16,8,4,512]{3,2,1,0:T(4,128)S(1)} async-done(((f32[16,8,4,512]{3,2,1,0:T(4,128)}), f32[16,8,4,512]{3,2,1,0:T(4,128)S(1)}, u32[]{:S(2)}, u32[]{:S(2)}) %all-to-all-start.1) | async-done | bytes 1048608 | tf_op jit(solution)/shard_map/all_to_all | solution.py:252
  73.8 2.0 broadcast_in_dim.99
  75.8 4.4 %all-to-all-start.2 = ((f32[16,9,4,1024]{3,2,1,0:T(4,128)}), f32[16,9,4,1024]{3,2,1,0:T(4,128)}, u32[]{:S(2)}, u32[]{:S(2)}) async-start(f32[16,9,4,1024]{3,2,1,0:T(4,128)} %broadcast_in_dim.99), calls=%async_computation.2 | async-start | bytes 4718592 | tf_op jit(solution)/shard_map/all_to_all | solution.py:252
  81.2 2.0 fusion.2
  84.6 1.6 place_panel.1
  86.2 22.2 %head.1 = (f32[512,512]{1,0:T(8,128)}, f32[64,512]{1,0:T(8,128)}, bf16[16,64,512]{2,1,0:T(8,128)(2,1)}) custom-call(f32[16,8,4,512]{3,2,1,0:T(4,128)} %copy-done.7, f32[64,512]{1,0:T(8,128)} %get-tuple-element.185.c_ref), custom_call_target="tpu_custom_call" | custom-call | flops 20000000000 | bytes 1048576 | tf_op jit(solution)/shard_map/head/pallas_call | solution.py:350
  108.4 1.8 collective-permute-start.12
  110.2 6.8 %all-to-all-start.3 = ((bf16[16,64,512]{2,1,0:T(8,128)(2,1)}), bf16[16,64,512]{2,1,0:T(8,128)(2,1)S(1)}, u32[]{:S(2)}, u32[]{:S(2)}) async-start(bf16[16,64,512]{2,1,0:T(8,128)(2,1)} %get-tuple-element.84.u0_ref), calls=%async_computation.3 | async-start | bytes 2097152 | tf_op jit(solution)/shard_map/all_to_all | solution.py:252
  117.0 25.5 %second.1 = (f32[64,512]{1,0:T(8,128)}, bf16[16,64,512]{2,1,0:T(8,128)(2,1)}) custom-call(s32[1]{0:T(128)} %bitcast.mask_ref, f32[16,9,4,1024]{3,2,1,0:T(4,128)} %all-to-all-done.2.d_ref, f32[512,512]{1,0:T(8,128)} %get-tuple-element.83.inv0_ref, f32[64,512]{1,0:T(8,128)} %get-tuple-element.184.c_ref, bf16[16,64,512]{2,1,0:T(8,128)(2,1)} %get-tuple-element.84.u0_ref), custom_call_target="tpu_custom_call" | custom-call | flops 30000001024 | bytes 1048576 | tf_op jit(solution)/shard_map/second/pallas_call | solution.py:357
  142.5 6.8 %all-to-all-start.4 = ((bf16[16,64,512]{2,1,0:T(8,128)(2,1)}), bf16[16,64,512]{2,1,0:T(8,128)(2,1)S(1)}, u32[]{:S(2)}, u32[]{:S(2)}) async-start(bf16[16,64,512]{2,1,0:T(8,128)(2,1)} %get-tuple-element.87), calls=%async_computation.4 | async-start | bytes 2097152 | tf_op jit(solution)/shard_map/all_to_all | solution.py:252
  150.3 2.1 pad_maximum_fusion.1.y_ref
  152.4 1.2 collective-permute-start.17
  153.6 4.3 %collective-permute-start.13 = (f32[2,32,512]{2,1,0:T(8,128)}, f32[2,32,512]{2,1,0:T(8,128)S(1)}, u32[]{:S(2)}, u32[]{:S(2)}) collective-permute-start(f32[2,32,512]{2,1,0:T(8,128)} %bitcast.176), channel_id=1, source_target_pairs={{0,1},{1,0},{2,3},{3,2},{4,5},{5,4},{6,7},{7,6},{8,9},{9,8},{10,11... | collective-permute-start | bytes 393224 | tf_op jit(solution)/shard_map/ppermute | solution.py:268
  157.9 1.3 collective-permute-start.15
  159.9 3.4 %place.1 = f32[16,64,512]{2,1,0:T(8,128)} custom-call(s32[64]{0:T(128)} %select_reduce_fusion.bulk_ref, f32[64,3072]{1,0:T(8,128)} %pad_maximum_fusion.1.y_ref), custom_call_target="tpu_custom_call" | custom-call | bytes 1048576 | tf_op jit(solution)/shard_map/place/pallas_call | solution.py:364
  164.2 8.4 %collective-permute-done.15 = f32[512,128]{0,1:T(8,128)S(1)} collective-permute-done((f32[512,128]{0,1:T(8,128)S(1)}, f32[512,128]{0,1:T(8,128)S(1)}, u32[]{:S(2)}, u32[]{:S(2)}) %collective-permute-start.15) | collective-permute-done | bytes 262176 | tf_op jit(solution)/shard_map/ppermute | solution.py:374
  173.4 1.0 copy-done.1
  174.4 11.7 %all-to-all-start.5 = ((f32[16,64,512]{2,1,0:T(8,128)}), f32[16,64,512]{2,1,0:T(8,128)S(1)}, u32[]{:S(2)}, u32[]{:S(2)}) async-start(f32[16,64,512]{2,1,0:T(8,128)} %place.1), calls=%async_computation.5 | async-start | bytes 4194304 | tf_op jit(solution)/shard_map/all_to_all | solution.py:252
  187.0 2.4 select.17
  189.4 9.9 %collective-permute-done.19.c2 = bf16[4,32,1024]{2,1,0:T(8,128)(2,1)S(1)} collective-permute-done((bf16[4,32,1024]{2,1,0:T(8,128)(2,1)}, bf16[4,32,1024]{2,1,0:T(8,128)(2,1)S(1)}, u32[]{:S(2)}, u32[]{:S(2)}) %collective-permute-start.19) | collective-permute-done | bytes 262176 | tf_op jit(solution)/shard_map/ppermute | solution.py:268
  199.9 1.6 fusion.12
  203.9 4.0 %panel.1 = (f32[128,512]{1,0:T(8,128)}, f32[128,512]{1,0:T(8,128)}) custom-call(s32[1]{0:T(128)} %bitcast.39.q_ref, s32[4]{0:T(128)} %get-tuple-element.144.rows_ref, s32[4]{0:T(128)} %slice_bitcast_fusion.6.panel_ref, bf16[32,32,512]{2,1,0:T(8,128)(2,1)} %bitcast.148, bf16[32,32,512]{2,1,0:T(8,128)(2,1)} %bitcast.151, f32[32,32,512]{2,1,0:T(8,128)} %bitcast.155, ...), custom_call_target="tpu_custom_call" | custom-call | flops 1000000000 | bytes 1048576 | tf_op jit(solution)/shard_map/panel/pallas_call | solution.py:386
  207.9 1.7 collective-permute-done.21.c2
  209.6 0.9 dynamic-slice_bitcast_fusion.9
  212.2 2.4 collective-permute-start.24
  214.6 1.0 fusion.1
  215.6 2.4 collective-permute-start.25
  219.2 6.0 %collective-permute-done.25 = f32[128,512]{1,0:T(8,128)S(1)} collective-permute-done((f32[128,512]{1,0:T(8,128)S(1)}, f32[128,512]{1,0:T(8,128)S(1)}, u32[]{:S(2)}, u32[]{:S(2)}) %collective-permute-start.25) | collective-permute-done | bytes 262176 | tf_op jit(solution)/shard_map/ppermute | solution.py:299
  225.3 0.9 collective-permute-start.28
  226.3 1.8 collective-permute-start.29
  228.0 4.7 %bulk.1 = (f32[768,256]{1,0:T(8,128)}, f32[768,256]{1,0:T(8,128)}, f32[128,256]{1,0:T(8,128)}, f32[128,256]{1,0:T(8,128)}) custom-call(s32[1]{0:T(128)} %bitcast.39.q_ref, s32[4]{0:T(128)} %slice_bitcast_fusion.6.panel_ref, bf16[32,32,512]{2,1,0:T(8,128)(2,1)} %bitcast.149, bf16[32,32,512]{2,1,0:T(8,128)(2,1)} %bitcast.152, f32[32,32,512]{2,1,0:T(8,128)} %bitcast.156, ...), custom_call_target="tpu_custom_call" | custom-call | flops 4000000000 | bytes 1048576 | tf_op jit(solution)/shard_map/bulk/pallas_call | solution.py:398
  232.9 6.1 %collective-permute-done.29.t2 = f32[4,32,512]{2,1,0:T(8,128)S(1)} collective-permute-done((f32[4,32,512]{2,1,0:T(8,128)S(1)}, f32[4,32,512]{2,1,0:T(8,128)S(1)}, u32[]{:S(2)}, u32[]{:S(2)}) %collective-permute-start.29) | collective-permute-done | bytes 262176 | tf_op jit(solution)/shard_map/ppermute | solution.py:268
  240.4 1.9 collective-permute-start.30
  242.6 5.1 %collective-permute-done.32 = f32[128,256]{1,0:T(8,128)S(1)} collective-permute-done((f32[128,256]{1,0:T(8,128)}, f32[128,256]{1,0:T(8,128)S(1)}, u32[]{:S(2)}, u32[]{:S(2)}) %collective-permute-start.32) | collective-permute-done | bytes 131104 | tf_op jit(solution)/shard_map/ppermute | solution.py:299
  247.6 0.9 fusion.3
  248.6 1.3 collective-permute-start.34
  249.9 1.1 collective-permute-start.38
  251.6 20.9 %root.1.inv_ref = f32[512,512]{1,0:T(8,128)} custom-call(s32[1]{0:T(128)} %bitcast.39.q_ref, f32[4,32,512]{2,1,0:T(8,128)} %bitcast.168, f32[4,32,512]{2,1,0:T(8,128)} %copy-done.24, f32[4,32,512]{2,1,0:T(8,128)} %copy-done.22, f32[4,32,512]{2,1,0:T(8,128)} %copy-done.25), custom_call_target="tpu_custom_call" | custom-call | flops 20000000000 | bytes 1048576 | tf_op jit(solution)/shard_map/root/pallas_call | solution.py:409
  273.4 3.6 %spread.1 = f32[64,32,256]{2,1,0:T(8,128)} custom-call(s32[64]{0:T(128)} %bitcast.180, s32[64]{0:T(128)} %get-tuple-element.199.theirs_ref, f32[24,32,256]{2,1,0:T(8,128)} %bitcast.160, f32[24,32,256]{2,1,0:T(8,128)} %bitcast.161), custom_call_target="tpu_custom_call" | custom-call | bytes 1048576 | tf_op jit(solution)/shard_map/spread/pallas_call | solution.py:411
  277.1 2.6 dynamic-slice_bitcast_fusion
  280.1 1.8 collective-permute-start.36
  281.9 1.6 collective-permute-start.37
  284.4 8.0 %all-gather.4.cloned.1.call-done.panel_ref = f32[2048,512]{1,0:T(8,128)} async-done(((f32[128,512]{1,0:T(8,128)}), f32[2048,512]{1,0:T(8,128)}) %all-gather.4.cloned.1.call-update) | async-done | bytes 4194320 | tf_op jit(solution)/shard_map/all_gather | solution.py:403
  292.4 11.4 %factor.1 = (f32[2048,512]{1,0:T(8,128)}, bf16[2048,512]{1,0:T(8,128)(2,1)}, bf16[512,256]{1,0:T(8,128)(2,1)}) custom-call(s32[2]{0:T(128)} %add_convert_fusion.flag_ref, f32[2048,512]{1,0:T(8,128)} %all-gather.4.cloned.1.call-done.panel_ref, f32[512,512]{1,0:T(8,128)} %root.1.inv_ref, f32[4,4,32,256]{3,2,1,0:T(8,128)} %pad_maximum_fusion.3.cp_ref), custom_call_target="tpu_custom_call" | custom-call | flops 10000000000 | bytes 1048576 | tf_op jit(solution)/shard_map/factor/pallas_call | solution.py:421
  303.8 2.7 collective-permute-done.37.g3
  307.3 5.4 %last.1 = f32[2048,256]{1,0:T(8,128)} custom-call(s32[1]{0:T(128)} %bitcast.39.q_ref, bf16[2048,512]{1,0:T(8,128)(2,1)} %get-tuple-element.133.u_ref, bf16[512,256]{1,0:T(8,128)(2,1)} %get-tuple-element.138.ug_ref, f32[2048,256]{1,0:T(8,128)} %root_ref.1, f32[16,32,256]{2,1,0:T(8,128)} %get-tuple-element.139.g0, f32[16,32,256]{2,1,0:T(8,128)} %copy-done.9, ...), custom_call_target="tpu_custom_call" | custom-call | tf_op jit(solution)/shard_map/last/pallas_call | solution.py:436
  312.7 1.0 select_bitcast_fusion.3
  313.8 1.0 copy.22
  (159 shorter events, 25.3 us)
Async XLA Ops:
  9.8 38.7 %copy-start.21 = (s32[2,24]{1,0:T(2,128)S(1)}, s32[2,24]{1,0:T(2,128)}, u32[]{:S(2)}) copy-start(s32[2,24]{1,0:T(2,128)} %param.5) | copy-start | bytes 580
  9.8 4.4 %collective-permute-start = (f32[64,1536]{1,0:T(8,128)}, f32[64,1536]{1,0:T(8,128)}, u32[]{:S(2)}, u32[]{:S(2)}) collective-permute-start(f32[64,1536]{1,0:T(8,128)} %get-tuple-element.158), channel_id=1, source_target_pairs={{0,1},{4,5},{8,9},{12,13},{16,17},{20,21},{24,25},{28,29},{32,33},... | collective-permute-start | bytes 1179656 | tf_op jit(solution)/shard_map/ppermute | solution.py:281
  11.2 3.0 collective-permute-start.1
  12.6 1.5 collective-permute-start.2
  16.3 15.5 %all-to-all-start = ((f32[16,4,1536]{2,1,0:T(4,128)}), f32[16,4,1536]{2,1,0:T(4,128)S(1)}, u32[]{:S(2)}, u32[]{:S(2)}) async-start(f32[16,4,1536]{2,1,0:T(4,128)} %reshape.141), calls=%async_computation | async-start | bytes 786432 | tf_op jit(solution)/shard_map/all_to_all | solution.py:252
  31.8 17.8 %collective-permute-start.4 = (f32[2,4,512]{2,1,0:T(4,128)S(1)}, f32[2,4,512]{2,1,0:T(4,128)S(1)}, u32[]{:S(2)}, u32[]{:S(2)}) collective-permute-start(f32[2,4,512]{2,1,0:T(4,128)S(1)} %slice.113), channel_id=1, source_target_pairs={{0,2},{1,3},{2,0},{3,1},{4,6},{5,7},{6,4},{7,5},{8,10},{9,11},{10,... | collective-permute-start | bytes 49160 | tf_op jit(solution)/shard_map/ppermute | solution.py:268
  48.5 3.5 %collective-permute-start.3 = (f32[2,4,512]{2,1,0:T(4,128)S(1)}, f32[2,4,512]{2,1,0:T(4,128)S(1)}, u32[]{:S(2)}, u32[]{:S(2)}) collective-permute-start(f32[2,4,512]{2,1,0:T(4,128)S(1)} %slice.113), channel_id=1, source_target_pairs={{0,1},{1,0},{2,3},{3,2},{4,5},{5,4},{6,7},{7,6},{8,9},{9,8},{10,11... | collective-permute-start | bytes 49160 | tf_op jit(solution)/shard_map/ppermute | solution.py:268
  49.6 3.3 %collective-permute-start.5 = (f32[2,4,512]{2,1,0:T(4,128)S(1)}, f32[2,4,512]{2,1,0:T(4,128)S(1)}, u32[]{:S(2)}, u32[]{:S(2)}) collective-permute-start(f32[2,4,512]{2,1,0:T(4,128)S(1)} %collective-permute-done.4), channel_id=1, source_target_pairs={{0,1},{1,0},{2,3},{3,2},{4,5},{5,4},{6,7},{7,6},{8,9},{9,8},{10,11... | collective-permute-start | bytes 49160 | tf_op jit(solution)/shard_map/ppermute | solution.py:268
  54.0 19.7 %all-to-all-start.1 = ((f32[16,8,4,512]{3,2,1,0:T(4,128)}), f32[16,8,4,512]{3,2,1,0:T(4,128)S(1)}, u32[]{:S(2)}, u32[]{:S(2)}) async-start(f32[16,8,4,512]{3,2,1,0:T(4,128)} %broadcast_in_dim.98), calls=%async_computation.1 | async-start | bytes 2097152 | tf_op jit(solution)/shard_map/all_to_all | solution.py:252
  58.2 128.0 %copy-start.20 = (s32[1,64]{1,0:T(1,128)}, s32[1,64]{1,0:T(1,128)S(1)}, u32[]{:S(2)}) copy-start(s32[1,64]{1,0:T(1,128)S(1)} %get-tuple-element.200) | copy-start | bytes 772
  58.7 4.6 %collective-permute-start.7 = (f32[2,4,1024]{2,1,0:T(4,128)S(1)}, f32[2,4,1024]{2,1,0:T(4,128)S(1)}, u32[]{:S(2)}, u32[]{:S(2)}) collective-permute-start(f32[2,4,1024]{2,1,0:T(4,128)S(1)} %slice.114), channel_id=1, source_target_pairs={{0,2},{1,3},{2,0},{3,1},{4,6},{5,7},{6,4},{7,5},{8,10},{9,11},{10,... | collective-permute-start | bytes 98312 | tf_op jit(solution)/shard_map/ppermute | solution.py:268
  59.6 9.4 %collective-permute-start.6 = (f32[2,4,1024]{2,1,0:T(4,128)S(1)}, f32[2,4,1024]{2,1,0:T(4,128)S(1)}, u32[]{:S(2)}, u32[]{:S(2)}) collective-permute-start(f32[2,4,1024]{2,1,0:T(4,128)S(1)} %slice.114), channel_id=1, source_target_pairs={{0,1},{1,0},{2,3},{3,2},{4,5},{5,4},{6,7},{7,6},{8,9},{9,8},{10,11... | collective-permute-start | bytes 98312 | tf_op jit(solution)/shard_map/ppermute | solution.py:268
  63.3 5.8 %collective-permute-start.8 = (f32[2,4,1024]{2,1,0:T(4,128)S(1)}, f32[2,4,1024]{2,1,0:T(4,128)S(1)}, u32[]{:S(2)}, u32[]{:S(2)}) collective-permute-start(f32[2,4,1024]{2,1,0:T(4,128)S(1)} %collective-permute-done.7), channel_id=1, source_target_pairs={{0,1},{1,0},{2,3},{3,2},{4,5},{5,4},{6,7},{7,6},{8,9},{9,8},{10,11... | collective-permute-start | bytes 98312 | tf_op jit(solution)/shard_map/ppermute | solution.py:268
  65.4 15.8 %collective-permute-start.10 = (f32[64,1024]{1,0:T(8,128)}, f32[64,1024]{1,0:T(8,128)}, u32[]{:S(2)}, u32[]{:S(2)}) collective-permute-start(f32[64,1024]{1,0:T(8,128)} %get-tuple-element.161), channel_id=1, source_target_pairs={{0,3},{1,2},{2,1},{3,0},{4,7},{5,6},{6,5},{7,4},{8,11},{9,10},{10,... | collective-permute-start | bytes 786440 | tf_op jit(solution)/shard_map/ppermute | solution.py:268
  66.0 15.2 %collective-permute-start.11 = (f32[64,1024]{1,0:T(8,128)}, f32[64,1024]{1,0:T(8,128)}, u32[]{:S(2)}, u32[]{:S(2)}) collective-permute-start(f32[64,1024]{1,0:T(8,128)} %get-tuple-element.160), channel_id=1, source_target_pairs={{0,2},{1,3},{2,0},{3,1},{4,6},{5,7},{6,4},{7,5},{8,10},{9,11},{10,... | collective-permute-start | bytes 786440 | tf_op jit(solution)/shard_map/ppermute | solution.py:268
  68.3 12.9 %collective-permute-start.9 = (f32[64,1024]{1,0:T(8,128)S(1)}, f32[64,1024]{1,0:T(8,128)}, u32[]{:S(2)}, u32[]{:S(2)}) collective-permute-start(f32[64,1024]{1,0:T(8,128)S(1)} %get-tuple-element.159), channel_id=1, source_target_pairs={{0,1},{1,0},{2,3},{3,2},{4,5},{5,4},{6,7},{7,6},{8,9},{9,8},{10,11... | collective-permute-start | bytes 786440 | tf_op jit(solution)/shard_map/ppermute | solution.py:268
  75.8 34.4 %all-to-all-start.2 = ((f32[16,9,4,1024]{3,2,1,0:T(4,128)}), f32[16,9,4,1024]{3,2,1,0:T(4,128)}, u32[]{:S(2)}, u32[]{:S(2)}) async-start(f32[16,9,4,1024]{3,2,1,0:T(4,128)} %broadcast_in_dim.99), calls=%async_computation.2 | async-start | bytes 4718592 | tf_op jit(solution)/shard_map/all_to_all | solution.py:252
  80.2 122.8 %all-gather.6.cloned.1.call-start = ((), (), s32[]{:S(2)}) async-start(), calls=%async_computation.7 | async-start | bytes 2228224 | tf_op jit(solution)/shard_map/all_gather | solution.py:352
  108.4 34.2 %collective-permute-start.12 = (f32[2,32,512]{2,1,0:T(8,128)}, f32[2,32,512]{2,1,0:T(8,128)S(1)}, u32[]{:S(2)}, u32[]{:S(2)}) collective-permute-start(f32[2,32,512]{2,1,0:T(8,128)} %bitcast.175), channel_id=1, source_target_pairs={{0,2},{1,3},{2,0},{3,1},{4,6},{5,7},{6,4},{7,5},{8,10},{9,11},{10,... | collective-permute-start | bytes 393224 | tf_op jit(solution)/shard_map/ppermute | solution.py:268
  110.2 32.3 %all-to-all-start.3 = ((bf16[16,64,512]{2,1,0:T(8,128)(2,1)}), bf16[16,64,512]{2,1,0:T(8,128)(2,1)S(1)}, u32[]{:S(2)}, u32[]{:S(2)}) async-start(bf16[16,64,512]{2,1,0:T(8,128)(2,1)} %get-tuple-element.84.u0_ref), calls=%async_computation.3 | async-start | bytes 2097152 | tf_op jit(solution)/shard_map/all_to_all | solution.py:252
  142.5 6.8 %copy-start.18 = (f32[2,32,512]{2,1,0:T(8,128)}, f32[2,32,512]{2,1,0:T(8,128)S(1)}, u32[]{:S(2)}) copy-start(f32[2,32,512]{2,1,0:T(8,128)S(1)} %collective-permute-done.12) | copy-start | bytes 393220
  142.5 9.8 %copy-start = (bf16[16,64,512]{2,1,0:T(8,128)(2,1)}, bf16[16,64,512]{2,1,0:T(8,128)(2,1)S(1)}, u32[]{:S(2)}) copy-start(bf16[16,64,512]{2,1,0:T(8,128)(2,1)S(1)} %all-to-all-done.3) | copy-start | bytes 3145732
  142.5 30.9 %all-to-all-start.4 = ((bf16[16,64,512]{2,1,0:T(8,128)(2,1)}), bf16[16,64,512]{2,1,0:T(8,128)(2,1)S(1)}, u32[]{:S(2)}, u32[]{:S(2)}) async-start(bf16[16,64,512]{2,1,0:T(8,128)(2,1)} %get-tuple-element.87), calls=%async_computation.4 | async-start | bytes 2097152 | tf_op jit(solution)/shard_map/all_to_all | solution.py:252
  152.4 10.9 %copy-start.17 = (f32[64,512]{1,0:T(8,128)S(1)}, f32[64,512]{1,0:T(8,128)}, u32[]{:S(2)}) copy-start(f32[64,512]{1,0:T(8,128)} %get-tuple-element.86) | copy-start | bytes 393220
  152.4 10.9 %copy-start.19 = (f32[2,32,512]{2,1,0:T(8,128)S(1)}, f32[2,32,512]{2,1,0:T(8,128)}, u32[]{:S(2)}) copy-start(f32[2,32,512]{2,1,0:T(8,128)} %copy-done.18) | copy-start | bytes 393220
  152.4 21.0 %collective-permute-start.17 = (f32[2,32,512]{2,1,0:T(8,128)}, f32[2,32,512]{2,1,0:T(8,128)}, u32[]{:S(2)}, u32[]{:S(2)}) collective-permute-start(f32[2,32,512]{2,1,0:T(8,128)} %bitcast.172), channel_id=1, source_target_pairs={{0,2},{1,3},{2,0},{3,1},{4,6},{5,7},{6,4},{7,5},{8,10},{9,11},{10,... | collective-permute-start | bytes 393224 | tf_op jit(solution)/shard_map/ppermute | solution.py:268
  153.6 9.7 %collective-permute-start.13 = (f32[2,32,512]{2,1,0:T(8,128)}, f32[2,32,512]{2,1,0:T(8,128)S(1)}, u32[]{:S(2)}, u32[]{:S(2)}) collective-permute-start(f32[2,32,512]{2,1,0:T(8,128)} %bitcast.176), channel_id=1, source_target_pairs={{0,1},{1,0},{2,3},{3,2},{4,5},{5,4},{6,7},{7,6},{8,9},{9,8},{10,11... | collective-permute-start | bytes 393224 | tf_op jit(solution)/shard_map/ppermute | solution.py:268
  157.9 5.4 %collective-permute-start.14 = (f32[2,32,512]{2,1,0:T(8,128)}, f32[2,32,512]{2,1,0:T(8,128)S(1)}, u32[]{:S(2)}, u32[]{:S(2)}) collective-permute-start(f32[2,32,512]{2,1,0:T(8,128)} %copy-done.18), channel_id=1, source_target_pairs={{0,1},{1,0},{2,3},{3,2},{4,5},{5,4},{6,7},{7,6},{8,9},{9,8},{10,11... | collective-permute-start | bytes 393224 | tf_op jit(solution)/shard_map/ppermute | solution.py:268
  157.9 14.8 %collective-permute-start.15 = (f32[512,128]{0,1:T(8,128)S(1)}, f32[512,128]{0,1:T(8,128)S(1)}, u32[]{:S(2)}, u32[]{:S(2)}) collective-permute-start(f32[512,128]{0,1:T(8,128)S(1)} %get-tuple-element.171), channel_id=1, source_target_pairs={{0,0},{4,8},{8,16},{12,24},{16,32},{20,40},{24,48},{28,56},{32,1},... | collective-permute-start | bytes 786440 | tf_op jit(solution)/shard_map/ppermute | solution.py:374
  159.2 13.5 %collective-permute-start.16 = (f32[512,128]{0,1:T(8,128)S(1)}, f32[512,128]{0,1:T(8,128)S(1)}, u32[]{:S(2)}, u32[]{:S(2)}) collective-permute-start(f32[512,128]{0,1:T(8,128)S(1)} %get-tuple-element.170), channel_id=1, source_target_pairs={{0,4},{4,12},{8,20},{12,28},{16,36},{20,44},{24,52},{28,60},{32,5}... | collective-permute-start | bytes 786440 | tf_op jit(solution)/shard_map/ppermute | solution.py:374
  174.4 50.9 %all-to-all-start.5 = ((f32[16,64,512]{2,1,0:T(8,128)}), f32[16,64,512]{2,1,0:T(8,128)S(1)}, u32[]{:S(2)}, u32[]{:S(2)}) async-start(f32[16,64,512]{2,1,0:T(8,128)} %place.1), calls=%async_computation.5 | async-start | bytes 4194304 | tf_op jit(solution)/shard_map/all_to_all | solution.py:252
  186.1 106.3 %all-gather.4.cloned.1.call-start = ((), (), s32[]{:S(2)}) async-start(), calls=%async_computation.6 | async-start | bytes 4456448 | tf_op jit(solution)/shard_map/all_gather | solution.py:403
  189.4 9.9 %collective-permute-start.19 = (bf16[4,32,1024]{2,1,0:T(8,128)(2,1)}, bf16[4,32,1024]{2,1,0:T(8,128)(2,1)S(1)}, u32[]{:S(2)}, u32[]{:S(2)}) collective-permute-start(bf16[4,32,1024]{2,1,0:T(8,128)(2,1)} %get-tuple-element.98.c0), channel_id=1, source_target_pairs={{0,2},{1,3},{2,0},{3,1},{4,6},{5,7},{6,4},{7,5},{8,10},{9,11},{10,... | collective-permute-start | bytes 786440 | tf_op jit(solution)/shard_map/ppermute | solution.py:268
  189.4 13.7 %collective-permute-start.18 = (bf16[4,32,1024]{2,1,0:T(8,128)(2,1)}, bf16[4,32,1024]{2,1,0:T(8,128)(2,1)S(1)}, u32[]{:S(2)}, u32[]{:S(2)}) collective-permute-start(bf16[4,32,1024]{2,1,0:T(8,128)(2,1)} %get-tuple-element.98.c0), channel_id=1, source_target_pairs={{0,1},{1,0},{2,3},{3,2},{4,5},{5,4},{6,7},{7,6},{8,9},{9,8},{10,11... | collective-permute-start | bytes 786440 | tf_op jit(solution)/shard_map/ppermute | solution.py:268
  199.3 3.8 %copy-start.13 = (bf16[4,32,1024]{2,1,0:T(8,128)(2,1)}, bf16[4,32,1024]{2,1,0:T(8,128)(2,1)S(1)}, u32[]{:S(2)}) copy-start(bf16[4,32,1024]{2,1,0:T(8,128)(2,1)S(1)} %collective-permute-done.19.c2) | copy-start | bytes 786436
  199.3 3.8 %collective-permute-start.20 = (bf16[4,32,1024]{2,1,0:T(8,128)(2,1)S(1)}, bf16[4,32,1024]{2,1,0:T(8,128)(2,1)S(1)}, u32[]{:S(2)}, u32[]{:S(2)}) collective-permute-start(bf16[4,32,1024]{2,1,0:T(8,128)(2,1)S(1)} %collective-permute-done.19.c2), channel_id=1, source_target_pairs={{0,1},{1,0},{2,3},{3,2},{4,5},{5,4},{6,7},{7,6},{8,9},{9,8},{10,11... | collective-permute-start | bytes 786440 | tf_op jit(solution)/shard_map/ppermute | solution.py:268
  199.9 9.8 %collective-permute-start.21 = (bf16[4,32,1024]{2,1,0:T(8,128)(2,1)}, bf16[4,32,1024]{2,1,0:T(8,128)(2,1)}, u32[]{:S(2)}, u32[]{:S(2)}) collective-permute-start(bf16[4,32,1024]{2,1,0:T(8,128)(2,1)} %get-tuple-element.110.c0), channel_id=1, source_target_pairs={{0,2},{1,3},{2,0},{3,1},{4,6},{5,7},{6,4},{7,5},{8,10},{9,11},{10,... | collective-permute-start | bytes 786440 | tf_op jit(solution)/shard_map/ppermute | solution.py:268
  202.4 22.8 %collective-permute-start.26 = (bf16[4,32,1024]{2,1,0:T(8,128)(2,1)}, bf16[4,32,1024]{2,1,0:T(8,128)(2,1)}, u32[]{:S(2)}, u32[]{:S(2)}) collective-permute-start(bf16[4,32,1024]{2,1,0:T(8,128)(2,1)} %get-tuple-element.110.c0), channel_id=1, source_target_pairs={{0,1},{1,0},{2,3},{3,2},{4,5},{5,4},{6,7},{7,6},{8,9},{9,8},{10,11... | collective-permute-start | bytes 786440 | tf_op jit(solution)/shard_map/ppermute | solution.py:268
  207.9 11.3 %copy-start.5 = (f32[512,128]{0,1:T(8,128)S(1)}, f32[512,128]{0,1:T(8,128)}, u32[]{:S(2)}) copy-start(f32[512,128]{0,1:T(8,128)} %add.157) | copy-start | bytes 786436
  210.5 7.5 %collective-permute-start.22 = (f32[32,512]{1,0:T(8,128)S(1)}, f32[32,512]{1,0:T(8,128)S(1)}, u32[]{:S(2)}, u32[]{:S(2)}) collective-permute-start(f32[32,512]{1,0:T(8,128)S(1)} %get-tuple-element.188), channel_id=1, source_target_pairs={{0,1},{1,0},{2,3},{3,2},{4,5},{5,4},{6,7},{7,6},{8,9},{9,8},{10,11... | collective-permute-start | bytes 196616 | tf_op jit(solution)/shard_map/ppermute | solution.py:268
  211.4 6.7 %collective-permute-start.23 = (f32[32,512]{1,0:T(8,128)S(1)}, f32[32,512]{1,0:T(8,128)S(1)}, u32[]{:S(2)}, u32[]{:S(2)}) collective-permute-start(f32[32,512]{1,0:T(8,128)S(1)} %get-tuple-element.190), channel_id=1, source_target_pairs={{0,2},{1,3},{2,0},{3,1},{4,6},{5,7},{6,4},{7,5},{8,10},{9,11},{10,... | collective-permute-start | bytes 196616 | tf_op jit(solution)/shard_map/ppermute | solution.py:268
  212.2 6.0 %collective-permute-start.24 = (f32[32,512]{1,0:T(8,128)S(1)}, f32[32,512]{1,0:T(8,128)S(1)}, u32[]{:S(2)}, u32[]{:S(2)}) collective-permute-start(f32[32,512]{1,0:T(8,128)S(1)} %get-tuple-element.189), channel_id=1, source_target_pairs={{0,3},{1,2},{2,1},{3,0},{4,7},{5,6},{6,5},{7,4},{8,11},{9,10},{10,... | collective-permute-start | bytes 196616 | tf_op jit(solution)/shard_map/ppermute | solution.py:268
  215.6 9.6 %collective-permute-start.25 = (f32[128,512]{1,0:T(8,128)S(1)}, f32[128,512]{1,0:T(8,128)S(1)}, u32[]{:S(2)}, u32[]{:S(2)}) collective-permute-start(f32[128,512]{1,0:T(8,128)S(1)} %fusion.1), channel_id=1, source_target_pairs={{0,64},{64,0},{1,65},{65,1},{2,66},{66,2},{3,67},{67,3},{4,68},{68... | collective-permute-start | bytes 786440 | tf_op jit(solution)/shard_map/ppermute | solution.py:299
  218.0 7.2 %collective-permute-start.27 = (bf16[4,32,1024]{2,1,0:T(8,128)(2,1)}, bf16[4,32,1024]{2,1,0:T(8,128)(2,1)S(1)}, u32[]{:S(2)}, u32[]{:S(2)}) collective-permute-start(bf16[4,32,1024]{2,1,0:T(8,128)(2,1)} %collective-permute-done.21.c2), channel_id=1, source_target_pairs={{0,1},{1,0},{2,3},{3,2},{4,5},{5,4},{6,7},{7,6},{8,9},{9,8},{10,11... | collective-permute-start | bytes 786440 | tf_op jit(solution)/shard_map/ppermute | solution.py:268
  225.2 15.2 %copy-start.12 = (f32[128,512]{1,0:T(8,128)}, f32[128,512]{1,0:T(8,128)S(1)}, u32[]{:S(2)}) copy-start(f32[128,512]{1,0:T(8,128)S(1)} %add.166) | copy-start | bytes 786436
  225.3 7.6 %collective-permute-start.28 = (f32[128,512]{1,0:T(8,128)S(1)}, f32[128,512]{1,0:T(8,128)S(1)}, u32[]{:S(2)}, u32[]{:S(2)}) collective-permute-start(f32[128,512]{1,0:T(8,128)S(1)} %bitcast_add_fusion), channel_id=1, source_target_pairs={{0,64},{64,0},{1,65},{65,1},{2,66},{66,2},{3,67},{67,3},{4,68},{68... | collective-permute-start | bytes 786440 | tf_op jit(solution)/shard_map/ppermute | solution.py:299
  226.3 12.7 %collective-permute-start.29 = (f32[4,32,512]{2,1,0:T(8,128)S(1)}, f32[4,32,512]{2,1,0:T(8,128)S(1)}, u32[]{:S(2)}, u32[]{:S(2)}) collective-permute-start(f32[4,32,512]{2,1,0:T(8,128)S(1)} %bitcast.166), channel_id=1, source_target_pairs={{0,2},{1,3},{2,0},{3,1},{4,6},{5,7},{6,4},{7,5},{8,10},{9,11},{10,... | collective-permute-start | bytes 786440 | tf_op jit(solution)/shard_map/ppermute | solution.py:268
  239.0 12.6 %copy-start.22 = (f32[4,32,512]{2,1,0:T(8,128)}, f32[4,32,512]{2,1,0:T(8,128)S(1)}, u32[]{:S(2)}) copy-start(f32[4,32,512]{2,1,0:T(8,128)S(1)} %collective-permute-done.29.t2) | copy-start | bytes 786436
  240.4 8.2 %collective-permute-start.30 = (f32[4,32,512]{2,1,0:T(8,128)S(1)}, f32[4,32,512]{2,1,0:T(8,128)S(1)}, u32[]{:S(2)}, u32[]{:S(2)}) collective-permute-start(f32[4,32,512]{2,1,0:T(8,128)S(1)} %bitcast.167), channel_id=1, source_target_pairs={{0,1},{1,0},{2,3},{3,2},{4,5},{5,4},{6,7},{7,6},{8,9},{9,8},{10,11... | collective-permute-start | bytes 786440 | tf_op jit(solution)/shard_map/ppermute | solution.py:268
  242.3 5.3 %collective-permute-start.32 = (f32[128,256]{1,0:T(8,128)}, f32[128,256]{1,0:T(8,128)S(1)}, u32[]{:S(2)}, u32[]{:S(2)}) collective-permute-start(f32[128,256]{1,0:T(8,128)} %get-tuple-element.122), channel_id=1, source_target_pairs={{0,64},{64,0},{1,65},{65,1},{2,66},{66,2},{3,67},{67,3},{4,68},{68... | collective-permute-start | bytes 393224 | tf_op jit(solution)/shard_map/ppermute | solution.py:299
  242.3 6.3 %collective-permute-start.31 = (f32[4,32,512]{2,1,0:T(8,128)S(1)}, f32[4,32,512]{2,1,0:T(8,128)S(1)}, u32[]{:S(2)}, u32[]{:S(2)}) collective-permute-start(f32[4,32,512]{2,1,0:T(8,128)S(1)} %collective-permute-done.29.t2), channel_id=1, source_target_pairs={{0,1},{1,0},{2,3},{3,2},{4,5},{5,4},{6,7},{7,6},{8,9},{9,8},{10,11... | collective-permute-start | bytes 786440 | tf_op jit(solution)/shard_map/ppermute | solution.py:268
  248.6 23.9 %collective-permute-start.34 = (f32[4,32,256]{2,1,0:T(8,128)S(1)}, f32[4,32,256]{2,1,0:T(8,128)S(1)}, u32[]{:S(2)}, u32[]{:S(2)}) collective-permute-start(f32[4,32,256]{2,1,0:T(8,128)S(1)} %bitcast.162), channel_id=1, source_target_pairs={{0,2},{1,3},{2,0},{3,1},{4,6},{5,7},{6,4},{7,5},{8,10},{9,11},{10,... | collective-permute-start | bytes 393224 | tf_op jit(solution)/shard_map/ppermute | solution.py:268
  249.9 33.5 %collective-permute-start.38 = (f32[4,32,256]{2,1,0:T(8,128)S(1)}, f32[4,32,256]{2,1,0:T(8,128)S(1)}, u32[]{:S(2)}, u32[]{:S(2)}) collective-permute-start(f32[4,32,256]{2,1,0:T(8,128)S(1)} %bitcast.163), channel_id=1, source_target_pairs={{0,1},{1,0},{2,3},{3,2},{4,5},{5,4},{6,7},{7,6},{8,9},{9,8},{10,11... | collective-permute-start | bytes 393224 | tf_op jit(solution)/shard_map/ppermute | solution.py:268
  251.0 21.5 %collective-permute-start.33 = (f32[768,256]{1,0:T(8,128)}, f32[768,256]{1,0:T(8,128)S(1)}, u32[]{:S(2)}, u32[]{:S(2)}) collective-permute-start(f32[768,256]{1,0:T(8,128)} %get-tuple-element.123), channel_id=1, source_target_pairs={{0,64},{64,0},{1,65},{65,1},{2,66},{66,2},{3,67},{67,3},{4,68},{68... | collective-permute-start | bytes 2359304 | tf_op jit(solution)/shard_map/ppermute | solution.py:299
  272.5 10.9 %collective-permute-start.39 = (f32[4,32,256]{2,1,0:T(8,128)S(1)}, f32[4,32,256]{2,1,0:T(8,128)S(1)}, u32[]{:S(2)}, u32[]{:S(2)}) collective-permute-start(f32[4,32,256]{2,1,0:T(8,128)S(1)} %collective-permute-done.34), channel_id=1, source_target_pairs={{0,1},{1,0},{2,3},{3,2},{4,5},{5,4},{6,7},{7,6},{8,9},{9,8},{10,11... | collective-permute-start | bytes 393224 | tf_op jit(solution)/shard_map/ppermute | solution.py:268
  279.7 24.1 %collective-permute-start.35 = (f32[16,32,256]{2,1,0:T(8,128)S(1)}, f32[16,32,256]{2,1,0:T(8,128)S(1)}, u32[]{:S(2)}, u32[]{:S(2)}) collective-permute-start(f32[16,32,256]{2,1,0:T(8,128)S(1)} %get-tuple-element.151), channel_id=1, source_target_pairs={{0,1},{1,0},{2,3},{3,2},{4,5},{5,4},{6,7},{7,6},{8,9},{9,8},{10,11... | collective-permute-start | bytes 1572872 | tf_op jit(solution)/shard_map/ppermute | solution.py:268
  280.1 23.6 %collective-permute-start.36 = (f32[16,32,256]{2,1,0:T(8,128)S(1)}, f32[16,32,256]{2,1,0:T(8,128)S(1)}, u32[]{:S(2)}, u32[]{:S(2)}) collective-permute-start(f32[16,32,256]{2,1,0:T(8,128)S(1)} %get-tuple-element.150), channel_id=1, source_target_pairs={{0,2},{1,3},{2,0},{3,1},{4,6},{5,7},{6,4},{7,5},{8,10},{9,11},{10,... | collective-permute-start | bytes 1572872 | tf_op jit(solution)/shard_map/ppermute | solution.py:268
  281.9 24.6 %collective-permute-start.37 = (f32[16,32,256]{2,1,0:T(8,128)S(1)}, f32[16,32,256]{2,1,0:T(8,128)S(1)}, u32[]{:S(2)}, u32[]{:S(2)}) collective-permute-start(f32[16,32,256]{2,1,0:T(8,128)S(1)} %get-tuple-element.149), channel_id=1, source_target_pairs={{0,3},{1,2},{2,1},{3,0},{4,7},{5,6},{6,5},{7,4},{8,11},{9,10},{10,... | collective-permute-start | bytes 1572872 | tf_op jit(solution)/shard_map/ppermute | solution.py:268
  284.4 22.2 %copy-start.16 = (f32[64,512]{1,0:T(8,128)S(1)}, f32[64,512]{1,0:T(8,128)}, u32[]{:S(2)}) copy-start(f32[64,512]{1,0:T(8,128)} %get-tuple-element.92) | copy-start | bytes 393220
  303.8 3.3 %copy-start.9 = (f32[16,32,256]{2,1,0:T(8,128)}, f32[16,32,256]{2,1,0:T(8,128)S(1)}, u32[]{:S(2)}) copy-start(f32[16,32,256]{2,1,0:T(8,128)S(1)} %collective-permute-done.35.g1) | copy-start | bytes 1572868
  303.8 3.3 %copy-start.10 = (f32[16,32,256]{2,1,0:T(8,128)}, f32[16,32,256]{2,1,0:T(8,128)S(1)}, u32[]{:S(2)}) copy-start(f32[16,32,256]{2,1,0:T(8,128)S(1)} %collective-permute-done.36.g2) | copy-start | bytes 1572868
  306.5 6.2 %collective-permute-start.41 = (f32[2,32,512]{2,1,0:T(8,128)}, f32[2,32,512]{2,1,0:T(8,128)S(1)}, u32[]{:S(2)}, u32[]{:S(2)}) collective-permute-start(f32[2,32,512]{2,1,0:T(8,128)} %collective-permute-done.17), channel_id=1, source_target_pairs={{0,1},{1,0},{2,3},{3,2},{4,5},{5,4},{6,7},{7,6},{8,9},{9,8},{10,11... | collective-permute-start | bytes 393224 | tf_op jit(solution)/shard_map/ppermute | solution.py:268
  306.6 6.1 %collective-permute-start.40 = (f32[2,32,512]{2,1,0:T(8,128)S(1)}, f32[2,32,512]{2,1,0:T(8,128)S(1)}, u32[]{:S(2)}, u32[]{:S(2)}) collective-permute-start(f32[2,32,512]{2,1,0:T(8,128)S(1)} %bitcast.173), channel_id=1, source_target_pairs={{0,1},{1,0},{2,3},{3,2},{4,5},{5,4},{6,7},{7,6},{8,9},{9,8},{10,11... | collective-permute-start | bytes 393224 | tf_op jit(solution)/shard_map/ppermute | solution.py:268
  307.3 6.4 %copy-start.3 = (f32[4,2,32,512]{3,2,1,0:T(8,128)S(1)}, f32[4,2,32,512]{3,2,1,0:T(8,128)}, u32[]{:S(2)}) copy-start(f32[4,2,32,512]{3,2,1,0:T(8,128)} %pad_maximum_fusion.2) | copy-start | bytes 1572868
  (12 other events, 19.7 us)
Sparse Core Ops, SparseCore 0:
  110.3 55.4 all-gather.5
  239.9 52.3 all-gather.3

commit v4 on v3

--- a/solution.py
+++ b/solution.py
@@ -353,29 +353,30 @@
     d1, u0 = lax.optimization_barrier((d1, u0))
     u0_all = exchange(u0, "row").reshape(32, 32, 512)
 
+    raw_rows = []
+    tile_top = after(root_front[0:512], inv0)
+    for j in range(2):
+        pairs = []
+        for g in range(32):
+            m = 2 * g + j
+            pairs.append((4 * g, (m // 32 * 16 + m % 16) * 4 + m // 16))
+        raw_rows.append(lax.ppermute(tile_top[:, 128 * j:128 * j + 128], ("child", "row", "col"), pairs))
+
     below = (r >= 2).astype(jnp.int32)[None]
     p1, u1 = call(
         second_kernel, (sds((64, 512)), sds((ROWS, 64, 512), BF16)), 1, 4,
         [pltpu.VMEM((512, 512), F32)] * 2 + CHOL, 3 * 10**10, "second")(below, d1, inv0, pack[:, 512:1024], u0)
     factor0 = p0.reshape(2, 32, 512)
-    u1, u0_all, far0 = lax.optimization_barrier((u1, u0_all, across(factor0, 2)))
+    u1, u0_all, far0, raw_rows = lax.optimization_barrier((u1, u0_all, across(factor0, 2), raw_rows))
+    raw_rows = (raw_rows[0] + raw_rows[1]).T
     u1_all = exchange(u1, "row").reshape(32, 32, 512)
     wide = after(jnp.concatenate([y[1], y[2], y[3]], axis=1), u1)
     placed = call(place_kernel, sds((16, 64, 512)), 1, 1, name="place")(bulk_idx, wide)
     factor0 = after(factor0, u1)
     factor0 = in_order(factor0, across(factor0, 1), far0, across(far0, 1), q)
-    raw_rows = 0.0
-    tile_top = after(root_front[0:512], u1)
-    for j in range(2):
-        pairs = []
-        for g in range(32):
-            m = 2 * g + j
-            pairs.append((4 * g, (m // 32 * 16 + m % 16) * 4 + m // 16))
-        raw_rows += lax.ppermute(tile_top[:, 128 * j:128 * j + 128], ("child", "row", "col"), pairs)
     factor1 = p1.reshape(2, 32, 512)
-    u1_all, placed, factor0, raw_rows, far1 = lax.optimization_barrier(
-        (u1_all, placed, factor0, raw_rows, across(after(factor1, u1), 2)))
-    raw_rows = raw_rows.T
+    u1_all, placed, factor0, far1 = lax.optimization_barrier(
+        (u1_all, placed, factor0, across(after(factor1, u1), 2)))
     f_bulk = exchange(placed, "row").reshape(32, 32, 512)
 
     some = sds((4, 32, 1024), BF16)

time: 327 us -> 317 us (0.969)
  waiting for transfers between devices: 66 us -> 49.1 us
  starting transfers between devices: 100 us -> 109 us
    ppermute x33, starting transfers between devices: 49.2 us -> 66.1 us  [across(): return lax.ppermute(x, 'col', [(i, i ^ k) for i in range(4)])]
    ppermute x33, waiting for transfers between devices: 25.6 us -> 14.9 us  [across(): return lax.ppermute(x, 'col', [(i, i ^ k) for i in range(4)])]
    ppermute x2, waiting for transfers between devices: 8.43 us -> 0.01 us  [local(): lax.ppermute(tile_top[:, 128 * j:128 * j + 128], ('child', 'row', 'col'),...]
    all_to_all x6, starting transfers between devices: 40.8 us -> 34.8 us  [exchange(): return lax.all_to_all(x, axis, split_axis=0, concat_axis=0, tiled=True)]
    all_to_all x6, waiting for transfers between devices: 12.6 us -> 16.8 us  [exchange(): return lax.all_to_all(x, axis, split_axis=0, concat_axis=0, tiled=True)]
  transfers between devices with their start and end apart: 50 -> 50, of which waited for: 16 -> 13; matrix products, arithmetic and copies ran while one was open for 7% -> 7% of each run, Pallas kernels for 33% -> 34%
where the time goes in v4:
time: 317 us; the launch traced here: 312 us
  starting transfers between devices  109 us (34%)
  Pallas kernels  105 us (33%)
  waiting for transfers between devices  49.1 us (15%)
  local copies, waits for them, and re-layouts  20.6 us (6%)
  between operations  15 us (5%)
  other arithmetic  12.9 us (4%)
    ppermute x33, starting transfers between devices, across(): return lax.ppermute(x, 'col', [(i, i ^ k) for i in range(4)])  66.1 us
    all_to_all x6, starting transfers between devices, exchange(): return lax.all_to_all(x, axis, split_axis=0, concat_axis=0, tiled=True)  34.8 us
    pallas_call x1, Pallas kernels, local(): call(second_kernel, (sds((64, 512)), sds((ROWS, 64, 512), BF16)), 1, 4, [...  25.5 us
    pallas_call x1, Pallas kernels, local(): call(head_kernel, (sds((512, 512)), sds((64, 512)), sds((ROWS, 64, 512),...  22.2 us
    pallas_call x1, Pallas kernels, local(): call(root_kernel, sds((512, 512)), 1, 4, CHOL, 2 * 10 ** 10, 'root')  21 us
    all_to_all x6, waiting for transfers between devices, exchange(): return lax.all_to_all(x, axis, split_axis=0, concat_axis=0, tiled=True)  16.8 us
    ppermute x33, waiting for transfers between devices, across(): return lax.ppermute(x, 'col', [(i, i ^ k) for i in range(4)])  14.9 us
    pallas_call x1, Pallas kernels, local(): pl.pallas_call(factor_kernel, out_shape=(sds((2048, 512)), sds((2048, 512...  11.4 us
  transfers between devices with their start and end apart: 50, of which 13 were waited for; matrix products, arithmetic and copies ran while one was open for 7% of the time, Pallas kernels for 34%

profile of v4, /device:TPU:1, one launch (start us, length us, event | category | flops | bytes accessed | tf_op | source)
XLA Modules:
  0.0 311.6 jit_solution(13843499355038742887)
XLA Ops:
  7.2 1.2 slice.81
  8.8 1.0 slice_bitcast_fusion.1
  9.7 1.4 collective-permute-start
  11.2 1.4 collective-permute-start.1
  12.6 1.4 collective-permute-start.2
  14.1 1.3 fusion
  16.3 7.4 %all-to-all-start = ((f32[16,4,1536]{2,1,0:T(4,128)}), f32[16,4,1536]{2,1,0:T(4,128)S(1)}, u32[]{:S(2)}, u32[]{:S(2)}) async-start(f32[16,4,1536]{2,1,0:T(4,128)} %reshape.141), calls=%async_computation | async-start | bytes 786432 | tf_op jit(solution)/shard_map/all_to_all | solution.py:252
  23.9 7.9 %all-to-all-done = f32[16,4,1536]{2,1,0:T(4,128)S(1)} async-done(((f32[16,4,1536]{2,1,0:T(4,128)}), f32[16,4,1536]{2,1,0:T(4,128)S(1)}, u32[]{:S(2)}, u32[]{:S(2)}) %all-to-all-start) | async-done | bytes 393248 | tf_op jit(solution)/shard_map/all_to_all | solution.py:252
  32.4 16.5 %collective-permute-start.4 = (f32[2,4,512]{2,1,0:T(4,128)S(1)}, f32[2,4,512]{2,1,0:T(4,128)S(1)}, u32[]{:S(2)}, u32[]{:S(2)}) collective-permute-start(f32[2,4,512]{2,1,0:T(4,128)S(1)} %slice.113), channel_id=1, source_target_pairs={{0,2},{1,3},{2,0},{3,1},{4,6},{5,7},{6,4},{7,5},{8,10},{9,11},{10,... | collective-permute-start | bytes 49160 | tf_op jit(solution)/shard_map/ppermute | solution.py:268
  48.9 1.1 collective-permute-done.4
  50.0 2.4 collective-permute-start.5
  53.4 1.2 broadcast_in_dim.98
  54.6 3.7 %all-to-all-start.1 = ((f32[16,8,4,512]{3,2,1,0:T(4,128)}), f32[16,8,4,512]{3,2,1,0:T(4,128)S(1)}, u32[]{:S(2)}, u32[]{:S(2)}) async-start(f32[16,8,4,512]{3,2,1,0:T(4,128)} %broadcast_in_dim.98), calls=%async_computation.1 | async-start | bytes 2097152 | tf_op jit(solution)/shard_map/all_to_all | solution.py:252
  60.9 2.5 collective-permute-done.7
  63.4 1.2 collective-permute-start.8
  64.6 0.9 dynamic-slice_bitcast_fusion.6
  66.1 2.2 collective-permute-start.11
  69.3 5.2 %all-to-all-done.1.d_ref = f32[16,8,4,512]{3,2,1,0:T(4,128)S(1)} async-done(((f32[16,8,4,512]{3,2,1,0:T(4,128)}), f32[16,8,4,512]{3,2,1,0:T(4,128)S(1)}, u32[]{:S(2)}, u32[]{:S(2)}) %all-to-all-start.1) | async-done | bytes 1048608 | tf_op jit(solution)/shard_map/all_to_all | solution.py:252
  74.5 2.0 broadcast_in_dim.99
  76.5 4.4 %all-to-all-start.2 = ((f32[16,9,4,1024]{3,2,1,0:T(4,128)}), f32[16,9,4,1024]{3,2,1,0:T(4,128)}, u32[]{:S(2)}, u32[]{:S(2)}) async-start(f32[16,9,4,1024]{3,2,1,0:T(4,128)} %broadcast_in_dim.99), calls=%async_computation.2 | async-start | bytes 4718592 | tf_op jit(solution)/shard_map/all_to_all | solution.py:252
  81.2 1.9 fusion.2
  83.8 1.6 place_panel.1
  85.4 22.2 %head.1 = (f32[512,512]{1,0:T(8,128)}, f32[64,512]{1,0:T(8,128)}, bf16[16,64,512]{2,1,0:T(8,128)(2,1)}) custom-call(f32[16,8,4,512]{3,2,1,0:T(4,128)} %copy-done.5, f32[64,512]{1,0:T(8,128)} %get-tuple-element.187.c_ref), custom_call_target="tpu_custom_call" | custom-call | flops 20000000000 | bytes 1048576 | tf_op jit(solution)/shard_map/head/pallas_call | solution.py:350
  107.6 1.3 collective-permute-start.13
  110.5 6.8 %all-to-all-start.3 = ((bf16[16,64,512]{2,1,0:T(8,128)(2,1)}), bf16[16,64,512]{2,1,0:T(8,128)(2,1)S(1)}, u32[]{:S(2)}, u32[]{:S(2)}) async-start(bf16[16,64,512]{2,1,0:T(8,128)(2,1)} %get-tuple-element.85.u0_ref), calls=%async_computation.3 | async-start | bytes 2097152 | tf_op jit(solution)/shard_map/all_to_all | solution.py:252
  117.2 25.5 %second.1 = (f32[64,512]{1,0:T(8,128)}, bf16[16,64,512]{2,1,0:T(8,128)(2,1)}) custom-call(s32[1]{0:T(128)} %bitcast.mask_ref, f32[16,9,4,1024]{3,2,1,0:T(4,128)} %all-to-all-done.2.d_ref, f32[512,512]{1,0:T(8,128)} %get-tuple-element.84.inv0_ref, f32[64,512]{1,0:T(8,128)} %get-tuple-element.186.c_ref, bf16[16,64,512]{2,1,0:T(8,128)(2,1)} %get-tuple-element.85.u0_ref), custom_call_target="tpu_custom_call" | custom-call | flops 30000001024 | bytes 1048576 | tf_op jit(solution)/shard_map/second/pallas_call | solution.py:366
  143.5 6.8 %all-to-all-start.4 = ((bf16[16,64,512]{2,1,0:T(8,128)(2,1)}), bf16[16,64,512]{2,1,0:T(8,128)(2,1)S(1)}, u32[]{:S(2)}, u32[]{:S(2)}) async-start(bf16[16,64,512]{2,1,0:T(8,128)(2,1)} %get-tuple-element.89), calls=%async_computation.4 | async-start | bytes 2097152 | tf_op jit(solution)/shard_map/all_to_all | solution.py:252
  151.0 6.0 %collective-permute-start.15 = (f32[2,32,512]{2,1,0:T(8,128)}, f32[2,32,512]{2,1,0:T(8,128)S(1)}, u32[]{:S(2)}, u32[]{:S(2)}) collective-permute-start(f32[2,32,512]{2,1,0:T(8,128)} %bitcast.176), channel_id=1, source_target_pairs={{0,1},{1,0},{2,3},{3,2},{4,5},{5,4},{6,7},{7,6},{8,9},{9,8},{10,11... | collective-permute-start | bytes 393224 | tf_op jit(solution)/shard_map/ppermute | solution.py:268
  157.0 0.9 pad_maximum_fusion.1.y_ref
  158.0 3.2 %collective-permute-start.17 = (f32[2,32,512]{2,1,0:T(8,128)}, f32[2,32,512]{2,1,0:T(8,128)S(1)}, u32[]{:S(2)}, u32[]{:S(2)}) collective-permute-start(f32[2,32,512]{2,1,0:T(8,128)} %bitcast.172), channel_id=1, source_target_pairs={{0,2},{1,3},{2,0},{3,1},{4,6},{5,7},{6,4},{7,5},{8,10},{9,11},{10,... | collective-permute-start | bytes 393224 | tf_op jit(solution)/shard_map/ppermute | solution.py:268
  161.2 3.4 %place.1 = f32[16,64,512]{2,1,0:T(8,128)} custom-call(s32[64]{0:T(128)} %select_reduce_fusion.bulk_ref, f32[64,3072]{1,0:T(8,128)} %pad_maximum_fusion.1.y_ref), custom_call_target="tpu_custom_call" | custom-call | bytes 1048576 | tf_op jit(solution)/shard_map/place/pallas_call | solution.py:374
  165.6 3.7 %all-to-all-done.4 = bf16[16,64,512]{2,1,0:T(8,128)(2,1)S(1)} async-done(((bf16[16,64,512]{2,1,0:T(8,128)(2,1)}), bf16[16,64,512]{2,1,0:T(8,128)(2,1)S(1)}, u32[]{:S(2)}, u32[]{:S(2)}) %all-to-all-start.4) | async-done | bytes 1048608 | tf_op jit(solution)/shard_map/all_to_all | solution.py:252
  169.3 1.0 copy-done.1
  170.3 5.7 %all-to-all-start.5 = ((f32[16,64,512]{2,1,0:T(8,128)}), f32[16,64,512]{2,1,0:T(8,128)S(1)}, u32[]{:S(2)}, u32[]{:S(2)}) async-start(f32[16,64,512]{2,1,0:T(8,128)} %place.1), calls=%async_computation.5 | async-start | bytes 4194304 | tf_op jit(solution)/shard_map/all_to_all | solution.py:252
  176.8 2.4 select.17
  179.2 2.3 collective-permute-start.19
  181.4 4.7 %collective-permute-start.18 = (bf16[4,32,1024]{2,1,0:T(8,128)(2,1)}, bf16[4,32,1024]{2,1,0:T(8,128)(2,1)S(1)}, u32[]{:S(2)}, u32[]{:S(2)}) collective-permute-start(bf16[4,32,1024]{2,1,0:T(8,128)(2,1)} %get-tuple-element.99.c0), channel_id=1, source_target_pairs={{0,1},{1,0},{2,3},{3,2},{4,5},{5,4},{6,7},{7,6},{8,9},{9,8},{10,11... | collective-permute-start | bytes 786440 | tf_op jit(solution)/shard_map/ppermute | solution.py:268
  186.4 4.7 %collective-permute-start.20 = (bf16[4,32,1024]{2,1,0:T(8,128)(2,1)S(1)}, bf16[4,32,1024]{2,1,0:T(8,128)(2,1)S(1)}, u32[]{:S(2)}, u32[]{:S(2)}) collective-permute-start(bf16[4,32,1024]{2,1,0:T(8,128)(2,1)S(1)} %collective-permute-done.19.c2), channel_id=1, source_target_pairs={{0,1},{1,0},{2,3},{3,2},{4,5},{5,4},{6,7},{7,6},{8,9},{9,8},{10,11... | collective-permute-start | bytes 786440 | tf_op jit(solution)/shard_map/ppermute | solution.py:268
  191.1 2.9 collective-permute-start.21
  193.9 1.6 fusion.12
  198.1 4.0 %panel.1 = (f32[128,512]{1,0:T(8,128)}, f32[128,512]{1,0:T(8,128)}) custom-call(s32[1]{0:T(128)} %bitcast.39.q_ref, s32[4]{0:T(128)} %get-tuple-element.146.rows_ref, s32[4]{0:T(128)} %slice_bitcast_fusion.6.panel_ref, bf16[32,32,512]{2,1,0:T(8,128)(2,1)} %bitcast.148, bf16[32,32,512]{2,1,0:T(8,128)(2,1)} %bitcast.151, f32[32,32,512]{2,1,0:T(8,128)} %bitcast.156, ...), custom_call_target="tpu_custom_call" | custom-call | flops 1000000000 | bytes 1048576 | tf_op jit(solution)/shard_map/panel/pallas_call | solution.py:387
  202.1 1.0 dynamic-slice_bitcast_fusion.9
  203.4 2.1 collective-permute-start.23
  205.5 1.3 collective-permute-start.24
  206.8 1.0 fusion.1
  208.7 2.3 collective-permute-done.24
  212.0 3.8 %collective-permute-done.25 = f32[128,512]{1,0:T(8,128)S(1)} collective-permute-done((f32[128,512]{1,0:T(8,128)S(1)}, f32[128,512]{1,0:T(8,128)S(1)}, u32[]{:S(2)}, u32[]{:S(2)}) %collective-permute-start.25) | collective-permute-done | bytes 262176 | tf_op jit(solution)/shard_map/ppermute | solution.py:299
  216.3 2.4 collective-permute-start.29
  218.7 4.7 %bulk.1 = (f32[768,256]{1,0:T(8,128)}, f32[768,256]{1,0:T(8,128)}, f32[128,256]{1,0:T(8,128)}, f32[128,256]{1,0:T(8,128)}) custom-call(s32[1]{0:T(128)} %bitcast.39.q_ref, s32[4]{0:T(128)} %slice_bitcast_fusion.6.panel_ref, bf16[32,32,512]{2,1,0:T(8,128)(2,1)} %bitcast.149, bf16[32,32,512]{2,1,0:T(8,128)(2,1)} %bitcast.152, f32[32,32,512]{2,1,0:T(8,128)} %bitcast.155, ...), custom_call_target="tpu_custom_call" | custom-call | flops 4000000000 | bytes 1048576 | tf_op jit(solution)/shard_map/bulk/pallas_call | solution.py:399
  223.4 6.3 %collective-permute-done.29.t2 = f32[4,32,512]{2,1,0:T(8,128)S(1)} collective-permute-done((f32[4,32,512]{2,1,0:T(8,128)S(1)}, f32[4,32,512]{2,1,0:T(8,128)S(1)}, u32[]{:S(2)}, u32[]{:S(2)}) %collective-permute-start.29) | collective-permute-done | bytes 262176 | tf_op jit(solution)/shard_map/ppermute | solution.py:268
  231.1 1.9 collective-permute-start.30
  233.2 5.1 %collective-permute-done.32 = f32[128,256]{1,0:T(8,128)S(1)} collective-permute-done((f32[128,256]{1,0:T(8,128)}, f32[128,256]{1,0:T(8,128)S(1)}, u32[]{:S(2)}, u32[]{:S(2)}) %collective-permute-start.32) | collective-permute-done | bytes 131104 | tf_op jit(solution)/shard_map/ppermute | solution.py:299
  238.3 0.9 fusion.3
  239.3 1.3 collective-permute-start.34
  242.3 21.0 %root.1.inv_ref = f32[512,512]{1,0:T(8,128)} custom-call(s32[1]{0:T(128)} %bitcast.39.q_ref, f32[4,32,512]{2,1,0:T(8,128)} %bitcast.168, f32[4,32,512]{2,1,0:T(8,128)} %copy-done.33, f32[4,32,512]{2,1,0:T(8,128)} %copy-done.31, f32[4,32,512]{2,1,0:T(8,128)} %copy-done.34), custom_call_target="tpu_custom_call" | custom-call | flops 20000000000 | bytes 1048576 | tf_op jit(solution)/shard_map/root/pallas_call | solution.py:410
  264.1 3.6 %spread.1 = f32[64,32,256]{2,1,0:T(8,128)} custom-call(s32[64]{0:T(128)} %bitcast.178, s32[64]{0:T(128)} %get-tuple-element.201.theirs_ref, f32[24,32,256]{2,1,0:T(8,128)} %bitcast.160, f32[24,32,256]{2,1,0:T(8,128)} %bitcast.161), custom_call_target="tpu_custom_call" | custom-call | bytes 1048576 | tf_op jit(solution)/shard_map/spread/pallas_call | solution.py:412
  267.8 2.6 dynamic-slice_bitcast_fusion
  270.8 1.8 collective-permute-start.36
  272.6 1.6 collective-permute-start.37
  275.1 8.3 %all-gather.4.cloned.1.call-done.panel_ref = f32[2048,512]{1,0:T(8,128)} async-done(((f32[128,512]{1,0:T(8,128)}), f32[2048,512]{1,0:T(8,128)}) %all-gather.4.cloned.1.call-update) | async-done | bytes 4194320 | tf_op jit(solution)/shard_map/all_gather | solution.py:404
  283.3 11.4 %factor.1 = (f32[2048,512]{1,0:T(8,128)}, bf16[2048,512]{1,0:T(8,128)(2,1)}, bf16[512,256]{1,0:T(8,128)(2,1)}) custom-call(s32[2]{0:T(128)} %add_convert_fusion.flag_ref, f32[2048,512]{1,0:T(8,128)} %all-gather.4.cloned.1.call-done.panel_ref, f32[512,512]{1,0:T(8,128)} %root.1.inv_ref, f32[4,4,32,256]{3,2,1,0:T(8,128)} %pad_maximum_fusion.3.cp_ref), custom_call_target="tpu_custom_call" | custom-call | flops 10000000000 | bytes 1048576 | tf_op jit(solution)/shard_map/factor/pallas_call | solution.py:422
  294.8 2.4 collective-permute-done.37.g3
  298.0 5.4 %last.1 = f32[2048,256]{1,0:T(8,128)} custom-call(s32[1]{0:T(128)} %bitcast.39.q_ref, bf16[2048,512]{1,0:T(8,128)(2,1)} %get-tuple-element.135.u_ref, bf16[512,256]{1,0:T(8,128)(2,1)} %get-tuple-element.140.ug_ref, f32[2048,256]{1,0:T(8,128)} %root_ref.1, f32[16,32,256]{2,1,0:T(8,128)} %get-tuple-element.141.g0, f32[16,32,256]{2,1,0:T(8,128)} %copy-done.8, ...), custom_call_target="tpu_custom_call" | custom-call | tf_op jit(solution)/shard_map/last/pallas_call | solution.py:437
  303.6 1.0 copy.22
  (176 shorter events, 24.6 us)
Async XLA Ops:
  9.7 14.0 %copy-start.30 = (s32[2,24]{1,0:T(2,128)S(1)}, s32[2,24]{1,0:T(2,128)}, u32[]{:S(2)}) copy-start(s32[2,24]{1,0:T(2,128)} %param.5) | copy-start | bytes 580
  9.7 4.4 %collective-permute-start = (f32[64,1536]{1,0:T(8,128)}, f32[64,1536]{1,0:T(8,128)}, u32[]{:S(2)}, u32[]{:S(2)}) collective-permute-start(f32[64,1536]{1,0:T(8,128)} %get-tuple-element.160), channel_id=1, source_target_pairs={{0,1},{4,5},{8,9},{12,13},{16,17},{20,21},{24,25},{28,29},{32,33},... | collective-permute-start | bytes 1179656 | tf_op jit(solution)/shard_map/ppermute | solution.py:281
  11.2 3.0 collective-permute-start.1
  12.6 1.5 collective-permute-start.2
  16.3 15.4 %all-to-all-start = ((f32[16,4,1536]{2,1,0:T(4,128)}), f32[16,4,1536]{2,1,0:T(4,128)S(1)}, u32[]{:S(2)}, u32[]{:S(2)}) async-start(f32[16,4,1536]{2,1,0:T(4,128)} %reshape.141), calls=%async_computation | async-start | bytes 786432 | tf_op jit(solution)/shard_map/all_to_all | solution.py:252
  32.4 17.7 %collective-permute-start.4 = (f32[2,4,512]{2,1,0:T(4,128)S(1)}, f32[2,4,512]{2,1,0:T(4,128)S(1)}, u32[]{:S(2)}, u32[]{:S(2)}) collective-permute-start(f32[2,4,512]{2,1,0:T(4,128)S(1)} %slice.113), channel_id=1, source_target_pairs={{0,2},{1,3},{2,0},{3,1},{4,6},{5,7},{6,4},{7,5},{8,10},{9,11},{10,... | collective-permute-start | bytes 49160 | tf_op jit(solution)/shard_map/ppermute | solution.py:268
  48.9 4.4 %collective-permute-start.3 = (f32[2,4,512]{2,1,0:T(4,128)S(1)}, f32[2,4,512]{2,1,0:T(4,128)S(1)}, u32[]{:S(2)}, u32[]{:S(2)}) collective-permute-start(f32[2,4,512]{2,1,0:T(4,128)S(1)} %slice.113), channel_id=1, source_target_pairs={{0,1},{1,0},{2,3},{3,2},{4,5},{5,4},{6,7},{7,6},{8,9},{9,8},{10,11... | collective-permute-start | bytes 49160 | tf_op jit(solution)/shard_map/ppermute | solution.py:268
  50.0 3.3 %collective-permute-start.5 = (f32[2,4,512]{2,1,0:T(4,128)S(1)}, f32[2,4,512]{2,1,0:T(4,128)S(1)}, u32[]{:S(2)}, u32[]{:S(2)}) collective-permute-start(f32[2,4,512]{2,1,0:T(4,128)S(1)} %collective-permute-done.4), channel_id=1, source_target_pairs={{0,1},{1,0},{2,3},{3,2},{4,5},{5,4},{6,7},{7,6},{8,9},{9,8},{10,11... | collective-permute-start | bytes 49160 | tf_op jit(solution)/shard_map/ppermute | solution.py:268
  54.6 19.9 %all-to-all-start.1 = ((f32[16,8,4,512]{3,2,1,0:T(4,128)}), f32[16,8,4,512]{3,2,1,0:T(4,128)S(1)}, u32[]{:S(2)}, u32[]{:S(2)}) async-start(f32[16,8,4,512]{3,2,1,0:T(4,128)} %broadcast_in_dim.98), calls=%async_computation.1 | async-start | bytes 2097152 | tf_op jit(solution)/shard_map/all_to_all | solution.py:252
  58.8 4.6 %collective-permute-start.7 = (f32[2,4,1024]{2,1,0:T(4,128)S(1)}, f32[2,4,1024]{2,1,0:T(4,128)S(1)}, u32[]{:S(2)}, u32[]{:S(2)}) collective-permute-start(f32[2,4,1024]{2,1,0:T(4,128)S(1)} %copy-done.27), channel_id=1, source_target_pairs={{0,2},{1,3},{2,0},{3,1},{4,6},{5,7},{6,4},{7,5},{8,10},{9,11},{10,... | collective-permute-start | bytes 98312 | tf_op jit(solution)/shard_map/ppermute | solution.py:268
  60.4 8.8 %collective-permute-start.6 = (f32[2,4,1024]{2,1,0:T(4,128)S(1)}, f32[2,4,1024]{2,1,0:T(4,128)S(1)}, u32[]{:S(2)}, u32[]{:S(2)}) collective-permute-start(f32[2,4,1024]{2,1,0:T(4,128)S(1)} %copy-done.27), channel_id=1, source_target_pairs={{0,1},{1,0},{2,3},{3,2},{4,5},{5,4},{6,7},{7,6},{8,9},{9,8},{10,11... | collective-permute-start | bytes 98312 | tf_op jit(solution)/shard_map/ppermute | solution.py:268
  63.4 5.8 %collective-permute-start.8 = (f32[2,4,1024]{2,1,0:T(4,128)S(1)}, f32[2,4,1024]{2,1,0:T(4,128)S(1)}, u32[]{:S(2)}, u32[]{:S(2)}) collective-permute-start(f32[2,4,1024]{2,1,0:T(4,128)S(1)} %collective-permute-done.7), channel_id=1, source_target_pairs={{0,1},{1,0},{2,3},{3,2},{4,5},{5,4},{6,7},{7,6},{8,9},{9,8},{10,11... | collective-permute-start | bytes 98312 | tf_op jit(solution)/shard_map/ppermute | solution.py:268
  65.5 15.7 %collective-permute-start.10 = (f32[64,1024]{1,0:T(8,128)}, f32[64,1024]{1,0:T(8,128)}, u32[]{:S(2)}, u32[]{:S(2)}) collective-permute-start(f32[64,1024]{1,0:T(8,128)} %get-tuple-element.163), channel_id=1, source_target_pairs={{0,3},{1,2},{2,1},{3,0},{4,7},{5,6},{6,5},{7,4},{8,11},{9,10},{10,... | collective-permute-start | bytes 786440 | tf_op jit(solution)/shard_map/ppermute | solution.py:268
  66.1 15.1 %collective-permute-start.11 = (f32[64,1024]{1,0:T(8,128)}, f32[64,1024]{1,0:T(8,128)}, u32[]{:S(2)}, u32[]{:S(2)}) collective-permute-start(f32[64,1024]{1,0:T(8,128)} %get-tuple-element.162), channel_id=1, source_target_pairs={{0,2},{1,3},{2,0},{3,1},{4,6},{5,7},{6,4},{7,5},{8,10},{9,11},{10,... | collective-permute-start | bytes 786440 | tf_op jit(solution)/shard_map/ppermute | solution.py:268
  68.3 12.8 %collective-permute-start.9 = (f32[64,1024]{1,0:T(8,128)}, f32[64,1024]{1,0:T(8,128)}, u32[]{:S(2)}, u32[]{:S(2)}) collective-permute-start(f32[64,1024]{1,0:T(8,128)} %get-tuple-element.161), channel_id=1, source_target_pairs={{0,1},{1,0},{2,3},{3,2},{4,5},{5,4},{6,7},{7,6},{8,9},{9,8},{10,11... | collective-permute-start | bytes 786440 | tf_op jit(solution)/shard_map/ppermute | solution.py:268
  76.5 34.0 %all-to-all-start.2 = ((f32[16,9,4,1024]{3,2,1,0:T(4,128)}), f32[16,9,4,1024]{3,2,1,0:T(4,128)}, u32[]{:S(2)}, u32[]{:S(2)}) async-start(f32[16,9,4,1024]{3,2,1,0:T(4,128)} %broadcast_in_dim.99), calls=%async_computation.2 | async-start | bytes 4718592 | tf_op jit(solution)/shard_map/all_to_all | solution.py:252
  80.9 116.3 %all-gather.6.cloned.1.call-start = ((), (), s32[]{:S(2)}) async-start(), calls=%async_computation.7 | async-start | bytes 2228224 | tf_op jit(solution)/shard_map/all_gather | solution.py:352
  107.6 35.2 %collective-permute-start.13 = (f32[512,128]{0,1:T(8,128)S(1)}, f32[512,128]{0,1:T(8,128)S(1)}, u32[]{:S(2)}, u32[]{:S(2)}) collective-permute-start(f32[512,128]{0,1:T(8,128)S(1)} %get-tuple-element.177), channel_id=1, source_target_pairs={{0,0},{4,8},{8,16},{12,24},{16,32},{20,40},{24,48},{28,56},{32,1},... | collective-permute-start | bytes 786440 | tf_op jit(solution)/shard_map/ppermute | solution.py:363
  108.9 33.9 %collective-permute-start.14 = (f32[512,128]{0,1:T(8,128)S(1)}, f32[512,128]{0,1:T(8,128)S(1)}, u32[]{:S(2)}, u32[]{:S(2)}) collective-permute-start(f32[512,128]{0,1:T(8,128)S(1)} %get-tuple-element.176), channel_id=1, source_target_pairs={{0,4},{4,12},{8,20},{12,28},{16,36},{20,44},{24,52},{28,60},{32,5}... | collective-permute-start | bytes 786440 | tf_op jit(solution)/shard_map/ppermute | solution.py:363
  109.6 33.2 %collective-permute-start.12 = (f32[2,32,512]{2,1,0:T(8,128)}, f32[2,32,512]{2,1,0:T(8,128)S(1)}, u32[]{:S(2)}, u32[]{:S(2)}) collective-permute-start(f32[2,32,512]{2,1,0:T(8,128)} %bitcast.175), channel_id=1, source_target_pairs={{0,2},{1,3},{2,0},{3,1},{4,6},{5,7},{6,4},{7,5},{8,10},{9,11},{10,... | collective-permute-start | bytes 393224 | tf_op jit(solution)/shard_map/ppermute | solution.py:268
  110.5 32.4 %all-to-all-start.3 = ((bf16[16,64,512]{2,1,0:T(8,128)(2,1)}), bf16[16,64,512]{2,1,0:T(8,128)(2,1)S(1)}, u32[]{:S(2)}, u32[]{:S(2)}) async-start(bf16[16,64,512]{2,1,0:T(8,128)(2,1)} %get-tuple-element.85.u0_ref), calls=%async_computation.3 | async-start | bytes 2097152 | tf_op jit(solution)/shard_map/all_to_all | solution.py:252
  142.8 7.5 %copy-start.29 = (s32[1,64]{1,0:T(1,128)S(1)}, s32[1,64]{1,0:T(1,128)}, u32[]{:S(2)}) copy-start(s32[1,64]{1,0:T(1,128)} %get-tuple-element.202) | copy-start | bytes 772
  142.8 14.3 %copy-start.6 = (f32[64,1024]{1,0:T(8,128)S(1)}, f32[64,1024]{1,0:T(8,128)}, u32[]{:S(2)}) copy-start(f32[64,1024]{1,0:T(8,128)} %get-tuple-element.156) | copy-start | bytes 786436
  142.8 21.8 %copy-start.15 = (f32[512,128]{0,1:T(8,128)}, f32[512,128]{0,1:T(8,128)S(1)}, u32[]{:S(2)}) copy-start(f32[512,128]{0,1:T(8,128)S(1)} %collective-permute-done.13) | copy-start | bytes 786436
  142.8 21.7 %copy-start = (bf16[16,64,512]{2,1,0:T(8,128)(2,1)}, bf16[16,64,512]{2,1,0:T(8,128)(2,1)S(1)}, u32[]{:S(2)}) copy-start(bf16[16,64,512]{2,1,0:T(8,128)(2,1)S(1)} %all-to-all-done.3) | copy-start | bytes 3145732
  143.5 25.8 %all-to-all-start.4 = ((bf16[16,64,512]{2,1,0:T(8,128)(2,1)}), bf16[16,64,512]{2,1,0:T(8,128)(2,1)S(1)}, u32[]{:S(2)}, u32[]{:S(2)}) async-start(bf16[16,64,512]{2,1,0:T(8,128)(2,1)} %get-tuple-element.89), calls=%async_computation.4 | async-start | bytes 2097152 | tf_op jit(solution)/shard_map/all_to_all | solution.py:252
  151.0 13.6 %collective-permute-start.15 = (f32[2,32,512]{2,1,0:T(8,128)}, f32[2,32,512]{2,1,0:T(8,128)S(1)}, u32[]{:S(2)}, u32[]{:S(2)}) collective-permute-start(f32[2,32,512]{2,1,0:T(8,128)} %bitcast.176), channel_id=1, source_target_pairs={{0,1},{1,0},{2,3},{3,2},{4,5},{5,4},{6,7},{7,6},{8,9},{9,8},{10,11... | collective-permute-start | bytes 393224 | tf_op jit(solution)/shard_map/ppermute | solution.py:268
  157.0 7.6 %collective-permute-start.16 = (f32[2,32,512]{2,1,0:T(8,128)}, f32[2,32,512]{2,1,0:T(8,128)S(1)}, u32[]{:S(2)}, u32[]{:S(2)}) collective-permute-start(f32[2,32,512]{2,1,0:T(8,128)} %copy-done.25), channel_id=1, source_target_pairs={{0,1},{1,0},{2,3},{3,2},{4,5},{5,4},{6,7},{7,6},{8,9},{9,8},{10,11... | collective-permute-start | bytes 393224 | tf_op jit(solution)/shard_map/ppermute | solution.py:268
  157.0 7.6 %copy-start.24 = (f32[64,512]{1,0:T(8,128)S(1)}, f32[64,512]{1,0:T(8,128)}, u32[]{:S(2)}) copy-start(f32[64,512]{1,0:T(8,128)} %get-tuple-element.87) | copy-start | bytes 393220
  157.0 7.6 %copy-start.26 = (f32[2,32,512]{2,1,0:T(8,128)S(1)}, f32[2,32,512]{2,1,0:T(8,128)}, u32[]{:S(2)}) copy-start(f32[2,32,512]{2,1,0:T(8,128)} %copy-done.25) | copy-start | bytes 393220
  158.0 7.6 %collective-permute-start.17 = (f32[2,32,512]{2,1,0:T(8,128)}, f32[2,32,512]{2,1,0:T(8,128)S(1)}, u32[]{:S(2)}, u32[]{:S(2)}) collective-permute-start(f32[2,32,512]{2,1,0:T(8,128)} %bitcast.172), channel_id=1, source_target_pairs={{0,2},{1,3},{2,0},{3,1},{4,6},{5,7},{6,4},{7,5},{8,10},{9,11},{10,... | collective-permute-start | bytes 393224 | tf_op jit(solution)/shard_map/ppermute | solution.py:268
  170.3 45.7 %all-to-all-start.5 = ((f32[16,64,512]{2,1,0:T(8,128)}), f32[16,64,512]{2,1,0:T(8,128)S(1)}, u32[]{:S(2)}, u32[]{:S(2)}) async-start(f32[16,64,512]{2,1,0:T(8,128)} %place.1), calls=%async_computation.5 | async-start | bytes 4194304 | tf_op jit(solution)/shard_map/all_to_all | solution.py:252
  176.0 107.4 %all-gather.4.cloned.1.call-start = ((), (), s32[]{:S(2)}) async-start(), calls=%async_computation.6 | async-start | bytes 4456448 | tf_op jit(solution)/shard_map/all_gather | solution.py:404
  179.2 7.2 %collective-permute-start.19 = (bf16[4,32,1024]{2,1,0:T(8,128)(2,1)}, bf16[4,32,1024]{2,1,0:T(8,128)(2,1)S(1)}, u32[]{:S(2)}, u32[]{:S(2)}) collective-permute-start(bf16[4,32,1024]{2,1,0:T(8,128)(2,1)} %get-tuple-element.99.c0), channel_id=1, source_target_pairs={{0,2},{1,3},{2,0},{3,1},{4,6},{5,7},{6,4},{7,5},{8,10},{9,11},{10,... | collective-permute-start | bytes 786440 | tf_op jit(solution)/shard_map/ppermute | solution.py:268
  181.4 15.8 %collective-permute-start.18 = (bf16[4,32,1024]{2,1,0:T(8,128)(2,1)}, bf16[4,32,1024]{2,1,0:T(8,128)(2,1)S(1)}, u32[]{:S(2)}, u32[]{:S(2)}) collective-permute-start(bf16[4,32,1024]{2,1,0:T(8,128)(2,1)} %get-tuple-element.99.c0), channel_id=1, source_target_pairs={{0,1},{1,0},{2,3},{3,2},{4,5},{5,4},{6,7},{7,6},{8,9},{9,8},{10,11... | collective-permute-start | bytes 786440 | tf_op jit(solution)/shard_map/ppermute | solution.py:268
  186.4 10.9 %copy-start.12 = (bf16[4,32,1024]{2,1,0:T(8,128)(2,1)}, bf16[4,32,1024]{2,1,0:T(8,128)(2,1)S(1)}, u32[]{:S(2)}) copy-start(bf16[4,32,1024]{2,1,0:T(8,128)(2,1)S(1)} %collective-permute-done.19.c2) | copy-start | bytes 786436
  186.4 10.9 %collective-permute-start.20 = (bf16[4,32,1024]{2,1,0:T(8,128)(2,1)S(1)}, bf16[4,32,1024]{2,1,0:T(8,128)(2,1)S(1)}, u32[]{:S(2)}, u32[]{:S(2)}) collective-permute-start(bf16[4,32,1024]{2,1,0:T(8,128)(2,1)S(1)} %collective-permute-done.19.c2), channel_id=1, source_target_pairs={{0,1},{1,0},{2,3},{3,2},{4,5},{5,4},{6,7},{7,6},{8,9},{9,8},{10,11... | collective-permute-start | bytes 786440 | tf_op jit(solution)/shard_map/ppermute | solution.py:268
  191.1 11.0 %collective-permute-start.21 = (bf16[4,32,1024]{2,1,0:T(8,128)(2,1)}, bf16[4,32,1024]{2,1,0:T(8,128)(2,1)}, u32[]{:S(2)}, u32[]{:S(2)}) collective-permute-start(bf16[4,32,1024]{2,1,0:T(8,128)(2,1)} %get-tuple-element.112.c0), channel_id=1, source_target_pairs={{0,2},{1,3},{2,0},{3,1},{4,6},{5,7},{6,4},{7,5},{8,10},{9,11},{10,... | collective-permute-start | bytes 786440 | tf_op jit(solution)/shard_map/ppermute | solution.py:268
  196.5 19.4 %collective-permute-start.26 = (bf16[4,32,1024]{2,1,0:T(8,128)(2,1)}, bf16[4,32,1024]{2,1,0:T(8,128)(2,1)}, u32[]{:S(2)}, u32[]{:S(2)}) collective-permute-start(bf16[4,32,1024]{2,1,0:T(8,128)(2,1)} %get-tuple-element.112.c0), channel_id=1, source_target_pairs={{0,1},{1,0},{2,3},{3,2},{4,5},{5,4},{6,7},{7,6},{8,9},{9,8},{10,11... | collective-permute-start | bytes 786440 | tf_op jit(solution)/shard_map/ppermute | solution.py:268
  202.1 9.9 %copy-start.16 = (f32[512,128]{0,1:T(8,128)S(1)}, f32[512,128]{0,1:T(8,128)}, u32[]{:S(2)}) copy-start(f32[512,128]{0,1:T(8,128)} %copy-done.15) | copy-start | bytes 786436
  202.1 9.9 %copy-start.18 = (f32[512,128]{0,1:T(8,128)S(1)}, f32[512,128]{0,1:T(8,128)}, u32[]{:S(2)}) copy-start(f32[512,128]{0,1:T(8,128)} %copy-done.17) | copy-start | bytes 786436
  203.1 5.2 %collective-permute-start.22 = (f32[32,512]{1,0:T(8,128)S(1)}, f32[32,512]{1,0:T(8,128)S(1)}, u32[]{:S(2)}, u32[]{:S(2)}) collective-permute-start(f32[32,512]{1,0:T(8,128)S(1)} %get-tuple-element.190), channel_id=1, source_target_pairs={{0,1},{1,0},{2,3},{3,2},{4,5},{5,4},{6,7},{7,6},{8,9},{9,8},{10,11... | collective-permute-start | bytes 196616 | tf_op jit(solution)/shard_map/ppermute | solution.py:268
  203.4 5.4 %collective-permute-start.23 = (f32[32,512]{1,0:T(8,128)S(1)}, f32[32,512]{1,0:T(8,128)S(1)}, u32[]{:S(2)}, u32[]{:S(2)}) collective-permute-start(f32[32,512]{1,0:T(8,128)S(1)} %get-tuple-element.192), channel_id=1, source_target_pairs={{0,2},{1,3},{2,0},{3,1},{4,6},{5,7},{6,4},{7,5},{8,10},{9,11},{10,... | collective-permute-start | bytes 196616 | tf_op jit(solution)/shard_map/ppermute | solution.py:268
  205.5 5.6 %collective-permute-start.24 = (f32[32,512]{1,0:T(8,128)S(1)}, f32[32,512]{1,0:T(8,128)S(1)}, u32[]{:S(2)}, u32[]{:S(2)}) collective-permute-start(f32[32,512]{1,0:T(8,128)S(1)} %get-tuple-element.191), channel_id=1, source_target_pairs={{0,3},{1,2},{2,1},{3,0},{4,7},{5,6},{6,5},{7,4},{8,11},{9,10},{10,... | collective-permute-start | bytes 196616 | tf_op jit(solution)/shard_map/ppermute | solution.py:268
  207.8 8.1 %collective-permute-start.25 = (f32[128,512]{1,0:T(8,128)S(1)}, f32[128,512]{1,0:T(8,128)S(1)}, u32[]{:S(2)}, u32[]{:S(2)}) collective-permute-start(f32[128,512]{1,0:T(8,128)S(1)} %fusion.1), channel_id=1, source_target_pairs={{0,64},{64,0},{1,65},{65,1},{2,66},{66,2},{3,67},{67,3},{4,68},{68... | collective-permute-start | bytes 786440 | tf_op jit(solution)/shard_map/ppermute | solution.py:299
  208.3 7.6 %collective-permute-start.27 = (bf16[4,32,1024]{2,1,0:T(8,128)(2,1)}, bf16[4,32,1024]{2,1,0:T(8,128)(2,1)S(1)}, u32[]{:S(2)}, u32[]{:S(2)}) collective-permute-start(bf16[4,32,1024]{2,1,0:T(8,128)(2,1)} %collective-permute-done.21.c2), channel_id=1, source_target_pairs={{0,1},{1,0},{2,3},{3,2},{4,5},{5,4},{6,7},{7,6},{8,9},{9,8},{10,11... | collective-permute-start | bytes 786440 | tf_op jit(solution)/shard_map/ppermute | solution.py:268
  215.9 15.2 %copy-start.11 = (f32[128,512]{1,0:T(8,128)}, f32[128,512]{1,0:T(8,128)S(1)}, u32[]{:S(2)}) copy-start(f32[128,512]{1,0:T(8,128)S(1)} %add.166) | copy-start | bytes 786436
  216.0 7.4 %collective-permute-start.28 = (f32[128,512]{1,0:T(8,128)S(1)}, f32[128,512]{1,0:T(8,128)S(1)}, u32[]{:S(2)}, u32[]{:S(2)}) collective-permute-start(f32[128,512]{1,0:T(8,128)S(1)} %bitcast_add_fusion), channel_id=1, source_target_pairs={{0,64},{64,0},{1,65},{65,1},{2,66},{66,2},{3,67},{67,3},{4,68},{68... | collective-permute-start | bytes 786440 | tf_op jit(solution)/shard_map/ppermute | solution.py:299
  216.3 13.4 %collective-permute-start.29 = (f32[4,32,512]{2,1,0:T(8,128)S(1)}, f32[4,32,512]{2,1,0:T(8,128)S(1)}, u32[]{:S(2)}, u32[]{:S(2)}) collective-permute-start(f32[4,32,512]{2,1,0:T(8,128)S(1)} %bitcast.166), channel_id=1, source_target_pairs={{0,2},{1,3},{2,0},{3,1},{4,6},{5,7},{6,4},{7,5},{8,10},{9,11},{10,... | collective-permute-start | bytes 786440 | tf_op jit(solution)/shard_map/ppermute | solution.py:268
  229.7 12.6 %copy-start.31 = (f32[4,32,512]{2,1,0:T(8,128)}, f32[4,32,512]{2,1,0:T(8,128)S(1)}, u32[]{:S(2)}) copy-start(f32[4,32,512]{2,1,0:T(8,128)S(1)} %collective-permute-done.29.t2) | copy-start | bytes 786436
  231.1 8.2 %collective-permute-start.30 = (f32[4,32,512]{2,1,0:T(8,128)S(1)}, f32[4,32,512]{2,1,0:T(8,128)S(1)}, u32[]{:S(2)}, u32[]{:S(2)}) collective-permute-start(f32[4,32,512]{2,1,0:T(8,128)S(1)} %bitcast.167), channel_id=1, source_target_pairs={{0,1},{1,0},{2,3},{3,2},{4,5},{5,4},{6,7},{7,6},{8,9},{9,8},{10,11... | collective-permute-start | bytes 786440 | tf_op jit(solution)/shard_map/ppermute | solution.py:268
  233.0 5.3 %collective-permute-start.32 = (f32[128,256]{1,0:T(8,128)}, f32[128,256]{1,0:T(8,128)S(1)}, u32[]{:S(2)}, u32[]{:S(2)}) collective-permute-start(f32[128,256]{1,0:T(8,128)} %get-tuple-element.124), channel_id=1, source_target_pairs={{0,64},{64,0},{1,65},{65,1},{2,66},{66,2},{3,67},{67,3},{4,68},{68... | collective-permute-start | bytes 393224 | tf_op jit(solution)/shard_map/ppermute | solution.py:299
  233.0 6.3 %collective-permute-start.31 = (f32[4,32,512]{2,1,0:T(8,128)S(1)}, f32[4,32,512]{2,1,0:T(8,128)S(1)}, u32[]{:S(2)}, u32[]{:S(2)}) collective-permute-start(f32[4,32,512]{2,1,0:T(8,128)S(1)} %collective-permute-done.29.t2), channel_id=1, source_target_pairs={{0,1},{1,0},{2,3},{3,2},{4,5},{5,4},{6,7},{7,6},{8,9},{9,8},{10,11... | collective-permute-start | bytes 786440 | tf_op jit(solution)/shard_map/ppermute | solution.py:268
  239.3 24.0 %collective-permute-start.34 = (f32[4,32,256]{2,1,0:T(8,128)S(1)}, f32[4,32,256]{2,1,0:T(8,128)S(1)}, u32[]{:S(2)}, u32[]{:S(2)}) collective-permute-start(f32[4,32,256]{2,1,0:T(8,128)S(1)} %bitcast.162), channel_id=1, source_target_pairs={{0,2},{1,3},{2,0},{3,1},{4,6},{5,7},{6,4},{7,5},{8,10},{9,11},{10,... | collective-permute-start | bytes 393224 | tf_op jit(solution)/shard_map/ppermute | solution.py:268
  240.5 33.7 %collective-permute-start.38 = (f32[4,32,256]{2,1,0:T(8,128)S(1)}, f32[4,32,256]{2,1,0:T(8,128)S(1)}, u32[]{:S(2)}, u32[]{:S(2)}) collective-permute-start(f32[4,32,256]{2,1,0:T(8,128)S(1)} %bitcast.163), channel_id=1, source_target_pairs={{0,1},{1,0},{2,3},{3,2},{4,5},{5,4},{6,7},{7,6},{8,9},{9,8},{10,11... | collective-permute-start | bytes 393224 | tf_op jit(solution)/shard_map/ppermute | solution.py:268
  241.4 21.9 %collective-permute-start.33 = (f32[768,256]{1,0:T(8,128)}, f32[768,256]{1,0:T(8,128)S(1)}, u32[]{:S(2)}, u32[]{:S(2)}) collective-permute-start(f32[768,256]{1,0:T(8,128)} %get-tuple-element.125), channel_id=1, source_target_pairs={{0,64},{64,0},{1,65},{65,1},{2,66},{66,2},{3,67},{67,3},{4,68},{68... | collective-permute-start | bytes 2359304 | tf_op jit(solution)/shard_map/ppermute | solution.py:299
  263.3 10.9 %collective-permute-start.39 = (f32[4,32,256]{2,1,0:T(8,128)S(1)}, f32[4,32,256]{2,1,0:T(8,128)S(1)}, u32[]{:S(2)}, u32[]{:S(2)}) collective-permute-start(f32[4,32,256]{2,1,0:T(8,128)S(1)} %collective-permute-done.34), channel_id=1, source_target_pairs={{0,1},{1,0},{2,3},{3,2},{4,5},{5,4},{6,7},{7,6},{8,9},{9,8},{10,11... | collective-permute-start | bytes 393224 | tf_op jit(solution)/shard_map/ppermute | solution.py:268
  270.4 24.3 %collective-permute-start.35 = (f32[16,32,256]{2,1,0:T(8,128)S(1)}, f32[16,32,256]{2,1,0:T(8,128)S(1)}, u32[]{:S(2)}, u32[]{:S(2)}) collective-permute-start(f32[16,32,256]{2,1,0:T(8,128)S(1)} %get-tuple-element.153), channel_id=1, source_target_pairs={{0,1},{1,0},{2,3},{3,2},{4,5},{5,4},{6,7},{7,6},{8,9},{9,8},{10,11... | collective-permute-start | bytes 1572872 | tf_op jit(solution)/shard_map/ppermute | solution.py:268
  270.8 24.0 %collective-permute-start.36 = (f32[16,32,256]{2,1,0:T(8,128)S(1)}, f32[16,32,256]{2,1,0:T(8,128)S(1)}, u32[]{:S(2)}, u32[]{:S(2)}) collective-permute-start(f32[16,32,256]{2,1,0:T(8,128)S(1)} %get-tuple-element.152), channel_id=1, source_target_pairs={{0,2},{1,3},{2,0},{3,1},{4,6},{5,7},{6,4},{7,5},{8,10},{9,11},{10,... | collective-permute-start | bytes 1572872 | tf_op jit(solution)/shard_map/ppermute | solution.py:268
  272.6 24.5 %collective-permute-start.37 = (f32[16,32,256]{2,1,0:T(8,128)S(1)}, f32[16,32,256]{2,1,0:T(8,128)S(1)}, u32[]{:S(2)}, u32[]{:S(2)}) collective-permute-start(f32[16,32,256]{2,1,0:T(8,128)S(1)} %get-tuple-element.151), channel_id=1, source_target_pairs={{0,3},{1,2},{2,1},{3,0},{4,7},{5,6},{6,5},{7,4},{8,11},{9,10},{10,... | collective-permute-start | bytes 1572872 | tf_op jit(solution)/shard_map/ppermute | solution.py:268
  275.1 22.1 %copy-start.22 = (f32[2,32,512]{2,1,0:T(8,128)S(1)}, f32[2,32,512]{2,1,0:T(8,128)}, u32[]{:S(2)}) copy-start(f32[2,32,512]{2,1,0:T(8,128)} %copy-done.21) | copy-start | bytes 393220
  275.1 22.1 %copy-start.19 = (f32[64,512]{1,0:T(8,128)S(1)}, f32[64,512]{1,0:T(8,128)}, u32[]{:S(2)}) copy-start(f32[64,512]{1,0:T(8,128)} %get-tuple-element.93) | copy-start | bytes 393220
  297.2 6.2 %collective-permute-start.41 = (f32[2,32,512]{2,1,0:T(8,128)S(1)}, f32[2,32,512]{2,1,0:T(8,128)S(1)}, u32[]{:S(2)}, u32[]{:S(2)}) collective-permute-start(f32[2,32,512]{2,1,0:T(8,128)S(1)} %copy-done.22), channel_id=1, source_target_pairs={{0,1},{1,0},{2,3},{3,2},{4,5},{5,4},{6,7},{7,6},{8,9},{9,8},{10,11... | collective-permute-start | bytes 393224 | tf_op jit(solution)/shard_map/ppermute | solution.py:268
  297.2 6.2 %collective-permute-start.40 = (f32[2,32,512]{2,1,0:T(8,128)S(1)}, f32[2,32,512]{2,1,0:T(8,128)S(1)}, u32[]{:S(2)}, u32[]{:S(2)}) collective-permute-start(f32[2,32,512]{2,1,0:T(8,128)S(1)} %bitcast.173), channel_id=1, source_target_pairs={{0,1},{1,0},{2,3},{3,2},{4,5},{5,4},{6,7},{7,6},{8,9},{9,8},{10,11... | collective-permute-start | bytes 393224 | tf_op jit(solution)/shard_map/ppermute | solution.py:268
  (21 other events, 56.8 us)
Sparse Core Ops, SparseCore 0:
  110.6 60.3 all-gather.5
  230.6 52.7 all-gather.3

commit v5 on v4

--- a/solution.py
+++ b/solution.py
@@ -404,11 +404,12 @@
     panel = lax.all_gather(z, "row", tiled=True)
 
     t_all = [t, across(t, 1), t_far, across(t_far, 1)]
-    head_cols = (top + first + swap_child(sent)).reshape(4, 32, 256)
-    t_all, z, other, head_cols = lax.optimization_barrier((t_all, z, other, head_cols))
+    sent = swap_child(sent)
+    t_all, z, other = lax.optimization_barrier((t_all, z, other))
+    inv_root = call(root_kernel, sds((512, 512)), 1, 4, CHOL, 2 * 10**10, "root")(at, *t_all)
+    got, inv_root, sent = lax.optimization_barrier((swap_child(other), inv_root, sent))
+    head_cols = (top + first + sent).reshape(4, 32, 256)
     head_far = across(head_cols, 2)
-    inv_root = call(root_kernel, sds((512, 512)), 1, 4, CHOL, 2 * 10**10, "root")(at, *t_all)
-    got, inv_root, head_far = lax.optimization_barrier((swap_child(other), inv_root, head_far))
     spread = call(spread_kernel, sds((64, 32, 256)), 2, 2, name="spread")(
         mine, theirs, own.reshape(24, 32, 256), got.reshape(24, 32, 256))
     arrived = sent_col(spread.reshape(4, 16, 32, 256), q)

time: 317 us -> 315 us (level)
    ppermute x4, waiting for transfers between devices: 8.96 us -> 3.84 us  [swap_child(): return lax.ppermute(x, 'child', [(0, 1), (1, 0)])]
    all_gather x1, waiting for transfers between devices: 8.25 us -> 12.1 us  [local(): panel = lax.all_gather(z, 'row', tiled=True)]
where the time goes in v5:
time: 315 us; the launch traced here: 310 us
  starting transfers between devices  109 us (35%)
  Pallas kernels  105 us (33%)
  waiting for transfers between devices  46.7 us (15%)
  local copies, waits for them, and re-layouts  20.4 us (6%)
  between operations  15 us (5%)
  other arithmetic  12.9 us (4%)
    ppermute x33, starting transfers between devices, across(): return lax.ppermute(x, 'col', [(i, i ^ k) for i in range(4)])  67.5 us
    all_to_all x6, starting transfers between devices, exchange(): return lax.all_to_all(x, axis, split_axis=0, concat_axis=0, tiled=True)  34.4 us
    pallas_call x1, Pallas kernels, local(): call(second_kernel, (sds((64, 512)), sds((ROWS, 64, 512), BF16)), 1, 4, [...  25.5 us
    pallas_call x1, Pallas kernels, local(): call(head_kernel, (sds((512, 512)), sds((64, 512)), sds((ROWS, 64, 512),...  22.2 us
    pallas_call x1, Pallas kernels, local(): call(root_kernel, sds((512, 512)), 1, 4, CHOL, 2 * 10 ** 10, 'root')  20.9 us
    all_to_all x6, waiting for transfers between devices, exchange(): return lax.all_to_all(x, axis, split_axis=0, concat_axis=0, tiled=True)  17.1 us
    ppermute x33, waiting for transfers between devices, across(): return lax.ppermute(x, 'col', [(i, i ^ k) for i in range(4)])  13.5 us
    all_gather x1, waiting for transfers between devices, local(): panel = lax.all_gather(z, 'row', tiled=True)  12.1 us
  transfers between devices with their start and end apart: 50, of which 13 were waited for; matrix products, arithmetic and copies ran while one was open for 7% of the time, Pallas kernels for 34%

profile of v5, /device:TPU:1, one launch (start us, length us, event | category | flops | bytes accessed | tf_op | source)
XLA Modules:
  0.0 309.6 jit_solution(15548853695410668688)
XLA Ops:
  7.2 1.2 slice.81
  8.8 1.0 slice_bitcast_fusion.1
  9.7 1.4 collective-permute-start
  11.2 1.4 collective-permute-start.1
  12.6 1.4 collective-permute-start.2
  14.1 1.3 fusion
  16.3 7.4 %all-to-all-start = ((f32[16,4,1536]{2,1,0:T(4,128)}), f32[16,4,1536]{2,1,0:T(4,128)S(1)}, u32[]{:S(2)}, u32[]{:S(2)}) async-start(f32[16,4,1536]{2,1,0:T(4,128)} %reshape.141), calls=%async_computation | async-start | bytes 786432 | tf_op jit(solution)/shard_map/all_to_all | solution.py:252
  23.9 7.9 %all-to-all-done = f32[16,4,1536]{2,1,0:T(4,128)S(1)} async-done(((f32[16,4,1536]{2,1,0:T(4,128)}), f32[16,4,1536]{2,1,0:T(4,128)S(1)}, u32[]{:S(2)}, u32[]{:S(2)}) %all-to-all-start) | async-done | bytes 393248 | tf_op jit(solution)/shard_map/all_to_all | solution.py:252
  32.4 16.6 %collective-permute-start.4 = (f32[2,4,512]{2,1,0:T(4,128)S(1)}, f32[2,4,512]{2,1,0:T(4,128)S(1)}, u32[]{:S(2)}, u32[]{:S(2)}) collective-permute-start(f32[2,4,512]{2,1,0:T(4,128)S(1)} %slice.113), channel_id=1, source_target_pairs={{0,2},{1,3},{2,0},{3,1},{4,6},{5,7},{6,4},{7,5},{8,10},{9,11},{10,... | collective-permute-start | bytes 49160 | tf_op jit(solution)/shard_map/ppermute | solution.py:268
  48.9 1.1 collective-permute-done.4
  50.0 2.4 collective-permute-start.5
  53.4 1.2 broadcast_in_dim.98
  54.5 3.7 %all-to-all-start.1 = ((f32[16,8,4,512]{3,2,1,0:T(4,128)}), f32[16,8,4,512]{3,2,1,0:T(4,128)S(1)}, u32[]{:S(2)}, u32[]{:S(2)}) async-start(f32[16,8,4,512]{3,2,1,0:T(4,128)} %broadcast_in_dim.98), calls=%async_computation.1 | async-start | bytes 2097152 | tf_op jit(solution)/shard_map/all_to_all | solution.py:252
  60.8 2.2 collective-permute-done.7
  63.0 1.5 collective-permute-start.8
  66.1 2.2 collective-permute-start.11
  69.2 5.2 %all-to-all-done.1.d_ref = f32[16,8,4,512]{3,2,1,0:T(4,128)S(1)} async-done(((f32[16,8,4,512]{3,2,1,0:T(4,128)}), f32[16,8,4,512]{3,2,1,0:T(4,128)S(1)}, u32[]{:S(2)}, u32[]{:S(2)}) %all-to-all-start.1) | async-done | bytes 1048608 | tf_op jit(solution)/shard_map/all_to_all | solution.py:252
  74.4 2.0 broadcast_in_dim.99
  76.4 4.4 %all-to-all-start.2 = ((f32[16,9,4,1024]{3,2,1,0:T(4,128)}), f32[16,9,4,1024]{3,2,1,0:T(4,128)}, u32[]{:S(2)}, u32[]{:S(2)}) async-start(f32[16,9,4,1024]{3,2,1,0:T(4,128)} %broadcast_in_dim.99), calls=%async_computation.2 | async-start | bytes 4718592 | tf_op jit(solution)/shard_map/all_to_all | solution.py:252
  81.1 1.9 fusion.2
  83.7 1.6 place_panel.1
  85.3 22.2 %head.1 = (f32[512,512]{1,0:T(8,128)}, f32[64,512]{1,0:T(8,128)}, bf16[16,64,512]{2,1,0:T(8,128)(2,1)}) custom-call(f32[16,8,4,512]{3,2,1,0:T(4,128)} %copy-done.5, f32[64,512]{1,0:T(8,128)} %get-tuple-element.185.c_ref), custom_call_target="tpu_custom_call" | custom-call | flops 20000000000 | bytes 1048576 | tf_op jit(solution)/shard_map/head/pallas_call | solution.py:350
  107.5 1.3 collective-permute-start.13
  109.5 1.1 collective-permute-start.12
  110.6 6.8 %all-to-all-start.3 = ((bf16[16,64,512]{2,1,0:T(8,128)(2,1)}), bf16[16,64,512]{2,1,0:T(8,128)(2,1)S(1)}, u32[]{:S(2)}, u32[]{:S(2)}) async-start(bf16[16,64,512]{2,1,0:T(8,128)(2,1)} %get-tuple-element.84.u0_ref), calls=%async_computation.3 | async-start | bytes 2097152 | tf_op jit(solution)/shard_map/all_to_all | solution.py:252
  117.4 25.5 %second.1 = (f32[64,512]{1,0:T(8,128)}, bf16[16,64,512]{2,1,0:T(8,128)(2,1)}) custom-call(s32[1]{0:T(128)} %bitcast.mask_ref, f32[16,9,4,1024]{3,2,1,0:T(4,128)} %all-to-all-done.2.d_ref, f32[512,512]{1,0:T(8,128)} %get-tuple-element.83.inv0_ref, f32[64,512]{1,0:T(8,128)} %get-tuple-element.184.c_ref, bf16[16,64,512]{2,1,0:T(8,128)(2,1)} %get-tuple-element.84.u0_ref), custom_call_target="tpu_custom_call" | custom-call | flops 30000001024 | bytes 1048576 | tf_op jit(solution)/shard_map/second/pallas_call | solution.py:366
  143.7 6.7 %all-to-all-start.4 = ((bf16[16,64,512]{2,1,0:T(8,128)(2,1)}), bf16[16,64,512]{2,1,0:T(8,128)(2,1)S(1)}, u32[]{:S(2)}, u32[]{:S(2)}) async-start(bf16[16,64,512]{2,1,0:T(8,128)(2,1)} %get-tuple-element.88), calls=%async_computation.4 | async-start | bytes 2097152 | tf_op jit(solution)/shard_map/all_to_all | solution.py:252
  151.2 5.9 %collective-permute-start.15 = (f32[2,32,512]{2,1,0:T(8,128)}, f32[2,32,512]{2,1,0:T(8,128)S(1)}, u32[]{:S(2)}, u32[]{:S(2)}) collective-permute-start(f32[2,32,512]{2,1,0:T(8,128)} %bitcast.176), channel_id=1, source_target_pairs={{0,1},{1,0},{2,3},{3,2},{4,5},{5,4},{6,7},{7,6},{8,9},{9,8},{10,11... | collective-permute-start | bytes 393224 | tf_op jit(solution)/shard_map/ppermute | solution.py:268
  157.1 0.9 pad_maximum_fusion.1.y_ref
  158.1 3.2 %collective-permute-start.17 = (f32[2,32,512]{2,1,0:T(8,128)}, f32[2,32,512]{2,1,0:T(8,128)S(1)}, u32[]{:S(2)}, u32[]{:S(2)}) collective-permute-start(f32[2,32,512]{2,1,0:T(8,128)} %bitcast.172), channel_id=1, source_target_pairs={{0,2},{1,3},{2,0},{3,1},{4,6},{5,7},{6,4},{7,5},{8,10},{9,11},{10,... | collective-permute-start | bytes 393224 | tf_op jit(solution)/shard_map/ppermute | solution.py:268
  161.3 3.4 %place.1 = f32[16,64,512]{2,1,0:T(8,128)} custom-call(s32[64]{0:T(128)} %select_reduce_fusion.bulk_ref, f32[64,3072]{1,0:T(8,128)} %pad_maximum_fusion.1.y_ref), custom_call_target="tpu_custom_call" | custom-call | bytes 1048576 | tf_op jit(solution)/shard_map/place/pallas_call | solution.py:374
  165.6 4.0 %all-to-all-done.4 = bf16[16,64,512]{2,1,0:T(8,128)(2,1)S(1)} async-done(((bf16[16,64,512]{2,1,0:T(8,128)(2,1)}), bf16[16,64,512]{2,1,0:T(8,128)(2,1)S(1)}, u32[]{:S(2)}, u32[]{:S(2)}) %all-to-all-start.4) | async-done | bytes 1048608 | tf_op jit(solution)/shard_map/all_to_all | solution.py:252
  169.7 1.0 copy-done.1
  170.6 5.3 %all-to-all-start.5 = ((f32[16,64,512]{2,1,0:T(8,128)}), f32[16,64,512]{2,1,0:T(8,128)S(1)}, u32[]{:S(2)}, u32[]{:S(2)}) async-start(f32[16,64,512]{2,1,0:T(8,128)} %place.1), calls=%async_computation.5 | async-start | bytes 4194304 | tf_op jit(solution)/shard_map/all_to_all | solution.py:252
  176.8 2.4 select.17
  179.2 2.2 collective-permute-start.19
  181.4 4.7 %collective-permute-start.18 = (bf16[4,32,1024]{2,1,0:T(8,128)(2,1)}, bf16[4,32,1024]{2,1,0:T(8,128)(2,1)S(1)}, u32[]{:S(2)}, u32[]{:S(2)}) collective-permute-start(bf16[4,32,1024]{2,1,0:T(8,128)(2,1)} %get-tuple-element.98.c0), channel_id=1, source_target_pairs={{0,1},{1,0},{2,3},{3,2},{4,5},{5,4},{6,7},{7,6},{8,9},{9,8},{10,11... | collective-permute-start | bytes 786440 | tf_op jit(solution)/shard_map/ppermute | solution.py:268
  186.4 4.7 %collective-permute-start.20 = (bf16[4,32,1024]{2,1,0:T(8,128)(2,1)S(1)}, bf16[4,32,1024]{2,1,0:T(8,128)(2,1)S(1)}, u32[]{:S(2)}, u32[]{:S(2)}) collective-permute-start(bf16[4,32,1024]{2,1,0:T(8,128)(2,1)S(1)} %collective-permute-done.19.c2), channel_id=1, source_target_pairs={{0,1},{1,0},{2,3},{3,2},{4,5},{5,4},{6,7},{7,6},{8,9},{9,8},{10,11... | collective-permute-start | bytes 786440 | tf_op jit(solution)/shard_map/ppermute | solution.py:268
  191.1 2.9 collective-permute-start.21
  194.0 1.6 fusion.12
  198.1 4.0 %panel.1 = (f32[128,512]{1,0:T(8,128)}, f32[128,512]{1,0:T(8,128)}) custom-call(s32[1]{0:T(128)} %bitcast.39.q_ref, s32[4]{0:T(128)} %get-tuple-element.144.rows_ref, s32[4]{0:T(128)} %slice_bitcast_fusion.6.panel_ref, bf16[32,32,512]{2,1,0:T(8,128)(2,1)} %bitcast.148, bf16[32,32,512]{2,1,0:T(8,128)(2,1)} %bitcast.151, f32[32,32,512]{2,1,0:T(8,128)} %bitcast.156, ...), custom_call_target="tpu_custom_call" | custom-call | flops 1000000000 | bytes 1048576 | tf_op jit(solution)/shard_map/panel/pallas_call | solution.py:387
  202.1 1.0 dynamic-slice_bitcast_fusion.9
  203.4 2.1 collective-permute-start.23
  205.5 1.3 collective-permute-start.24
  206.8 1.0 fusion.1
  208.8 2.3 collective-permute-done.24
  212.1 3.8 %collective-permute-done.25 = f32[128,512]{1,0:T(8,128)S(1)} collective-permute-done((f32[128,512]{1,0:T(8,128)S(1)}, f32[128,512]{1,0:T(8,128)S(1)}, u32[]{:S(2)}, u32[]{:S(2)}) %collective-permute-start.25) | collective-permute-done | bytes 262176 | tf_op jit(solution)/shard_map/ppermute | solution.py:299
  216.3 2.4 collective-permute-start.29
  218.7 4.7 %bulk.1 = (f32[768,256]{1,0:T(8,128)}, f32[768,256]{1,0:T(8,128)}, f32[128,256]{1,0:T(8,128)}, f32[128,256]{1,0:T(8,128)}) custom-call(s32[1]{0:T(128)} %bitcast.39.q_ref, s32[4]{0:T(128)} %slice_bitcast_fusion.6.panel_ref, bf16[32,32,512]{2,1,0:T(8,128)(2,1)} %bitcast.149, bf16[32,32,512]{2,1,0:T(8,128)(2,1)} %bitcast.152, f32[32,32,512]{2,1,0:T(8,128)} %bitcast.155, ...), custom_call_target="tpu_custom_call" | custom-call | flops 4000000000 | bytes 1048576 | tf_op jit(solution)/shard_map/bulk/pallas_call | solution.py:399
  223.4 6.2 %collective-permute-done.29.t2 = f32[4,32,512]{2,1,0:T(8,128)S(1)} collective-permute-done((f32[4,32,512]{2,1,0:T(8,128)S(1)}, f32[4,32,512]{2,1,0:T(8,128)S(1)}, u32[]{:S(2)}, u32[]{:S(2)}) %collective-permute-start.29) | collective-permute-done | bytes 262176 | tf_op jit(solution)/shard_map/ppermute | solution.py:268
  230.5 2.0 collective-permute-start.30
  232.6 1.0 collective-permute-done.30.t1
  234.7 20.9 %root.1.inv_ref = f32[512,512]{1,0:T(8,128)} custom-call(s32[1]{0:T(128)} %bitcast.39.q_ref, f32[4,32,512]{2,1,0:T(8,128)} %bitcast.168, f32[4,32,512]{2,1,0:T(8,128)} %copy-done.35, f32[4,32,512]{2,1,0:T(8,128)} %copy-done.34, f32[4,32,512]{2,1,0:T(8,128)} %copy-done.36), custom_call_target="tpu_custom_call" | custom-call | flops 20000000000 | bytes 1048576 | tf_op jit(solution)/shard_map/root/pallas_call | solution.py:409
  255.6 1.8 collective-permute-start.38
  258.1 0.9 collective-permute-start.37
  259.0 3.6 %spread.1 = f32[64,32,256]{2,1,0:T(8,128)} custom-call(s32[64]{0:T(128)} %bitcast.178, s32[64]{0:T(128)} %get-tuple-element.199.theirs_ref, f32[24,32,256]{2,1,0:T(8,128)} %bitcast.160, f32[24,32,256]{2,1,0:T(8,128)} %bitcast.161), custom_call_target="tpu_custom_call" | custom-call | bytes 1048576 | tf_op jit(solution)/shard_map/spread/pallas_call | solution.py:413
  263.1 2.5 dynamic-slice_bitcast_fusion
  266.1 1.7 collective-permute-start.35
  267.7 1.7 collective-permute-start.36
  269.5 1.0 select_bitcast_fusion.7
  271.3 12.1 %all-gather.4.cloned.1.call-done.panel_ref = f32[2048,512]{1,0:T(8,128)} async-done(((f32[128,512]{1,0:T(8,128)}), f32[2048,512]{1,0:T(8,128)}) %all-gather.4.cloned.1.call-update) | async-done | bytes 4194320 | tf_op jit(solution)/shard_map/all_gather | solution.py:404
  283.3 11.4 %factor.1 = (f32[2048,512]{1,0:T(8,128)}, bf16[2048,512]{1,0:T(8,128)(2,1)}, bf16[512,256]{1,0:T(8,128)(2,1)}) custom-call(s32[2]{0:T(128)} %add_convert_fusion.flag_ref, f32[2048,512]{1,0:T(8,128)} %all-gather.4.cloned.1.call-done.panel_ref, f32[512,512]{1,0:T(8,128)} %root.1.inv_ref, f32[4,4,32,256]{3,2,1,0:T(8,128)} %pad_maximum_fusion.3.cp_ref), custom_call_target="tpu_custom_call" | custom-call | flops 10000000000 | bytes 1048576 | tf_op jit(solution)/shard_map/factor/pallas_call | solution.py:423
  295.9 5.4 %last.1 = f32[2048,256]{1,0:T(8,128)} custom-call(s32[1]{0:T(128)} %bitcast.39.q_ref, bf16[2048,512]{1,0:T(8,128)(2,1)} %get-tuple-element.133.u_ref, bf16[512,256]{1,0:T(8,128)(2,1)} %get-tuple-element.138.ug_ref, f32[2048,256]{1,0:T(8,128)} %root_ref.1, f32[16,32,256]{2,1,0:T(8,128)} %get-tuple-element.139.g0, f32[16,32,256]{2,1,0:T(8,128)} %copy-done.8, ...), custom_call_target="tpu_custom_call" | custom-call | tf_op jit(solution)/shard_map/last/pallas_call | solution.py:438
  301.5 1.0 copy.22
  (180 shorter events, 23.9 us)
Async XLA Ops:
  9.7 14.0 %copy-start.32 = (s32[2,24]{1,0:T(2,128)S(1)}, s32[2,24]{1,0:T(2,128)}, u32[]{:S(2)}) copy-start(s32[2,24]{1,0:T(2,128)} %param.5) | copy-start | bytes 580
  9.7 4.4 %collective-permute-start = (f32[64,1536]{1,0:T(8,128)}, f32[64,1536]{1,0:T(8,128)}, u32[]{:S(2)}, u32[]{:S(2)}) collective-permute-start(f32[64,1536]{1,0:T(8,128)} %get-tuple-element.158), channel_id=1, source_target_pairs={{0,1},{4,5},{8,9},{12,13},{16,17},{20,21},{24,25},{28,29},{32,33},... | collective-permute-start | bytes 1179656 | tf_op jit(solution)/shard_map/ppermute | solution.py:281
  11.2 3.0 collective-permute-start.1
  12.6 1.6 collective-permute-start.2
  16.3 15.4 %all-to-all-start = ((f32[16,4,1536]{2,1,0:T(4,128)}), f32[16,4,1536]{2,1,0:T(4,128)S(1)}, u32[]{:S(2)}, u32[]{:S(2)}) async-start(f32[16,4,1536]{2,1,0:T(4,128)} %reshape.141), calls=%async_computation | async-start | bytes 786432 | tf_op jit(solution)/shard_map/all_to_all | solution.py:252
  32.4 17.7 %collective-permute-start.4 = (f32[2,4,512]{2,1,0:T(4,128)S(1)}, f32[2,4,512]{2,1,0:T(4,128)S(1)}, u32[]{:S(2)}, u32[]{:S(2)}) collective-permute-start(f32[2,4,512]{2,1,0:T(4,128)S(1)} %slice.113), channel_id=1, source_target_pairs={{0,2},{1,3},{2,0},{3,1},{4,6},{5,7},{6,4},{7,5},{8,10},{9,11},{10,... | collective-permute-start | bytes 49160 | tf_op jit(solution)/shard_map/ppermute | solution.py:268
  48.9 4.4 %collective-permute-start.3 = (f32[2,4,512]{2,1,0:T(4,128)S(1)}, f32[2,4,512]{2,1,0:T(4,128)S(1)}, u32[]{:S(2)}, u32[]{:S(2)}) collective-permute-start(f32[2,4,512]{2,1,0:T(4,128)S(1)} %slice.113), channel_id=1, source_target_pairs={{0,1},{1,0},{2,3},{3,2},{4,5},{5,4},{6,7},{7,6},{8,9},{9,8},{10,11... | collective-permute-start | bytes 49160 | tf_op jit(solution)/shard_map/ppermute | solution.py:268
  50.0 3.3 %collective-permute-start.5 = (f32[2,4,512]{2,1,0:T(4,128)S(1)}, f32[2,4,512]{2,1,0:T(4,128)S(1)}, u32[]{:S(2)}, u32[]{:S(2)}) collective-permute-start(f32[2,4,512]{2,1,0:T(4,128)S(1)} %collective-permute-done.4), channel_id=1, source_target_pairs={{0,1},{1,0},{2,3},{3,2},{4,5},{5,4},{6,7},{7,6},{8,9},{9,8},{10,11... | collective-permute-start | bytes 49160 | tf_op jit(solution)/shard_map/ppermute | solution.py:268
  54.5 19.9 %all-to-all-start.1 = ((f32[16,8,4,512]{3,2,1,0:T(4,128)}), f32[16,8,4,512]{3,2,1,0:T(4,128)S(1)}, u32[]{:S(2)}, u32[]{:S(2)}) async-start(f32[16,8,4,512]{3,2,1,0:T(4,128)} %broadcast_in_dim.98), calls=%async_computation.1 | async-start | bytes 2097152 | tf_op jit(solution)/shard_map/all_to_all | solution.py:252
  58.7 4.3 %collective-permute-start.7 = (f32[2,4,1024]{2,1,0:T(4,128)S(1)}, f32[2,4,1024]{2,1,0:T(4,128)S(1)}, u32[]{:S(2)}, u32[]{:S(2)}) collective-permute-start(f32[2,4,1024]{2,1,0:T(4,128)S(1)} %copy-done.29), channel_id=1, source_target_pairs={{0,2},{1,3},{2,0},{3,1},{4,6},{5,7},{6,4},{7,5},{8,10},{9,11},{10,... | collective-permute-start | bytes 98312 | tf_op jit(solution)/shard_map/ppermute | solution.py:268
  60.3 8.8 %collective-permute-start.6 = (f32[2,4,1024]{2,1,0:T(4,128)S(1)}, f32[2,4,1024]{2,1,0:T(4,128)S(1)}, u32[]{:S(2)}, u32[]{:S(2)}) collective-permute-start(f32[2,4,1024]{2,1,0:T(4,128)S(1)} %copy-done.29), channel_id=1, source_target_pairs={{0,1},{1,0},{2,3},{3,2},{4,5},{5,4},{6,7},{7,6},{8,9},{9,8},{10,11... | collective-permute-start | bytes 98312 | tf_op jit(solution)/shard_map/ppermute | solution.py:268
  63.0 6.1 %collective-permute-start.8 = (f32[2,4,1024]{2,1,0:T(4,128)S(1)}, f32[2,4,1024]{2,1,0:T(4,128)S(1)}, u32[]{:S(2)}, u32[]{:S(2)}) collective-permute-start(f32[2,4,1024]{2,1,0:T(4,128)S(1)} %collective-permute-done.7), channel_id=1, source_target_pairs={{0,1},{1,0},{2,3},{3,2},{4,5},{5,4},{6,7},{7,6},{8,9},{9,8},{10,11... | collective-permute-start | bytes 98312 | tf_op jit(solution)/shard_map/ppermute | solution.py:268
  65.4 15.7 %collective-permute-start.10 = (f32[64,1024]{1,0:T(8,128)}, f32[64,1024]{1,0:T(8,128)}, u32[]{:S(2)}, u32[]{:S(2)}) collective-permute-start(f32[64,1024]{1,0:T(8,128)} %get-tuple-element.161), channel_id=1, source_target_pairs={{0,3},{1,2},{2,1},{3,0},{4,7},{5,6},{6,5},{7,4},{8,11},{9,10},{10,... | collective-permute-start | bytes 786440 | tf_op jit(solution)/shard_map/ppermute | solution.py:268
  66.1 15.1 %collective-permute-start.11 = (f32[64,1024]{1,0:T(8,128)}, f32[64,1024]{1,0:T(8,128)}, u32[]{:S(2)}, u32[]{:S(2)}) collective-permute-start(f32[64,1024]{1,0:T(8,128)} %get-tuple-element.160), channel_id=1, source_target_pairs={{0,2},{1,3},{2,0},{3,1},{4,6},{5,7},{6,4},{7,5},{8,10},{9,11},{10,... | collective-permute-start | bytes 786440 | tf_op jit(solution)/shard_map/ppermute | solution.py:268
  68.3 12.8 %collective-permute-start.9 = (f32[64,1024]{1,0:T(8,128)}, f32[64,1024]{1,0:T(8,128)}, u32[]{:S(2)}, u32[]{:S(2)}) collective-permute-start(f32[64,1024]{1,0:T(8,128)} %get-tuple-element.159), channel_id=1, source_target_pairs={{0,1},{1,0},{2,3},{3,2},{4,5},{5,4},{6,7},{7,6},{8,9},{9,8},{10,11... | collective-permute-start | bytes 786440 | tf_op jit(solution)/shard_map/ppermute | solution.py:268
  76.4 34.2 %all-to-all-start.2 = ((f32[16,9,4,1024]{3,2,1,0:T(4,128)}), f32[16,9,4,1024]{3,2,1,0:T(4,128)}, u32[]{:S(2)}, u32[]{:S(2)}) async-start(f32[16,9,4,1024]{3,2,1,0:T(4,128)} %broadcast_in_dim.99), calls=%async_computation.2 | async-start | bytes 4718592 | tf_op jit(solution)/shard_map/all_to_all | solution.py:252
  80.9 116.4 %all-gather.6.cloned.1.call-start = ((), (), s32[]{:S(2)}) async-start(), calls=%async_computation.7 | async-start | bytes 2228224 | tf_op jit(solution)/shard_map/all_gather | solution.py:352
  107.5 35.4 %collective-permute-start.13 = (f32[512,128]{0,1:T(8,128)S(1)}, f32[512,128]{0,1:T(8,128)S(1)}, u32[]{:S(2)}, u32[]{:S(2)}) collective-permute-start(f32[512,128]{0,1:T(8,128)S(1)} %get-tuple-element.175), channel_id=1, source_target_pairs={{0,0},{4,8},{8,16},{12,24},{16,32},{20,40},{24,48},{28,56},{32,1},... | collective-permute-start | bytes 786440 | tf_op jit(solution)/shard_map/ppermute | solution.py:363
  108.8 34.1 %collective-permute-start.14 = (f32[512,128]{0,1:T(8,128)S(1)}, f32[512,128]{0,1:T(8,128)S(1)}, u32[]{:S(2)}, u32[]{:S(2)}) collective-permute-start(f32[512,128]{0,1:T(8,128)S(1)} %get-tuple-element.174), channel_id=1, source_target_pairs={{0,4},{4,12},{8,20},{12,28},{16,36},{20,44},{24,52},{28,60},{32,5}... | collective-permute-start | bytes 786440 | tf_op jit(solution)/shard_map/ppermute | solution.py:363
  109.5 33.4 %collective-permute-start.12 = (f32[2,32,512]{2,1,0:T(8,128)}, f32[2,32,512]{2,1,0:T(8,128)S(1)}, u32[]{:S(2)}, u32[]{:S(2)}) collective-permute-start(f32[2,32,512]{2,1,0:T(8,128)} %bitcast.175), channel_id=1, source_target_pairs={{0,2},{1,3},{2,0},{3,1},{4,6},{5,7},{6,4},{7,5},{8,10},{9,11},{10,... | collective-permute-start | bytes 393224 | tf_op jit(solution)/shard_map/ppermute | solution.py:268
  110.6 32.4 %all-to-all-start.3 = ((bf16[16,64,512]{2,1,0:T(8,128)(2,1)}), bf16[16,64,512]{2,1,0:T(8,128)(2,1)S(1)}, u32[]{:S(2)}, u32[]{:S(2)}) async-start(bf16[16,64,512]{2,1,0:T(8,128)(2,1)} %get-tuple-element.84.u0_ref), calls=%async_computation.3 | async-start | bytes 2097152 | tf_op jit(solution)/shard_map/all_to_all | solution.py:252
  142.9 7.5 %copy-start.31 = (s32[1,64]{1,0:T(1,128)S(1)}, s32[1,64]{1,0:T(1,128)}, u32[]{:S(2)}) copy-start(s32[1,64]{1,0:T(1,128)} %get-tuple-element.200) | copy-start | bytes 772
  142.9 14.2 %copy-start.6 = (f32[64,1024]{1,0:T(8,128)S(1)}, f32[64,1024]{1,0:T(8,128)}, u32[]{:S(2)}) copy-start(f32[64,1024]{1,0:T(8,128)} %get-tuple-element.154) | copy-start | bytes 786436
  142.9 21.7 %copy-start.15 = (f32[512,128]{0,1:T(8,128)}, f32[512,128]{0,1:T(8,128)S(1)}, u32[]{:S(2)}) copy-start(f32[512,128]{0,1:T(8,128)S(1)} %collective-permute-done.13) | copy-start | bytes 786436
  143.0 21.7 %copy-start = (bf16[16,64,512]{2,1,0:T(8,128)(2,1)}, bf16[16,64,512]{2,1,0:T(8,128)(2,1)S(1)}, u32[]{:S(2)}) copy-start(bf16[16,64,512]{2,1,0:T(8,128)(2,1)S(1)} %all-to-all-done.3) | copy-start | bytes 3145732
  143.7 26.0 %all-to-all-start.4 = ((bf16[16,64,512]{2,1,0:T(8,128)(2,1)}), bf16[16,64,512]{2,1,0:T(8,128)(2,1)S(1)}, u32[]{:S(2)}, u32[]{:S(2)}) async-start(bf16[16,64,512]{2,1,0:T(8,128)(2,1)} %get-tuple-element.88), calls=%async_computation.4 | async-start | bytes 2097152 | tf_op jit(solution)/shard_map/all_to_all | solution.py:252
  151.2 13.5 %collective-permute-start.15 = (f32[2,32,512]{2,1,0:T(8,128)}, f32[2,32,512]{2,1,0:T(8,128)S(1)}, u32[]{:S(2)}, u32[]{:S(2)}) collective-permute-start(f32[2,32,512]{2,1,0:T(8,128)} %bitcast.176), channel_id=1, source_target_pairs={{0,1},{1,0},{2,3},{3,2},{4,5},{5,4},{6,7},{7,6},{8,9},{9,8},{10,11... | collective-permute-start | bytes 393224 | tf_op jit(solution)/shard_map/ppermute | solution.py:268
  157.1 7.6 %collective-permute-start.16 = (f32[2,32,512]{2,1,0:T(8,128)}, f32[2,32,512]{2,1,0:T(8,128)S(1)}, u32[]{:S(2)}, u32[]{:S(2)}) collective-permute-start(f32[2,32,512]{2,1,0:T(8,128)} %copy-done.25), channel_id=1, source_target_pairs={{0,1},{1,0},{2,3},{3,2},{4,5},{5,4},{6,7},{7,6},{8,9},{9,8},{10,11... | collective-permute-start | bytes 393224 | tf_op jit(solution)/shard_map/ppermute | solution.py:268
  157.1 7.6 %copy-start.24 = (f32[64,512]{1,0:T(8,128)S(1)}, f32[64,512]{1,0:T(8,128)}, u32[]{:S(2)}) copy-start(f32[64,512]{1,0:T(8,128)} %get-tuple-element.86) | copy-start | bytes 393220
  157.1 7.6 %copy-start.26 = (f32[2,32,512]{2,1,0:T(8,128)S(1)}, f32[2,32,512]{2,1,0:T(8,128)}, u32[]{:S(2)}) copy-start(f32[2,32,512]{2,1,0:T(8,128)} %copy-done.25) | copy-start | bytes 393220
  158.1 7.6 %collective-permute-start.17 = (f32[2,32,512]{2,1,0:T(8,128)}, f32[2,32,512]{2,1,0:T(8,128)S(1)}, u32[]{:S(2)}, u32[]{:S(2)}) collective-permute-start(f32[2,32,512]{2,1,0:T(8,128)} %bitcast.172), channel_id=1, source_target_pairs={{0,2},{1,3},{2,0},{3,1},{4,6},{5,7},{6,4},{7,5},{8,10},{9,11},{10,... | collective-permute-start | bytes 393224 | tf_op jit(solution)/shard_map/ppermute | solution.py:268
  170.6 45.4 %all-to-all-start.5 = ((f32[16,64,512]{2,1,0:T(8,128)}), f32[16,64,512]{2,1,0:T(8,128)S(1)}, u32[]{:S(2)}, u32[]{:S(2)}) async-start(f32[16,64,512]{2,1,0:T(8,128)} %place.1), calls=%async_computation.5 | async-start | bytes 4194304 | tf_op jit(solution)/shard_map/all_to_all | solution.py:252
  176.0 107.4 %all-gather.4.cloned.1.call-start = ((), (), s32[]{:S(2)}) async-start(), calls=%async_computation.6 | async-start | bytes 4456448 | tf_op jit(solution)/shard_map/all_gather | solution.py:404
  179.2 7.2 %collective-permute-start.19 = (bf16[4,32,1024]{2,1,0:T(8,128)(2,1)}, bf16[4,32,1024]{2,1,0:T(8,128)(2,1)S(1)}, u32[]{:S(2)}, u32[]{:S(2)}) collective-permute-start(bf16[4,32,1024]{2,1,0:T(8,128)(2,1)} %get-tuple-element.98.c0), channel_id=1, source_target_pairs={{0,2},{1,3},{2,0},{3,1},{4,6},{5,7},{6,4},{7,5},{8,10},{9,11},{10,... | collective-permute-start | bytes 786440 | tf_op jit(solution)/shard_map/ppermute | solution.py:268
  181.4 15.8 %collective-permute-start.18 = (bf16[4,32,1024]{2,1,0:T(8,128)(2,1)}, bf16[4,32,1024]{2,1,0:T(8,128)(2,1)S(1)}, u32[]{:S(2)}, u32[]{:S(2)}) collective-permute-start(bf16[4,32,1024]{2,1,0:T(8,128)(2,1)} %get-tuple-element.98.c0), channel_id=1, source_target_pairs={{0,1},{1,0},{2,3},{3,2},{4,5},{5,4},{6,7},{7,6},{8,9},{9,8},{10,11... | collective-permute-start | bytes 786440 | tf_op jit(solution)/shard_map/ppermute | solution.py:268
  186.4 10.9 %copy-start.12 = (bf16[4,32,1024]{2,1,0:T(8,128)(2,1)}, bf16[4,32,1024]{2,1,0:T(8,128)(2,1)S(1)}, u32[]{:S(2)}) copy-start(bf16[4,32,1024]{2,1,0:T(8,128)(2,1)S(1)} %collective-permute-done.19.c2) | copy-start | bytes 786436
  186.4 10.8 %collective-permute-start.20 = (bf16[4,32,1024]{2,1,0:T(8,128)(2,1)S(1)}, bf16[4,32,1024]{2,1,0:T(8,128)(2,1)S(1)}, u32[]{:S(2)}, u32[]{:S(2)}) collective-permute-start(bf16[4,32,1024]{2,1,0:T(8,128)(2,1)S(1)} %collective-permute-done.19.c2), channel_id=1, source_target_pairs={{0,1},{1,0},{2,3},{3,2},{4,5},{5,4},{6,7},{7,6},{8,9},{9,8},{10,11... | collective-permute-start | bytes 786440 | tf_op jit(solution)/shard_map/ppermute | solution.py:268
  191.1 11.0 %collective-permute-start.21 = (bf16[4,32,1024]{2,1,0:T(8,128)(2,1)}, bf16[4,32,1024]{2,1,0:T(8,128)(2,1)}, u32[]{:S(2)}, u32[]{:S(2)}) collective-permute-start(bf16[4,32,1024]{2,1,0:T(8,128)(2,1)} %get-tuple-element.111.c0), channel_id=1, source_target_pairs={{0,2},{1,3},{2,0},{3,1},{4,6},{5,7},{6,4},{7,5},{8,10},{9,11},{10,... | collective-permute-start | bytes 786440 | tf_op jit(solution)/shard_map/ppermute | solution.py:268
  196.5 19.5 %collective-permute-start.26 = (bf16[4,32,1024]{2,1,0:T(8,128)(2,1)}, bf16[4,32,1024]{2,1,0:T(8,128)(2,1)}, u32[]{:S(2)}, u32[]{:S(2)}) collective-permute-start(bf16[4,32,1024]{2,1,0:T(8,128)(2,1)} %get-tuple-element.111.c0), channel_id=1, source_target_pairs={{0,1},{1,0},{2,3},{3,2},{4,5},{5,4},{6,7},{7,6},{8,9},{9,8},{10,11... | collective-permute-start | bytes 786440 | tf_op jit(solution)/shard_map/ppermute | solution.py:268
  202.1 9.9 %copy-start.16 = (f32[512,128]{0,1:T(8,128)S(1)}, f32[512,128]{0,1:T(8,128)}, u32[]{:S(2)}) copy-start(f32[512,128]{0,1:T(8,128)} %copy-done.15) | copy-start | bytes 786436
  202.1 9.9 %copy-start.18 = (f32[512,128]{0,1:T(8,128)S(1)}, f32[512,128]{0,1:T(8,128)}, u32[]{:S(2)}) copy-start(f32[512,128]{0,1:T(8,128)} %copy-done.17) | copy-start | bytes 786436
  203.1 5.2 %collective-permute-start.22 = (f32[32,512]{1,0:T(8,128)S(1)}, f32[32,512]{1,0:T(8,128)S(1)}, u32[]{:S(2)}, u32[]{:S(2)}) collective-permute-start(f32[32,512]{1,0:T(8,128)S(1)} %get-tuple-element.188), channel_id=1, source_target_pairs={{0,1},{1,0},{2,3},{3,2},{4,5},{5,4},{6,7},{7,6},{8,9},{9,8},{10,11... | collective-permute-start | bytes 196616 | tf_op jit(solution)/shard_map/ppermute | solution.py:268
  203.4 5.4 %collective-permute-start.23 = (f32[32,512]{1,0:T(8,128)S(1)}, f32[32,512]{1,0:T(8,128)S(1)}, u32[]{:S(2)}, u32[]{:S(2)}) collective-permute-start(f32[32,512]{1,0:T(8,128)S(1)} %get-tuple-element.190), channel_id=1, source_target_pairs={{0,2},{1,3},{2,0},{3,1},{4,6},{5,7},{6,4},{7,5},{8,10},{9,11},{10,... | collective-permute-start | bytes 196616 | tf_op jit(solution)/shard_map/ppermute | solution.py:268
  205.5 5.6 %collective-permute-start.24 = (f32[32,512]{1,0:T(8,128)S(1)}, f32[32,512]{1,0:T(8,128)S(1)}, u32[]{:S(2)}, u32[]{:S(2)}) collective-permute-start(f32[32,512]{1,0:T(8,128)S(1)} %get-tuple-element.189), channel_id=1, source_target_pairs={{0,3},{1,2},{2,1},{3,0},{4,7},{5,6},{6,5},{7,4},{8,11},{9,10},{10,... | collective-permute-start | bytes 196616 | tf_op jit(solution)/shard_map/ppermute | solution.py:268
  207.8 8.1 %collective-permute-start.25 = (f32[128,512]{1,0:T(8,128)S(1)}, f32[128,512]{1,0:T(8,128)S(1)}, u32[]{:S(2)}, u32[]{:S(2)}) collective-permute-start(f32[128,512]{1,0:T(8,128)S(1)} %fusion.1), channel_id=1, source_target_pairs={{0,64},{64,0},{1,65},{65,1},{2,66},{66,2},{3,67},{67,3},{4,68},{68... | collective-permute-start | bytes 786440 | tf_op jit(solution)/shard_map/ppermute | solution.py:299
  208.3 7.6 %collective-permute-start.27 = (bf16[4,32,1024]{2,1,0:T(8,128)(2,1)}, bf16[4,32,1024]{2,1,0:T(8,128)(2,1)S(1)}, u32[]{:S(2)}, u32[]{:S(2)}) collective-permute-start(bf16[4,32,1024]{2,1,0:T(8,128)(2,1)} %collective-permute-done.21.c2), channel_id=1, source_target_pairs={{0,1},{1,0},{2,3},{3,2},{4,5},{5,4},{6,7},{7,6},{8,9},{9,8},{10,11... | collective-permute-start | bytes 786440 | tf_op jit(solution)/shard_map/ppermute | solution.py:268
  215.9 14.5 %copy-start.11 = (f32[128,512]{1,0:T(8,128)}, f32[128,512]{1,0:T(8,128)S(1)}, u32[]{:S(2)}) copy-start(f32[128,512]{1,0:T(8,128)S(1)} %add.166) | copy-start | bytes 786436
  216.0 7.4 %collective-permute-start.28 = (f32[128,512]{1,0:T(8,128)S(1)}, f32[128,512]{1,0:T(8,128)S(1)}, u32[]{:S(2)}, u32[]{:S(2)}) collective-permute-start(f32[128,512]{1,0:T(8,128)S(1)} %bitcast_add_fusion), channel_id=1, source_target_pairs={{0,64},{64,0},{1,65},{65,1},{2,66},{66,2},{3,67},{67,3},{4,68},{68... | collective-permute-start | bytes 786440 | tf_op jit(solution)/shard_map/ppermute | solution.py:299
  216.3 13.4 %collective-permute-start.29 = (f32[4,32,512]{2,1,0:T(8,128)S(1)}, f32[4,32,512]{2,1,0:T(8,128)S(1)}, u32[]{:S(2)}, u32[]{:S(2)}) collective-permute-start(f32[4,32,512]{2,1,0:T(8,128)S(1)} %bitcast.166), channel_id=1, source_target_pairs={{0,2},{1,3},{2,0},{3,1},{4,6},{5,7},{6,4},{7,5},{8,10},{9,11},{10,... | collective-permute-start | bytes 786440 | tf_op jit(solution)/shard_map/ppermute | solution.py:268
  230.5 3.1 %collective-permute-start.30 = (f32[4,32,512]{2,1,0:T(8,128)S(1)}, f32[4,32,512]{2,1,0:T(8,128)S(1)}, u32[]{:S(2)}, u32[]{:S(2)}) collective-permute-start(f32[4,32,512]{2,1,0:T(8,128)S(1)} %bitcast.167), channel_id=1, source_target_pairs={{0,1},{1,0},{2,3},{3,2},{4,5},{5,4},{6,7},{7,6},{8,9},{9,8},{10,11... | collective-permute-start | bytes 786440 | tf_op jit(solution)/shard_map/ppermute | solution.py:268
  232.4 1.5 collective-permute-start.31
  232.5 23.1 %copy-start.28 = (f32[128,256]{1,0:T(8,128)S(1)}, f32[128,256]{1,0:T(8,128)}, u32[]{:S(2)}) copy-start(f32[128,256]{1,0:T(8,128)} %get-tuple-element.130) | copy-start | bytes 393220
  232.6 23.0 %collective-permute-start.33 = (f32[128,256]{1,0:T(8,128)}, f32[128,256]{1,0:T(8,128)S(1)}, u32[]{:S(2)}, u32[]{:S(2)}) collective-permute-start(f32[128,256]{1,0:T(8,128)} %get-tuple-element.127), channel_id=1, source_target_pairs={{0,64},{64,0},{1,65},{65,1},{2,66},{66,2},{3,67},{67,3},{4,68},{68... | collective-permute-start | bytes 393224 | tf_op jit(solution)/shard_map/ppermute | solution.py:299
  234.0 21.6 %collective-permute-start.32 = (f32[768,256]{1,0:T(8,128)}, f32[768,256]{1,0:T(8,128)S(1)}, u32[]{:S(2)}, u32[]{:S(2)}) collective-permute-start(f32[768,256]{1,0:T(8,128)} %get-tuple-element.122), channel_id=1, source_target_pairs={{0,64},{64,0},{1,65},{65,1},{2,66},{66,2},{3,67},{67,3},{4,68},{68... | collective-permute-start | bytes 2359304 | tf_op jit(solution)/shard_map/ppermute | solution.py:299
  255.6 7.0 %collective-permute-start.38 = (f32[4,32,256]{2,1,0:T(8,128)S(1)}, f32[4,32,256]{2,1,0:T(8,128)S(1)}, u32[]{:S(2)}, u32[]{:S(2)}) collective-permute-start(f32[4,32,256]{2,1,0:T(8,128)S(1)} %bitcast.162), channel_id=1, source_target_pairs={{0,2},{1,3},{2,0},{3,1},{4,6},{5,7},{6,4},{7,5},{8,10},{9,11},{10,... | collective-permute-start | bytes 393224 | tf_op jit(solution)/shard_map/ppermute | solution.py:268
  258.1 11.4 %collective-permute-start.37 = (f32[4,32,256]{2,1,0:T(8,128)S(1)}, f32[4,32,256]{2,1,0:T(8,128)S(1)}, u32[]{:S(2)}, u32[]{:S(2)}) collective-permute-start(f32[4,32,256]{2,1,0:T(8,128)S(1)} %bitcast.163), channel_id=1, source_target_pairs={{0,1},{1,0},{2,3},{3,2},{4,5},{5,4},{6,7},{7,6},{8,9},{9,8},{10,11... | collective-permute-start | bytes 393224 | tf_op jit(solution)/shard_map/ppermute | solution.py:268
  262.7 6.8 %collective-permute-start.39 = (f32[4,32,256]{2,1,0:T(8,128)S(1)}, f32[4,32,256]{2,1,0:T(8,128)S(1)}, u32[]{:S(2)}, u32[]{:S(2)}) collective-permute-start(f32[4,32,256]{2,1,0:T(8,128)S(1)} %collective-permute-done.38), channel_id=1, source_target_pairs={{0,1},{1,0},{2,3},{3,2},{4,5},{5,4},{6,7},{7,6},{8,9},{9,8},{10,11... | collective-permute-start | bytes 393224 | tf_op jit(solution)/shard_map/ppermute | solution.py:268
  265.7 29.1 %collective-permute-start.34 = (f32[16,32,256]{2,1,0:T(8,128)S(1)}, f32[16,32,256]{2,1,0:T(8,128)S(1)}, u32[]{:S(2)}, u32[]{:S(2)}) collective-permute-start(f32[16,32,256]{2,1,0:T(8,128)S(1)} %get-tuple-element.151), channel_id=1, source_target_pairs={{0,1},{1,0},{2,3},{3,2},{4,5},{5,4},{6,7},{7,6},{8,9},{9,8},{10,11... | collective-permute-start | bytes 1572872 | tf_op jit(solution)/shard_map/ppermute | solution.py:268
  266.1 28.7 %collective-permute-start.35 = (f32[16,32,256]{2,1,0:T(8,128)S(1)}, f32[16,32,256]{2,1,0:T(8,128)S(1)}, u32[]{:S(2)}, u32[]{:S(2)}) collective-permute-start(f32[16,32,256]{2,1,0:T(8,128)S(1)} %get-tuple-element.150), channel_id=1, source_target_pairs={{0,2},{1,3},{2,0},{3,1},{4,6},{5,7},{6,4},{7,5},{8,10},{9,11},{10,... | collective-permute-start | bytes 1572872 | tf_op jit(solution)/shard_map/ppermute | solution.py:268
  267.7 27.0 %collective-permute-start.36 = (f32[16,32,256]{2,1,0:T(8,128)S(1)}, f32[16,32,256]{2,1,0:T(8,128)S(1)}, u32[]{:S(2)}, u32[]{:S(2)}) collective-permute-start(f32[16,32,256]{2,1,0:T(8,128)S(1)} %get-tuple-element.149), channel_id=1, source_target_pairs={{0,3},{1,2},{2,1},{3,0},{4,7},{5,6},{6,5},{7,4},{8,11},{9,10},{10,... | collective-permute-start | bytes 1572872 | tf_op jit(solution)/shard_map/ppermute | solution.py:268
  271.3 23.5 %copy-start.22 = (f32[2,32,512]{2,1,0:T(8,128)S(1)}, f32[2,32,512]{2,1,0:T(8,128)}, u32[]{:S(2)}) copy-start(f32[2,32,512]{2,1,0:T(8,128)} %copy-done.21) | copy-start | bytes 393220
  271.3 24.3 %copy-start.19 = (f32[64,512]{1,0:T(8,128)S(1)}, f32[64,512]{1,0:T(8,128)}, u32[]{:S(2)}) copy-start(f32[64,512]{1,0:T(8,128)} %get-tuple-element.92) | copy-start | bytes 393220
  294.8 6.5 %collective-permute-start.41 = (f32[2,32,512]{2,1,0:T(8,128)S(1)}, f32[2,32,512]{2,1,0:T(8,128)S(1)}, u32[]{:S(2)}, u32[]{:S(2)}) collective-permute-start(f32[2,32,512]{2,1,0:T(8,128)S(1)} %copy-done.22), channel_id=1, source_target_pairs={{0,1},{1,0},{2,3},{3,2},{4,5},{5,4},{6,7},{7,6},{8,9},{9,8},{10,11... | collective-permute-start | bytes 393224 | tf_op jit(solution)/shard_map/ppermute | solution.py:268
  295.6 5.7 %collective-permute-start.40 = (f32[2,32,512]{2,1,0:T(8,128)S(1)}, f32[2,32,512]{2,1,0:T(8,128)S(1)}, u32[]{:S(2)}, u32[]{:S(2)}) collective-permute-start(f32[2,32,512]{2,1,0:T(8,128)S(1)} %bitcast.173), channel_id=1, source_target_pairs={{0,1},{1,0},{2,3},{3,2},{4,5},{5,4},{6,7},{7,6},{8,9},{9,8},{10,11... | collective-permute-start | bytes 393224 | tf_op jit(solution)/shard_map/ppermute | solution.py:268
  (23 other events, 58.9 us)
Sparse Core Ops, SparseCore 0:
  110.7 60.1 all-gather.5
  230.6 52.7 all-gather.3
